TPU v7x, 128 devices: a whole 4x4x4 slice. The times are simulated.
128 devices in a mesh: freq: 8 (over x, core), frame: 16 (over z, y).
Axes of the slice: x: 4, y: 4, z: 4, core: 2. Of those that a mesh axis runs over, the one named last changes fastest.
Arguments:
- spectra: bfloat16 [2, 24, 1024, 4096], P(None, None, 'freq', 'frame'), may hold values from -6 to 6
- norm_gain: float32 [1024], replicated, may hold values from 0.25 to 1.75
- w_in: bfloat16 [1024, 1024], replicated, may hold values from -0.1875 to 0.1875
- b_in: float32 [1024], replicated, may hold values from -3 to 3
- w_mid: bfloat16 [1024, 1024], replicated, may hold values from -0.1875 to 0.1875
- b_mid: float32 [1024], replicated, may hold values from -3 to 3
- w_out: bfloat16 [1024, 1024], replicated, may hold values from -0.1875 to 0.1875
- b_out: float32 [1024], replicated, may hold values from -3 to 3
Outputs:
- demixed: float32 [2, 24, 1024, 4096], P(None, None, 'freq', 'frame')
- variances: bfloat16 [24, 1024, 4096], P(None, 'freq', 'frame')
All inputs are finite; a program needn't handle non-finite values.
Results may differ from a plain program's by a relative error of at most 0.0032.
Values may be sent and summed in bfloat16 or wider, within the bound.
A program may use at most 128 MiB of HBM per device.

v0:
```python
import jax
import jax.numpy as jnp
from jax import lax
from jax.sharding import PartitionSpec as P

epsilon = 1e-05
power_floor = 0.001
variance_floor = 0.25


def coefficients(numer_real, numer_imag, denom, source, count):
    is_self = (jnp.arange(count, dtype=jnp.int32) == source)[:, None]
    coef_real = jnp.where(is_self, 1.0 - lax.rsqrt(denom), numer_real / denom)
    coef_imag = jnp.where(is_self, 0.0, numer_imag / denom)
    return (coef_real, coef_imag)


def on_device(spectra, norm_gain, w_in, b_in, w_mid, b_mid, w_out, b_out):
    real_part = spectra[0].astype(jnp.float32)
    imag_part = spectra[1].astype(jnp.float32)
    count = spectra.shape[1]
    frames = spectra.shape[3] * lax.axis_size("frame")
    logpower = jnp.log(real_part * real_part + imag_part * imag_part + power_floor).astype(
        jnp.bfloat16
    )
    values = lax.all_to_all(logpower, "freq", split_axis=2, concat_axis=1, tiled=True).astype(
        jnp.float32
    )
    average = jnp.mean(values, axis=1, keepdims=True)
    centred = values - average
    spread = jnp.mean(centred * centred, axis=1, keepdims=True)
    normed = (centred * lax.rsqrt(spread + epsilon) * norm_gain[None, :, None]).astype(jnp.bfloat16)
    hidden_one = jax.nn.silu(
        jnp.einsum("nft,fh->nth", normed, w_in, preferred_element_type=jnp.float32) + b_in
    ).astype(jnp.bfloat16)
    hidden_two = jax.nn.silu(
        jnp.einsum("nth,hg->ntg", hidden_one, w_mid, preferred_element_type=jnp.float32) + b_mid
    ).astype(jnp.bfloat16)
    output_pre = (
        jnp.einsum("nth,hf->nft", hidden_two, w_out, preferred_element_type=jnp.float32)
        + b_out[None, :, None]
    )
    frame_variances = (jax.nn.softplus(output_pre) + variance_floor).astype(jnp.bfloat16)
    variances = lax.all_to_all(frame_variances, "freq", split_axis=1, concat_axis=2, tiled=True)
    weight = 1.0 / variances.astype(jnp.float32)

    def sweep(source, carry):
        demix_real, demix_imag = carry
        pick_real = lax.dynamic_index_in_dim(demix_real, source, 0, keepdims=False)
        pick_imag = lax.dynamic_index_in_dim(demix_imag, source, 0, keepdims=False)
        numer_real = jnp.sum(weight * (demix_real * pick_real + demix_imag * pick_imag), axis=2)
        numer_imag = jnp.sum(weight * (demix_imag * pick_real - demix_real * pick_imag), axis=2)
        denom = jnp.sum(weight * (pick_real * pick_real + pick_imag * pick_imag), axis=2)
        numer_real, numer_imag, denom = lax.psum((numer_real, numer_imag, denom), "frame")
        coef_real, coef_imag = coefficients(
            numer_real / frames, numer_imag / frames, denom / frames, source, count
        )
        coef_real = coef_real[:, :, None]
        coef_imag = coef_imag[:, :, None]
        new_real = demix_real - (coef_real * pick_real - coef_imag * pick_imag)
        new_imag = demix_imag - (coef_real * pick_imag + coef_imag * pick_real)
        return (new_real, new_imag)

    demix_real, demix_imag = lax.fori_loop(0, count, sweep, (real_part, imag_part))
    return (jnp.stack([demix_real, demix_imag]), variances)


def solution(mesh):
    in_specs = (P(None, None, "freq", "frame"), P(), P(), P(), P(), P(), P(), P())
    out_specs = (P(None, None, "freq", "frame"), P(None, "freq", "frame"))
    return jax.shard_map(
        on_device, mesh=mesh, in_specs=in_specs, out_specs=out_specs, check_vma=False
    )
```

profile of v0, /device:TPU:0, one launch (start us, length us, event | category | flops | bytes accessed | tf_op | source)
XLA Modules:
  0.0 2055.1 jit_solution(8530623988659163088)
XLA Ops:
  13.0 26.0 %all_to_all.27 = bf16[24,128,256]{1,0,2:T(8,128)(2,1)S(1)} all-to-all(bf16[24,128,256]{1,0,2:T(8,128)(2,1)S(1)} %log_convert_fusion), channel_id=1, replica_groups=mesh['freq'=8,'frame'=16] {'freq'}, dimensions={2} | all-to-all | bytes 3145728 | tf_op jit(solution)/shard_map/all_to_all | solution.py:26
  42.1 7.7 fusion.15
  49.8 5.9 fusion.5
  61.5 9.5 reshape.44
  85.9 10.3 all-to-all-done.1
  101.6 6.5 copy.42
  114.2 1934.5 %while.15 = (s32[]{:T(128)}, f32[24,128,256]{2,1,0:T(8,128)}, f32[24,128,256]{2,1,0:T(8,128)}, f32[24,128,256]{2,1,0:T(8,128)S(1)}, s32[]{:T(128)}) while((s32[]{:T(128)}, f32[24,128,256]{2,1,0:T(8,128)}, f32[24,128,256]{2,1,0:T(8,128)}, f32[24,128,256]{2,1,0:T(8,128)S(1)}, s32[]{:T(128)}) %tuple.56), condition=%wide.region_9.10_spmd, body=%wide.region_2.9_spmd.sunk | while | flops 15851546 | bytes 23527548 | solution.py:64
  119.8 75.9 %all-reduce.2 = (f32[24,128]{1,0:T(8,128)S(1)}, f32[24,128]{1,0:T(8,128)S(1)}, f32[24,128]{1,0:T(8,128)S(1)}) all-reduce(f32[24,128]{1,0:T(8,128)S(1)} %get-tuple-element.174, f32[24,128]{1,0:T(8,128)S(1)} %get-tuple-element.175, f32[24,128]{1,0:T(8,128)S(1)} %get-tuple-element.176), channel_id=1, replica_groups=mesh['freq'=8,'frame'=16] {'frame'}, use_global_device_ids=true, to_apply=%region_8.8 | all-reduce | flops 9216 | bytes 73728 | tf_op jit(solution)/shard_map/while/body/eval_jaxpr/psum | solution.py:54
  206.4 69.6 %all-reduce.2 = (f32[24,128]{1,0:T(8,128)S(1)}, f32[24,128]{1,0:T(8,128)S(1)}, f32[24,128]{1,0:T(8,128)S(1)}) all-reduce(f32[24,128]{1,0:T(8,128)S(1)} %get-tuple-element.174, f32[24,128]{1,0:T(8,128)S(1)} %get-tuple-element.175, f32[24,128]{1,0:T(8,128)S(1)} %get-tuple-element.176), channel_id=1, replica_groups=mesh['freq'=8,'frame'=16] {'frame'}, use_global_device_ids=true, to_apply=%region_8.8 | all-reduce | flops 9216 | bytes 73728 | tf_op jit(solution)/shard_map/while/body/eval_jaxpr/psum | solution.py:54
  286.7 69.6 %all-reduce.2 = (f32[24,128]{1,0:T(8,128)S(1)}, f32[24,128]{1,0:T(8,128)S(1)}, f32[24,128]{1,0:T(8,128)S(1)}) all-reduce(f32[24,128]{1,0:T(8,128)S(1)} %get-tuple-element.174, f32[24,128]{1,0:T(8,128)S(1)} %get-tuple-element.175, f32[24,128]{1,0:T(8,128)S(1)} %get-tuple-element.176), channel_id=1, replica_groups=mesh['freq'=8,'frame'=16] {'frame'}, use_global_device_ids=true, to_apply=%region_8.8 | all-reduce | flops 9216 | bytes 73728 | tf_op jit(solution)/shard_map/while/body/eval_jaxpr/psum | solution.py:54
  367.1 69.6 %all-reduce.2 = (f32[24,128]{1,0:T(8,128)S(1)}, f32[24,128]{1,0:T(8,128)S(1)}, f32[24,128]{1,0:T(8,128)S(1)}) all-reduce(f32[24,128]{1,0:T(8,128)S(1)} %get-tuple-element.174, f32[24,128]{1,0:T(8,128)S(1)} %get-tuple-element.175, f32[24,128]{1,0:T(8,128)S(1)} %get-tuple-element.176), channel_id=1, replica_groups=mesh['freq'=8,'frame'=16] {'frame'}, use_global_device_ids=true, to_apply=%region_8.8 | all-reduce | flops 9216 | bytes 73728 | tf_op jit(solution)/shard_map/while/body/eval_jaxpr/psum | solution.py:54
  447.4 69.6 %all-reduce.2 = (f32[24,128]{1,0:T(8,128)S(1)}, f32[24,128]{1,0:T(8,128)S(1)}, f32[24,128]{1,0:T(8,128)S(1)}) all-reduce(f32[24,128]{1,0:T(8,128)S(1)} %get-tuple-element.174, f32[24,128]{1,0:T(8,128)S(1)} %get-tuple-element.175, f32[24,128]{1,0:T(8,128)S(1)} %get-tuple-element.176), channel_id=1, replica_groups=mesh['freq'=8,'frame'=16] {'frame'}, use_global_device_ids=true, to_apply=%region_8.8 | all-reduce | flops 9216 | bytes 73728 | tf_op jit(solution)/shard_map/while/body/eval_jaxpr/psum | solution.py:54
  527.7 69.6 %all-reduce.2 = (f32[24,128]{1,0:T(8,128)S(1)}, f32[24,128]{1,0:T(8,128)S(1)}, f32[24,128]{1,0:T(8,128)S(1)}) all-reduce(f32[24,128]{1,0:T(8,128)S(1)} %get-tuple-element.174, f32[24,128]{1,0:T(8,128)S(1)} %get-tuple-element.175, f32[24,128]{1,0:T(8,128)S(1)} %get-tuple-element.176), channel_id=1, replica_groups=mesh['freq'=8,'frame'=16] {'frame'}, use_global_device_ids=true, to_apply=%region_8.8 | all-reduce | flops 9216 | bytes 73728 | tf_op jit(solution)/shard_map/while/body/eval_jaxpr/psum | solution.py:54
  608.1 69.6 %all-reduce.2 = (f32[24,128]{1,0:T(8,128)S(1)}, f32[24,128]{1,0:T(8,128)S(1)}, f32[24,128]{1,0:T(8,128)S(1)}) all-reduce(f32[24,128]{1,0:T(8,128)S(1)} %get-tuple-element.174, f32[24,128]{1,0:T(8,128)S(1)} %get-tuple-element.175, f32[24,128]{1,0:T(8,128)S(1)} %get-tuple-element.176), channel_id=1, replica_groups=mesh['freq'=8,'frame'=16] {'frame'}, use_global_device_ids=true, to_apply=%region_8.8 | all-reduce | flops 9216 | bytes 73728 | tf_op jit(solution)/shard_map/while/body/eval_jaxpr/psum | solution.py:54
  688.4 69.6 %all-reduce.2 = (f32[24,128]{1,0:T(8,128)S(1)}, f32[24,128]{1,0:T(8,128)S(1)}, f32[24,128]{1,0:T(8,128)S(1)}) all-reduce(f32[24,128]{1,0:T(8,128)S(1)} %get-tuple-element.174, f32[24,128]{1,0:T(8,128)S(1)} %get-tuple-element.175, f32[24,128]{1,0:T(8,128)S(1)} %get-tuple-element.176), channel_id=1, replica_groups=mesh['freq'=8,'frame'=16] {'frame'}, use_global_device_ids=true, to_apply=%region_8.8 | all-reduce | flops 9216 | bytes 73728 | tf_op jit(solution)/shard_map/while/body/eval_jaxpr/psum | solution.py:54
  768.8 69.6 %all-reduce.2 = (f32[24,128]{1,0:T(8,128)S(1)}, f32[24,128]{1,0:T(8,128)S(1)}, f32[24,128]{1,0:T(8,128)S(1)}) all-reduce(f32[24,128]{1,0:T(8,128)S(1)} %get-tuple-element.174, f32[24,128]{1,0:T(8,128)S(1)} %get-tuple-element.175, f32[24,128]{1,0:T(8,128)S(1)} %get-tuple-element.176), channel_id=1, replica_groups=mesh['freq'=8,'frame'=16] {'frame'}, use_global_device_ids=true, to_apply=%region_8.8 | all-reduce | flops 9216 | bytes 73728 | tf_op jit(solution)/shard_map/while/body/eval_jaxpr/psum | solution.py:54
  849.1 69.6 %all-reduce.2 = (f32[24,128]{1,0:T(8,128)S(1)}, f32[24,128]{1,0:T(8,128)S(1)}, f32[24,128]{1,0:T(8,128)S(1)}) all-reduce(f32[24,128]{1,0:T(8,128)S(1)} %get-tuple-element.174, f32[24,128]{1,0:T(8,128)S(1)} %get-tuple-element.175, f32[24,128]{1,0:T(8,128)S(1)} %get-tuple-element.176), channel_id=1, replica_groups=mesh['freq'=8,'frame'=16] {'frame'}, use_global_device_ids=true, to_apply=%region_8.8 | all-reduce | flops 9216 | bytes 73728 | tf_op jit(solution)/shard_map/while/body/eval_jaxpr/psum | solution.py:54
  929.4 69.6 %all-reduce.2 = (f32[24,128]{1,0:T(8,128)S(1)}, f32[24,128]{1,0:T(8,128)S(1)}, f32[24,128]{1,0:T(8,128)S(1)}) all-reduce(f32[24,128]{1,0:T(8,128)S(1)} %get-tuple-element.174, f32[24,128]{1,0:T(8,128)S(1)} %get-tuple-element.175, f32[24,128]{1,0:T(8,128)S(1)} %get-tuple-element.176), channel_id=1, replica_groups=mesh['freq'=8,'frame'=16] {'frame'}, use_global_device_ids=true, to_apply=%region_8.8 | all-reduce | flops 9216 | bytes 73728 | tf_op jit(solution)/shard_map/while/body/eval_jaxpr/psum | solution.py:54
  1009.8 69.6 %all-reduce.2 = (f32[24,128]{1,0:T(8,128)S(1)}, f32[24,128]{1,0:T(8,128)S(1)}, f32[24,128]{1,0:T(8,128)S(1)}) all-reduce(f32[24,128]{1,0:T(8,128)S(1)} %get-tuple-element.174, f32[24,128]{1,0:T(8,128)S(1)} %get-tuple-element.175, f32[24,128]{1,0:T(8,128)S(1)} %get-tuple-element.176), channel_id=1, replica_groups=mesh['freq'=8,'frame'=16] {'frame'}, use_global_device_ids=true, to_apply=%region_8.8 | all-reduce | flops 9216 | bytes 73728 | tf_op jit(solution)/shard_map/while/body/eval_jaxpr/psum | solution.py:54
  1090.1 69.7 %all-reduce.2 = (f32[24,128]{1,0:T(8,128)S(1)}, f32[24,128]{1,0:T(8,128)S(1)}, f32[24,128]{1,0:T(8,128)S(1)}) all-reduce(f32[24,128]{1,0:T(8,128)S(1)} %get-tuple-element.174, f32[24,128]{1,0:T(8,128)S(1)} %get-tuple-element.175, f32[24,128]{1,0:T(8,128)S(1)} %get-tuple-element.176), channel_id=1, replica_groups=mesh['freq'=8,'frame'=16] {'frame'}, use_global_device_ids=true, to_apply=%region_8.8 | all-reduce | flops 9216 | bytes 73728 | tf_op jit(solution)/shard_map/while/body/eval_jaxpr/psum | solution.py:54
  1170.5 69.6 %all-reduce.2 = (f32[24,128]{1,0:T(8,128)S(1)}, f32[24,128]{1,0:T(8,128)S(1)}, f32[24,128]{1,0:T(8,128)S(1)}) all-reduce(f32[24,128]{1,0:T(8,128)S(1)} %get-tuple-element.174, f32[24,128]{1,0:T(8,128)S(1)} %get-tuple-element.175, f32[24,128]{1,0:T(8,128)S(1)} %get-tuple-element.176), channel_id=1, replica_groups=mesh['freq'=8,'frame'=16] {'frame'}, use_global_device_ids=true, to_apply=%region_8.8 | all-reduce | flops 9216 | bytes 73728 | tf_op jit(solution)/shard_map/while/body/eval_jaxpr/psum | solution.py:54
  1250.8 69.6 %all-reduce.2 = (f32[24,128]{1,0:T(8,128)S(1)}, f32[24,128]{1,0:T(8,128)S(1)}, f32[24,128]{1,0:T(8,128)S(1)}) all-reduce(f32[24,128]{1,0:T(8,128)S(1)} %get-tuple-element.174, f32[24,128]{1,0:T(8,128)S(1)} %get-tuple-element.175, f32[24,128]{1,0:T(8,128)S(1)} %get-tuple-element.176), channel_id=1, replica_groups=mesh['freq'=8,'frame'=16] {'frame'}, use_global_device_ids=true, to_apply=%region_8.8 | all-reduce | flops 9216 | bytes 73728 | tf_op jit(solution)/shard_map/while/body/eval_jaxpr/psum | solution.py:54
  1331.2 69.6 %all-reduce.2 = (f32[24,128]{1,0:T(8,128)S(1)}, f32[24,128]{1,0:T(8,128)S(1)}, f32[24,128]{1,0:T(8,128)S(1)}) all-reduce(f32[24,128]{1,0:T(8,128)S(1)} %get-tuple-element.174, f32[24,128]{1,0:T(8,128)S(1)} %get-tuple-element.175, f32[24,128]{1,0:T(8,128)S(1)} %get-tuple-element.176), channel_id=1, replica_groups=mesh['freq'=8,'frame'=16] {'frame'}, use_global_device_ids=true, to_apply=%region_8.8 | all-reduce | flops 9216 | bytes 73728 | tf_op jit(solution)/shard_map/while/body/eval_jaxpr/psum | solution.py:54
  1411.5 69.6 %all-reduce.2 = (f32[24,128]{1,0:T(8,128)S(1)}, f32[24,128]{1,0:T(8,128)S(1)}, f32[24,128]{1,0:T(8,128)S(1)}) all-reduce(f32[24,128]{1,0:T(8,128)S(1)} %get-tuple-element.174, f32[24,128]{1,0:T(8,128)S(1)} %get-tuple-element.175, f32[24,128]{1,0:T(8,128)S(1)} %get-tuple-element.176), channel_id=1, replica_groups=mesh['freq'=8,'frame'=16] {'frame'}, use_global_device_ids=true, to_apply=%region_8.8 | all-reduce | flops 9216 | bytes 73728 | tf_op jit(solution)/shard_map/while/body/eval_jaxpr/psum | solution.py:54
  1491.8 69.6 %all-reduce.2 = (f32[24,128]{1,0:T(8,128)S(1)}, f32[24,128]{1,0:T(8,128)S(1)}, f32[24,128]{1,0:T(8,128)S(1)}) all-reduce(f32[24,128]{1,0:T(8,128)S(1)} %get-tuple-element.174, f32[24,128]{1,0:T(8,128)S(1)} %get-tuple-element.175, f32[24,128]{1,0:T(8,128)S(1)} %get-tuple-element.176), channel_id=1, replica_groups=mesh['freq'=8,'frame'=16] {'frame'}, use_global_device_ids=true, to_apply=%region_8.8 | all-reduce | flops 9216 | bytes 73728 | tf_op jit(solution)/shard_map/while/body/eval_jaxpr/psum | solution.py:54
  1572.2 69.6 %all-reduce.2 = (f32[24,128]{1,0:T(8,128)S(1)}, f32[24,128]{1,0:T(8,128)S(1)}, f32[24,128]{1,0:T(8,128)S(1)}) all-reduce(f32[24,128]{1,0:T(8,128)S(1)} %get-tuple-element.174, f32[24,128]{1,0:T(8,128)S(1)} %get-tuple-element.175, f32[24,128]{1,0:T(8,128)S(1)} %get-tuple-element.176), channel_id=1, replica_groups=mesh['freq'=8,'frame'=16] {'frame'}, use_global_device_ids=true, to_apply=%region_8.8 | all-reduce | flops 9216 | bytes 73728 | tf_op jit(solution)/shard_map/while/body/eval_jaxpr/psum | solution.py:54
  1652.5 69.6 %all-reduce.2 = (f32[24,128]{1,0:T(8,128)S(1)}, f32[24,128]{1,0:T(8,128)S(1)}, f32[24,128]{1,0:T(8,128)S(1)}) all-reduce(f32[24,128]{1,0:T(8,128)S(1)} %get-tuple-element.174, f32[24,128]{1,0:T(8,128)S(1)} %get-tuple-element.175, f32[24,128]{1,0:T(8,128)S(1)} %get-tuple-element.176), channel_id=1, replica_groups=mesh['freq'=8,'frame'=16] {'frame'}, use_global_device_ids=true, to_apply=%region_8.8 | all-reduce | flops 9216 | bytes 73728 | tf_op jit(solution)/shard_map/while/body/eval_jaxpr/psum | solution.py:54
  1732.9 69.6 %all-reduce.2 = (f32[24,128]{1,0:T(8,128)S(1)}, f32[24,128]{1,0:T(8,128)S(1)}, f32[24,128]{1,0:T(8,128)S(1)}) all-reduce(f32[24,128]{1,0:T(8,128)S(1)} %get-tuple-element.174, f32[24,128]{1,0:T(8,128)S(1)} %get-tuple-element.175, f32[24,128]{1,0:T(8,128)S(1)} %get-tuple-element.176), channel_id=1, replica_groups=mesh['freq'=8,'frame'=16] {'frame'}, use_global_device_ids=true, to_apply=%region_8.8 | all-reduce | flops 9216 | bytes 73728 | tf_op jit(solution)/shard_map/while/body/eval_jaxpr/psum | solution.py:54
  1813.2 69.6 %all-reduce.2 = (f32[24,128]{1,0:T(8,128)S(1)}, f32[24,128]{1,0:T(8,128)S(1)}, f32[24,128]{1,0:T(8,128)S(1)}) all-reduce(f32[24,128]{1,0:T(8,128)S(1)} %get-tuple-element.174, f32[24,128]{1,0:T(8,128)S(1)} %get-tuple-element.175, f32[24,128]{1,0:T(8,128)S(1)} %get-tuple-element.176), channel_id=1, replica_groups=mesh['freq'=8,'frame'=16] {'frame'}, use_global_device_ids=true, to_apply=%region_8.8 | all-reduce | flops 9216 | bytes 73728 | tf_op jit(solution)/shard_map/while/body/eval_jaxpr/psum | solution.py:54
  1893.5 69.6 %all-reduce.2 = (f32[24,128]{1,0:T(8,128)S(1)}, f32[24,128]{1,0:T(8,128)S(1)}, f32[24,128]{1,0:T(8,128)S(1)}) all-reduce(f32[24,128]{1,0:T(8,128)S(1)} %get-tuple-element.174, f32[24,128]{1,0:T(8,128)S(1)} %get-tuple-element.175, f32[24,128]{1,0:T(8,128)S(1)} %get-tuple-element.176), channel_id=1, replica_groups=mesh['freq'=8,'frame'=16] {'frame'}, use_global_device_ids=true, to_apply=%region_8.8 | all-reduce | flops 9216 | bytes 73728 | tf_op jit(solution)/shard_map/while/body/eval_jaxpr/psum | solution.py:54
  1973.9 69.6 %all-reduce.2 = (f32[24,128]{1,0:T(8,128)S(1)}, f32[24,128]{1,0:T(8,128)S(1)}, f32[24,128]{1,0:T(8,128)S(1)}) all-reduce(f32[24,128]{1,0:T(8,128)S(1)} %get-tuple-element.174, f32[24,128]{1,0:T(8,128)S(1)} %get-tuple-element.175, f32[24,128]{1,0:T(8,128)S(1)} %get-tuple-element.176), channel_id=1, replica_groups=mesh['freq'=8,'frame'=16] {'frame'}, use_global_device_ids=true, to_apply=%region_8.8 | all-reduce | flops 9216 | bytes 73728 | tf_op jit(solution)/shard_map/while/body/eval_jaxpr/psum | solution.py:54
  2048.7 6.4 pad_maximum_fusion
  (155 shorter events, 304.3 us)
Async XLA Ops:
  0.6 41.4 %copy-start = (bf16[1024,1024]{1,0:T(8,128)(2,1)S(1)}, bf16[1024,1024]{1,0:T(8,128)(2,1)}, u32[]{:S(2)}) copy-start(bf16[1024,1024]{1,0:T(8,128)(2,1)} %param.14) | copy-start | bytes 6291460
  41.2 0.9 copy-start.4
  41.2 0.9 copy-start.5
  42.1 7.7 copy-start.6
  42.1 7.7 copy-start.7
  71.0 3.9 copy-start.3
  71.0 25.2 %all-to-all-start.1 = ((bf16[8,2,49152]{2,1,0:T(2,128)(2,1)}), bf16[8,2,49152]{2,1,0:T(2,128)(2,1)S(1)}, u32[]{:S(2)}, u32[]{:S(2)}) async-start(bf16[8,2,49152]{2,1,0:T(2,128)(2,1)} %reshape.44), calls=%async_computation.1 | async-start | bytes 3145728 | tf_op jit(solution)/shard_map/all_to_all | solution.py:44
  76.8 3.7 copy-start.2
  2048.7 6.4 copy-start.1
where the time goes:
time: 2060 us
  blocking collectives  1700 us (83%)
  other arithmetic  275 us (13%)
  local copies, waits for them, and re-layouts  48 us (2%)
    psum x24, blocking collectives, sweep(): lax.psum((numer_real, numer_imag, denom), 'frame')  1680 us
    sub x24, other arithmetic, sweep(): new_imag = demix_imag - (coef_real * pick_imag + coef_imag * pick_real)  122 us
    reduce_sum x24, other arithmetic, sweep(): jnp.sum(weight * (demix_real * pick_real + demix_imag * pick_imag), axis=2)  109 us
  transfers between devices with their start and end apart: 1, of which 1 were waited for; matrix products, arithmetic and copies ran while one was open for 1% of the time, Pallas kernels for 0%

commit v1 on v0

--- a/solution.py
+++ b/solution.py
@@ -15,11 +15,9 @@
     return (coef_real, coef_imag)
 
 
-def on_device(spectra, norm_gain, w_in, b_in, w_mid, b_mid, w_out, b_out):
+def source_model(spectra, norm_gain, w_in, b_in, w_mid, b_mid, w_out, b_out):
     real_part = spectra[0].astype(jnp.float32)
     imag_part = spectra[1].astype(jnp.float32)
-    count = spectra.shape[1]
-    frames = spectra.shape[3] * lax.axis_size("frame")
     logpower = jnp.log(real_part * real_part + imag_part * imag_part + power_floor).astype(
         jnp.bfloat16
     )
@@ -41,17 +39,27 @@
         + b_out[None, :, None]
     )
     frame_variances = (jax.nn.softplus(output_pre) + variance_floor).astype(jnp.bfloat16)
-    variances = lax.all_to_all(frame_variances, "freq", split_axis=1, concat_axis=2, tiled=True)
-    weight = 1.0 / variances.astype(jnp.float32)
+    return lax.all_to_all(frame_variances, "freq", split_axis=1, concat_axis=2, tiled=True)
+
+
+def on_device(spectra, norm_gain, w_in, b_in, w_mid, b_mid, w_out, b_out):
+    count = spectra.shape[1]
+    frames = spectra.shape[3] * lax.axis_size("frame")
+    variances = source_model(spectra, norm_gain, w_in, b_in, w_mid, b_mid, w_out, b_out)
+
+    spec_sw = lax.all_to_all(spectra, "frame", split_axis=2, concat_axis=3, tiled=True)
+    var_sw = lax.all_to_all(variances, "frame", split_axis=1, concat_axis=2, tiled=True)
+    weight = 1.0 / var_sw.astype(jnp.float32)
+    bins = spec_sw.shape[2]
+    eye = jnp.broadcast_to(jnp.eye(count, dtype=jnp.float32)[:, :, None], (count, count, bins))
 
     def sweep(source, carry):
-        demix_real, demix_imag = carry
+        demix_real, demix_imag, mix_real, mix_imag = carry
         pick_real = lax.dynamic_index_in_dim(demix_real, source, 0, keepdims=False)
         pick_imag = lax.dynamic_index_in_dim(demix_imag, source, 0, keepdims=False)
         numer_real = jnp.sum(weight * (demix_real * pick_real + demix_imag * pick_imag), axis=2)
         numer_imag = jnp.sum(weight * (demix_imag * pick_real - demix_real * pick_imag), axis=2)
         denom = jnp.sum(weight * (pick_real * pick_real + pick_imag * pick_imag), axis=2)
-        numer_real, numer_imag, denom = lax.psum((numer_real, numer_imag, denom), "frame")
         coef_real, coef_imag = coefficients(
             numer_real / frames, numer_imag / frames, denom / frames, source, count
         )
@@ -59,10 +67,28 @@
         coef_imag = coef_imag[:, :, None]
         new_real = demix_real - (coef_real * pick_real - coef_imag * pick_imag)
         new_imag = demix_imag - (coef_real * pick_imag + coef_imag * pick_real)
-        return (new_real, new_imag)
+        row_real = lax.dynamic_index_in_dim(mix_real, source, 0, keepdims=False)[None]
+        row_imag = lax.dynamic_index_in_dim(mix_imag, source, 0, keepdims=False)[None]
+        cr = coef_real[:, None, :, 0]
+        ci = coef_imag[:, None, :, 0]
+        new_mix_real = mix_real - (cr * row_real - ci * row_imag)
+        new_mix_imag = mix_imag - (cr * row_imag + ci * row_real)
+        return (new_real, new_imag, new_mix_real, new_mix_imag)
 
-    demix_real, demix_imag = lax.fori_loop(0, count, sweep, (real_part, imag_part))
-    return (jnp.stack([demix_real, demix_imag]), variances)
+    init = (spec_sw[0].astype(jnp.float32), spec_sw[1].astype(jnp.float32), eye, jnp.zeros_like(eye))
+    _, _, mix_real, mix_imag = lax.fori_loop(0, count, sweep, init)
+
+    mix_real = lax.all_gather(mix_real, "frame", axis=2, tiled=True)
+    mix_imag = lax.all_gather(mix_imag, "frame", axis=2, tiled=True)
+    top = jnp.concatenate([mix_real, -mix_imag], axis=1)
+    bottom = jnp.concatenate([mix_imag, mix_real], axis=1)
+    mix = jnp.concatenate([top, bottom], axis=0)
+    stacked = spectra.reshape(2 * count, spectra.shape[2], spectra.shape[3]).astype(jnp.float32)
+    demixed = jnp.einsum(
+        "jaf,aft->jft", mix, stacked, precision=lax.Precision.HIGHEST,
+        preferred_element_type=jnp.float32,
+    )
+    return (demixed.reshape(spectra.shape), variances)
 
 
 def solution(mesh):

time: 2060 us -> 533 us (0.26)
  blocking collectives: 1700 us -> 74.6 us
  waiting for transfers between devices: 10.3 us -> 63.3 us
    psum x24 -> x0, blocking collectives: 1680 us -> none  [sweep(): lax.psum((numer_real, numer_imag, denom), 'frame')]
    all_to_all x1 -> x3, waiting for transfers between devices: 10.3 us -> 63.3 us  [the longest x1 30.9 us: on_device(): lax.all_to_all(spectra, 'frame', split_axis=2, concat_axis=3, tiled=True)]
    all_gather x0 -> x2, blocking collectives: none -> 48.6 us  [the longest x1 24.7 us: on_device(): mix_real = lax.all_gather(mix_real, 'frame', axis=2, tiled=True)]
  transfers between devices with their start and end apart: 1 -> 3, of which waited for: 1 -> 3; matrix products, arithmetic and copies ran while one was open for 1% -> 5% of each run, Pallas kernels for 0% -> 0%
where the time goes in v1:
time: 533 us; the launch traced here: 531 us
  other arithmetic  293 us (55%)
  blocking collectives  74.6 us (14%)
  waiting for transfers between devices  63.3 us (12%)
  local copies, waits for them, and re-layouts  61.3 us (12%)
  matrix products  20 us (4%)
  starting transfers between devices  17.2 us (3%)
    sub x24, other arithmetic, sweep(): new_imag = demix_imag - (coef_real * pick_imag + coef_imag * pick_real)  140 us
    reduce_sum x24, other arithmetic, sweep(): jnp.sum(weight * (demix_real * pick_real + demix_imag * pick_imag), axis=2)  110 us
    unnamed x23, local copies, waits for them, and re-layouts  34.3 us
    all_to_all x1, waiting for transfers between devices, on_device(): lax.all_to_all(spectra, 'frame', split_axis=2, concat_axis=3, tiled=True)  30.9 us
    all_to_all x1, blocking collectives, source_model(): lax.all_to_all(logpower, 'freq', split_axis=2, concat_axis=1, tiled=True)  26 us
    all_gather x1, blocking collectives, on_device(): mix_real = lax.all_gather(mix_real, 'frame', axis=2, tiled=True)  24.7 us
    all_gather x1, blocking collectives, on_device(): mix_imag = lax.all_gather(mix_imag, 'frame', axis=2, tiled=True)  23.9 us
    mul x24, other arithmetic, sweep(): weight * (pick_real * pick_real + pick_imag * pick_imag)  22.5 us
  transfers between devices with their start and end apart: 3, of which 3 were waited for; matrix products, arithmetic and copies ran while one was open for 5% of the time, Pallas kernels for 0%

profile of v1, /device:TPU:0, one launch (start us, length us, event | category | flops | bytes accessed | tf_op | source)
XLA Modules:
  0.0 531.1 jit_solution(5450022777000983309)
XLA Ops:
  13.0 26.0 %all_to_all.51 = bf16[24,128,256]{1,0,2:T(8,128)(2,1)S(1)} all-to-all(bf16[24,128,256]{1,0,2:T(8,128)(2,1)S(1)} %fusion.21), channel_id=1, replica_groups=mesh['freq'=8,'frame'=16] {'freq'}, dimensions={2} | all-to-all | bytes 3145728 | tf_op jit(solution)/shard_map/all_to_all | solution.py:24
  42.1 7.7 %fusion.17 = f32[24,32,1024]{2,1,0:T(8,128)} fusion(bf16[1024,1024]{1,0:T(8,128)(2,1)S(1)} %copy-done, f32[1024]{0:T(1024)S(1)} %copy-done.4, bf16[1024,1024]{1,0:T(8,128)(2,1)} %param.12, f32[24,8,4,8,128]{4,3,2,1,0:T(8,128)} %get-tuple-element.178, f32[1024]{0:T(1024)S(1)} %copy-done.5, f32[24,32]{1,0:T(8,128)S(1)} %add_rsqrt_fusion, ...), kind=kOutput, calls=%fused_computation.43 | convolution fusion | flops 3229089792 | bytes 10500096 | tf_op jit(solution)/shard_map/nth,hg->ntg/dot_general | solution.py:35
  49.8 5.9 %fusion.5 = bf16[24,1024,32]{1,2,0:T(8,128)(2,1)S(1)} fusion(f32[1024]{0:T(1024)S(1)} %copy-done.6, bf16[1024,1024]{1,0:T(8,128)(2,1)} %param.16, f32[24,32,1024]{2,1,0:T(8,128)} %fusion.17, f32[1024]{0:T(1024)S(1)} %copy-done.7), kind=kOutput, calls=%fused_computation.24 | convolution fusion | flops 1622409216 | bytes 6823936 | tf_op jit(solution)/shard_map/nth,hf->nft/dot_general | solution.py:38
  55.7 5.9 %copy.84 = bf16[24,1024,32]{2,0,1:T(8,128)(2,1)} copy(bf16[24,1024,32]{1,2,0:T(8,128)(2,1)S(1)} %fusion.5) | data formatting | bytes 3145728 | tf_op jit(solution)/shard_map/convert_element_type | solution.py:41
  61.5 9.5 %reshape.185 = bf16[8,2,49152]{2,1,0:T(2,128)(2,1)} reshape(bf16[1024,24,32]{2,1,0:T(8,128)(2,1)} %bitcast.101) | data formatting | bytes 3145728
  79.2 17.9 %all-to-all-done.2 = bf16[8,2,49152]{2,1,0:T(2,128)(2,1)} async-done(((bf16[8,2,49152]{2,1,0:T(2,128)(2,1)}), bf16[8,2,49152]{2,1,0:T(2,128)(2,1)}, u32[]{:S(2)}, u32[]{:S(2)}) %all-to-all-start.2) | async-done | bytes 1572896 | tf_op jit(solution)/shard_map/all_to_all | solution.py:42
  97.2 8.1 %all-to-all-start = ((bf16[2,24,128,256]{3,1,0,2:T(8,128)(2,1)}), bf16[2,24,128,256]{3,1,0,2:T(8,128)(2,1)}, u32[]{:S(2)}, u32[]{:S(2)}) async-start(bf16[2,24,128,256]{3,1,0,2:T(8,128)(2,1)} %copy.77), calls=%async_computation | async-start | bytes 6291456 | tf_op jit(solution)/shard_map/all_to_all | solution.py:50
  105.3 7.9 %reshape.186 = bf16[1024,24,32]{2,1,0:T(8,128)(2,1)} reshape(bf16[8,2,49152]{2,1,0:T(2,128)(2,1)} %all-to-all-done.2) | data formatting | bytes 3145728
  113.1 6.5 %copy.86 = bf16[24,128,8,32]{1,3,2,0:T(8,128)(2,1)S(1)} copy(bf16[24,128,8,32]{3,0,1,2:T(8,128)(2,1)} %bitcast.102) | data formatting | bytes 3145728 | tf_op jit(solution)/shard_map/all_to_all | solution.py:42
  121.4 30.9 %all-to-all-done = bf16[2,24,128,256]{3,1,0,2:T(8,128)(2,1)} async-done(((bf16[2,24,128,256]{3,1,0,2:T(8,128)(2,1)}), bf16[2,24,128,256]{3,1,0,2:T(8,128)(2,1)}, u32[]{:S(2)}, u32[]{:S(2)}) %all-to-all-start) | async-done | bytes 3145760 | tf_op jit(solution)/shard_map/all_to_all | solution.py:50
  164.7 14.5 %all-to-all-done.3 = bf16[24,128,256]{2,0,1:T(8,128)(2,1)} async-done(((bf16[24,128,256]{2,0,1:T(8,128)(2,1)}), bf16[24,128,256]{2,0,1:T(8,128)(2,1)}, u32[]{:S(2)}, u32[]{:S(2)}) %all-to-all-start.3) | async-done | bytes 1572896 | tf_op jit(solution)/shard_map/all_to_all | solution.py:51
  182.7 278.9 %while.20 = (s32[]{:T(128)}, f32[24,8,4096]{2,1,0:T(8,128)}, f32[24,8,4096]{2,1,0:T(8,128)S(1)}, f32[24,24,8]{1,2,0:T(8,128)S(1)}, f32[24,24,8]{1,2,0:T(8,128)S(...) while((s32[]{:T(128)}, f32[24,8,4096]{2,1,0:T(8,128)}, f32[24,8,4096]{2,1,0:T(8,128)S(1)}, ...), condition=%wide.region_6.7_spmd.clone, body=%wide.region_2.6_spmd.clone.sunk | while | flops 15874011 | bytes 23455392 | solution.py:79
  188.5 5.8 %add_subtract_fusion.4 = (f32[24,8,4096]{2,1,0:T(8,128)S(1)}, f32[24,8,4096]{2,1,0:T(8,128)}) fusion(f32[24,8,4096]{2,1,0:T(8,128)S(1)} %get-tuple-element.254, f32[24,8]{1,0:T(8,128)S(1)} %get-tuple-element.236, f32[24,8]{1,0:T(8,128)S(1)} %get-tuple-element.237, f32[8,4096]{1,0:T(8,128)S(1)} %get-tuple-element.230, ...), kind=kLoop, calls=%fused_computation.clone.1 | loop fusion | flops 6291456 | bytes 12846592 | tf_op jit(solution)/shard_map/while/body/eval_jaxpr/sub | solution.py:69
  200.1 5.8 %add_subtract_fusion.4 = (f32[24,8,4096]{2,1,0:T(8,128)S(1)}, f32[24,8,4096]{2,1,0:T(8,128)}) fusion(f32[24,8,4096]{2,1,0:T(8,128)S(1)} %get-tuple-element.254, f32[24,8]{1,0:T(8,128)S(1)} %get-tuple-element.236, f32[24,8]{1,0:T(8,128)S(1)} %get-tuple-element.237, f32[8,4096]{1,0:T(8,128)S(1)} %get-tuple-element.230, ...), kind=kLoop, calls=%fused_computation.clone.1 | loop fusion | flops 6291456 | bytes 12846592 | tf_op jit(solution)/shard_map/while/body/eval_jaxpr/sub | solution.py:69
  211.7 5.8 %add_subtract_fusion.4 = (f32[24,8,4096]{2,1,0:T(8,128)S(1)}, f32[24,8,4096]{2,1,0:T(8,128)}) fusion(f32[24,8,4096]{2,1,0:T(8,128)S(1)} %get-tuple-element.254, f32[24,8]{1,0:T(8,128)S(1)} %get-tuple-element.236, f32[24,8]{1,0:T(8,128)S(1)} %get-tuple-element.237, f32[8,4096]{1,0:T(8,128)S(1)} %get-tuple-element.230, ...), kind=kLoop, calls=%fused_computation.clone.1 | loop fusion | flops 6291456 | bytes 12846592 | tf_op jit(solution)/shard_map/while/body/eval_jaxpr/sub | solution.py:69
  223.4 5.8 %add_subtract_fusion.4 = (f32[24,8,4096]{2,1,0:T(8,128)S(1)}, f32[24,8,4096]{2,1,0:T(8,128)}) fusion(f32[24,8,4096]{2,1,0:T(8,128)S(1)} %get-tuple-element.254, f32[24,8]{1,0:T(8,128)S(1)} %get-tuple-element.236, f32[24,8]{1,0:T(8,128)S(1)} %get-tuple-element.237, f32[8,4096]{1,0:T(8,128)S(1)} %get-tuple-element.230, ...), kind=kLoop, calls=%fused_computation.clone.1 | loop fusion | flops 6291456 | bytes 12846592 | tf_op jit(solution)/shard_map/while/body/eval_jaxpr/sub | solution.py:69
  235.0 5.8 %add_subtract_fusion.4 = (f32[24,8,4096]{2,1,0:T(8,128)S(1)}, f32[24,8,4096]{2,1,0:T(8,128)}) fusion(f32[24,8,4096]{2,1,0:T(8,128)S(1)} %get-tuple-element.254, f32[24,8]{1,0:T(8,128)S(1)} %get-tuple-element.236, f32[24,8]{1,0:T(8,128)S(1)} %get-tuple-element.237, f32[8,4096]{1,0:T(8,128)S(1)} %get-tuple-element.230, ...), kind=kLoop, calls=%fused_computation.clone.1 | loop fusion | flops 6291456 | bytes 12846592 | tf_op jit(solution)/shard_map/while/body/eval_jaxpr/sub | solution.py:69
  246.6 5.8 %add_subtract_fusion.4 = (f32[24,8,4096]{2,1,0:T(8,128)S(1)}, f32[24,8,4096]{2,1,0:T(8,128)}) fusion(f32[24,8,4096]{2,1,0:T(8,128)S(1)} %get-tuple-element.254, f32[24,8]{1,0:T(8,128)S(1)} %get-tuple-element.236, f32[24,8]{1,0:T(8,128)S(1)} %get-tuple-element.237, f32[8,4096]{1,0:T(8,128)S(1)} %get-tuple-element.230, ...), kind=kLoop, calls=%fused_computation.clone.1 | loop fusion | flops 6291456 | bytes 12846592 | tf_op jit(solution)/shard_map/while/body/eval_jaxpr/sub | solution.py:69
  258.2 5.8 %add_subtract_fusion.4 = (f32[24,8,4096]{2,1,0:T(8,128)S(1)}, f32[24,8,4096]{2,1,0:T(8,128)}) fusion(f32[24,8,4096]{2,1,0:T(8,128)S(1)} %get-tuple-element.254, f32[24,8]{1,0:T(8,128)S(1)} %get-tuple-element.236, f32[24,8]{1,0:T(8,128)S(1)} %get-tuple-element.237, f32[8,4096]{1,0:T(8,128)S(1)} %get-tuple-element.230, ...), kind=kLoop, calls=%fused_computation.clone.1 | loop fusion | flops 6291456 | bytes 12846592 | tf_op jit(solution)/shard_map/while/body/eval_jaxpr/sub | solution.py:69
  269.8 5.8 %add_subtract_fusion.4 = (f32[24,8,4096]{2,1,0:T(8,128)S(1)}, f32[24,8,4096]{2,1,0:T(8,128)}) fusion(f32[24,8,4096]{2,1,0:T(8,128)S(1)} %get-tuple-element.254, f32[24,8]{1,0:T(8,128)S(1)} %get-tuple-element.236, f32[24,8]{1,0:T(8,128)S(1)} %get-tuple-element.237, f32[8,4096]{1,0:T(8,128)S(1)} %get-tuple-element.230, ...), kind=kLoop, calls=%fused_computation.clone.1 | loop fusion | flops 6291456 | bytes 12846592 | tf_op jit(solution)/shard_map/while/body/eval_jaxpr/sub | solution.py:69
  281.5 5.8 %add_subtract_fusion.4 = (f32[24,8,4096]{2,1,0:T(8,128)S(1)}, f32[24,8,4096]{2,1,0:T(8,128)}) fusion(f32[24,8,4096]{2,1,0:T(8,128)S(1)} %get-tuple-element.254, f32[24,8]{1,0:T(8,128)S(1)} %get-tuple-element.236, f32[24,8]{1,0:T(8,128)S(1)} %get-tuple-element.237, f32[8,4096]{1,0:T(8,128)S(1)} %get-tuple-element.230, ...), kind=kLoop, calls=%fused_computation.clone.1 | loop fusion | flops 6291456 | bytes 12846592 | tf_op jit(solution)/shard_map/while/body/eval_jaxpr/sub | solution.py:69
  293.1 5.8 %add_subtract_fusion.4 = (f32[24,8,4096]{2,1,0:T(8,128)S(1)}, f32[24,8,4096]{2,1,0:T(8,128)}) fusion(f32[24,8,4096]{2,1,0:T(8,128)S(1)} %get-tuple-element.254, f32[24,8]{1,0:T(8,128)S(1)} %get-tuple-element.236, f32[24,8]{1,0:T(8,128)S(1)} %get-tuple-element.237, f32[8,4096]{1,0:T(8,128)S(1)} %get-tuple-element.230, ...), kind=kLoop, calls=%fused_computation.clone.1 | loop fusion | flops 6291456 | bytes 12846592 | tf_op jit(solution)/shard_map/while/body/eval_jaxpr/sub | solution.py:69
  304.7 5.8 %add_subtract_fusion.4 = (f32[24,8,4096]{2,1,0:T(8,128)S(1)}, f32[24,8,4096]{2,1,0:T(8,128)}) fusion(f32[24,8,4096]{2,1,0:T(8,128)S(1)} %get-tuple-element.254, f32[24,8]{1,0:T(8,128)S(1)} %get-tuple-element.236, f32[24,8]{1,0:T(8,128)S(1)} %get-tuple-element.237, f32[8,4096]{1,0:T(8,128)S(1)} %get-tuple-element.230, ...), kind=kLoop, calls=%fused_computation.clone.1 | loop fusion | flops 6291456 | bytes 12846592 | tf_op jit(solution)/shard_map/while/body/eval_jaxpr/sub | solution.py:69
  316.3 5.8 %add_subtract_fusion.4 = (f32[24,8,4096]{2,1,0:T(8,128)S(1)}, f32[24,8,4096]{2,1,0:T(8,128)}) fusion(f32[24,8,4096]{2,1,0:T(8,128)S(1)} %get-tuple-element.254, f32[24,8]{1,0:T(8,128)S(1)} %get-tuple-element.236, f32[24,8]{1,0:T(8,128)S(1)} %get-tuple-element.237, f32[8,4096]{1,0:T(8,128)S(1)} %get-tuple-element.230, ...), kind=kLoop, calls=%fused_computation.clone.1 | loop fusion | flops 6291456 | bytes 12846592 | tf_op jit(solution)/shard_map/while/body/eval_jaxpr/sub | solution.py:69
  327.9 5.8 %add_subtract_fusion.4 = (f32[24,8,4096]{2,1,0:T(8,128)S(1)}, f32[24,8,4096]{2,1,0:T(8,128)}) fusion(f32[24,8,4096]{2,1,0:T(8,128)S(1)} %get-tuple-element.254, f32[24,8]{1,0:T(8,128)S(1)} %get-tuple-element.236, f32[24,8]{1,0:T(8,128)S(1)} %get-tuple-element.237, f32[8,4096]{1,0:T(8,128)S(1)} %get-tuple-element.230, ...), kind=kLoop, calls=%fused_computation.clone.1 | loop fusion | flops 6291456 | bytes 12846592 | tf_op jit(solution)/shard_map/while/body/eval_jaxpr/sub | solution.py:69
  339.6 5.8 %add_subtract_fusion.4 = (f32[24,8,4096]{2,1,0:T(8,128)S(1)}, f32[24,8,4096]{2,1,0:T(8,128)}) fusion(f32[24,8,4096]{2,1,0:T(8,128)S(1)} %get-tuple-element.254, f32[24,8]{1,0:T(8,128)S(1)} %get-tuple-element.236, f32[24,8]{1,0:T(8,128)S(1)} %get-tuple-element.237, f32[8,4096]{1,0:T(8,128)S(1)} %get-tuple-element.230, ...), kind=kLoop, calls=%fused_computation.clone.1 | loop fusion | flops 6291456 | bytes 12846592 | tf_op jit(solution)/shard_map/while/body/eval_jaxpr/sub | solution.py:69
  351.2 5.8 %add_subtract_fusion.4 = (f32[24,8,4096]{2,1,0:T(8,128)S(1)}, f32[24,8,4096]{2,1,0:T(8,128)}) fusion(f32[24,8,4096]{2,1,0:T(8,128)S(1)} %get-tuple-element.254, f32[24,8]{1,0:T(8,128)S(1)} %get-tuple-element.236, f32[24,8]{1,0:T(8,128)S(1)} %get-tuple-element.237, f32[8,4096]{1,0:T(8,128)S(1)} %get-tuple-element.230, ...), kind=kLoop, calls=%fused_computation.clone.1 | loop fusion | flops 6291456 | bytes 12846592 | tf_op jit(solution)/shard_map/while/body/eval_jaxpr/sub | solution.py:69
  362.8 5.8 %add_subtract_fusion.4 = (f32[24,8,4096]{2,1,0:T(8,128)S(1)}, f32[24,8,4096]{2,1,0:T(8,128)}) fusion(f32[24,8,4096]{2,1,0:T(8,128)S(1)} %get-tuple-element.254, f32[24,8]{1,0:T(8,128)S(1)} %get-tuple-element.236, f32[24,8]{1,0:T(8,128)S(1)} %get-tuple-element.237, f32[8,4096]{1,0:T(8,128)S(1)} %get-tuple-element.230, ...), kind=kLoop, calls=%fused_computation.clone.1 | loop fusion | flops 6291456 | bytes 12846592 | tf_op jit(solution)/shard_map/while/body/eval_jaxpr/sub | solution.py:69
  461.7 23.9 %all_gather.7 = f32[24,24,128]{1,0,2:T(8,128)S(1)} all-gather(f32[24,24,8]{1,0,2:T(8,128)S(1)} %copy.90), channel_id=1, replica_groups=mesh['freq'=8,'frame'=16] {'frame'}, dimensions={2}, use_global_device_ids=true | all-gather | bytes 313344 | tf_op jit(solution)/shard_map/all_gather | solution.py:82
  486.8 24.7 %all_gather.6 = f32[24,24,128]{1,0,2:T(8,128)S(1)} all-gather(f32[24,24,8]{1,0,2:T(8,128)S(1)} %copy.89), channel_id=1, replica_groups=mesh['freq'=8,'frame'=16] {'frame'}, dimensions={2}, use_global_device_ids=true | all-gather | bytes 313344 | tf_op jit(solution)/shard_map/all_gather | solution.py:81
  518.3 6.5 %fusion.13 = f32[128,48,256]{2,1,0:T(8,128)S(1)} fusion(f32[48,48,128]{1,0,2:T(8,128)} %copy.95, bf16[48,128,256]{2,1,0:T(8,128)(2,1)S(1)} %bitcast.99), kind=kOutput, calls=%fused_computation.35 | convolution fusion | flops 905969664 | bytes 10616832 | tf_op jit(solution)/shard_map/jaf,aft->jft/dot_general | solution.py:87
  524.8 6.3 %copy.97 = f32[2,24,128,256]{3,2,1,0:T(8,128)} copy(f32[2,24,128,256]{3,1,0,2:T(8,128)S(1)} %bitcast.100) | data formatting | bytes 12582912
  (220 shorter events, 234.6 us)
Async XLA Ops:
  0.6 41.4 %copy-start = (bf16[1024,1024]{1,0:T(8,128)(2,1)S(1)}, bf16[1024,1024]{1,0:T(8,128)(2,1)}, u32[]{:S(2)}) copy-start(bf16[1024,1024]{1,0:T(8,128)(2,1)} %param.14) | copy-start | bytes 6291460
  41.2 0.9 copy-start.4
  41.2 0.9 copy-start.5
  42.1 7.7 %copy-start.6 = (f32[1024]{0:T(1024)S(1)}, f32[1024]{0:T(1024)}, u32[]{:S(2)}) copy-start(f32[1024]{0:T(1024)} %param.17) | copy-start | bytes 12292
  42.1 7.7 %copy-start.7 = (f32[1024]{0:T(1024)S(1)}, f32[1024]{0:T(1024)}, u32[]{:S(2)}) copy-start(f32[1024]{0:T(1024)} %param.15) | copy-start | bytes 12292
  71.0 4.7 copy-start.2
  71.0 26.1 %all-to-all-start.2 = ((bf16[8,2,49152]{2,1,0:T(2,128)(2,1)}), bf16[8,2,49152]{2,1,0:T(2,128)(2,1)}, u32[]{:S(2)}, u32[]{:S(2)}) async-start(bf16[8,2,49152]{2,1,0:T(2,128)(2,1)} %reshape.185), calls=%async_computation.2 | async-start | bytes 3145728 | tf_op jit(solution)/shard_map/all_to_all | solution.py:42
  97.2 55.1 %all-to-all-start = ((bf16[2,24,128,256]{3,1,0,2:T(8,128)(2,1)}), bf16[2,24,128,256]{3,1,0,2:T(8,128)(2,1)}, u32[]{:S(2)}, u32[]{:S(2)}) async-start(bf16[2,24,128,256]{3,1,0,2:T(8,128)(2,1)} %copy.77), calls=%async_computation | async-start | bytes 6291456 | tf_op jit(solution)/shard_map/all_to_all | solution.py:50
  152.3 26.9 %all-to-all-start.3 = ((bf16[24,128,256]{2,0,1:T(8,128)(2,1)}), bf16[24,128,256]{2,0,1:T(8,128)(2,1)}, u32[]{:S(2)}, u32[]{:S(2)}) async-start(bf16[24,128,256]{2,0,1:T(8,128)(2,1)} %copy.87), calls=%async_computation.3 | async-start | bytes 3145728 | tf_op jit(solution)/shard_map/all_to_all | solution.py:51
  512.7 5.6 %copy-start.3 = (bf16[2,24,128,256]{3,2,1,0:T(8,128)(2,1)S(1)}, bf16[2,24,128,256]{3,2,1,0:T(8,128)(2,1)}, u32[]{:S(2)}) copy-start(bf16[2,24,128,256]{3,2,1,0:T(8,128)(2,1)} %param.10) | copy-start | bytes 9437188
  524.8 6.4 %copy-start.1 = (bf16[1024,1024]{1,0:T(8,128)(2,1)S(1)}, bf16[1024,1024]{1,0:T(8,128)(2,1)}, u32[]{:S(2)}) copy-start(bf16[1024,1024]{1,0:T(8,128)(2,1)} %param.14) | copy-start | bytes 6291460

commit v2 on v1

v2 whole, which is shorter than its diff:
```python
import functools

import jax
import jax.numpy as jnp
from jax import lax
from jax.experimental import pallas as pl
from jax.experimental.pallas import tpu as pltpu
from jax.sharding import PartitionSpec as P

epsilon = 1e-05
power_floor = 0.001
variance_floor = 0.25


def source_model(spectra, norm_gain, w_in, b_in, w_mid, b_mid, w_out, b_out):
    real_part = spectra[0].astype(jnp.float32)
    imag_part = spectra[1].astype(jnp.float32)
    logpower = jnp.log(real_part * real_part + imag_part * imag_part + power_floor).astype(
        jnp.bfloat16
    )
    values = lax.all_to_all(logpower, "freq", split_axis=2, concat_axis=1, tiled=True).astype(
        jnp.float32
    )
    average = jnp.mean(values, axis=1, keepdims=True)
    centred = values - average
    spread = jnp.mean(centred * centred, axis=1, keepdims=True)
    normed = (centred * lax.rsqrt(spread + epsilon) * norm_gain[None, :, None]).astype(jnp.bfloat16)
    hidden_one = jax.nn.silu(
        jnp.einsum("nft,fh->nth", normed, w_in, preferred_element_type=jnp.float32) + b_in
    ).astype(jnp.bfloat16)
    hidden_two = jax.nn.silu(
        jnp.einsum("nth,hg->ntg", hidden_one, w_mid, preferred_element_type=jnp.float32) + b_mid
    ).astype(jnp.bfloat16)
    output_pre = (
        jnp.einsum("nth,hf->nft", hidden_two, w_out, preferred_element_type=jnp.float32)
        + b_out[None, :, None]
    )
    frame_variances = (jax.nn.softplus(output_pre) + variance_floor).astype(jnp.bfloat16)
    return lax.all_to_all(frame_variances, "freq", split_axis=1, concat_axis=2, tiled=True)


def sweep_kernel(frames, spec_ref, var_ref, mr_ref, mi_ref, yr, yi, w, pr, pi, pp):
    count, bins, length = yr.shape
    chunk = 512
    chunks = length // chunk

    def init(j, carry):
        yr[j] = spec_ref[0, j].astype(jnp.float32)
        yi[j] = spec_ref[1, j].astype(jnp.float32)
        w[j] = 1.0 / var_ref[j].astype(jnp.float32)
        lane = lax.broadcasted_iota(jnp.int32, (bins, mr_ref.shape[2]), 1)
        mr_ref[j] = jnp.where(lane == j, 1.0, 0.0).astype(jnp.float32)
        mi_ref[j] = jnp.zeros((bins, mr_ref.shape[2]), jnp.float32)
        return carry

    lax.fori_loop(0, count, init, 0)

    def step(k, carry):
        pr[...] = yr[k]
        pi[...] = yi[k]
        pp[...] = pr[...] * pr[...] + pi[...] * pi[...]
        mkr = mr_ref[k]
        mki = mi_ref[k]

        def per_source(j, carry):
            acc_r = jnp.zeros((bins, chunk), jnp.float32)
            acc_i = jnp.zeros((bins, chunk), jnp.float32)
            acc_d = jnp.zeros((bins, chunk), jnp.float32)
            for c in range(chunks):
                sl = pl.ds(c * chunk, chunk)
                a_r = yr[j, :, sl]
                a_i = yi[j, :, sl]
                ww = w[j, :, sl]
                b_r = pr[:, sl]
                b_i = pi[:, sl]
                acc_r = acc_r + ww * (a_r * b_r + a_i * b_i)
                acc_i = acc_i + ww * (a_i * b_r - a_r * b_i)
                acc_d = acc_d + ww * pp[:, sl]
            numer_real = jnp.sum(acc_r, axis=1, keepdims=True) / frames
            numer_imag = jnp.sum(acc_i, axis=1, keepdims=True) / frames
            denom = jnp.sum(acc_d, axis=1, keepdims=True) / frames
            is_self = j == k
            coef_real = jnp.where(is_self, 1.0 - lax.rsqrt(denom), numer_real / denom)
            coef_imag = jnp.where(is_self, 0.0, numer_imag / denom)
            for c in range(chunks):
                sl = pl.ds(c * chunk, chunk)
                b_r = pr[:, sl]
                b_i = pi[:, sl]
                yr[j, :, sl] = yr[j, :, sl] - (coef_real * b_r - coef_imag * b_i)
                yi[j, :, sl] = yi[j, :, sl] - (coef_real * b_i + coef_imag * b_r)
            mr_ref[j] = mr_ref[j] - (coef_real * mkr - coef_imag * mki)
            mi_ref[j] = mi_ref[j] - (coef_real * mki + coef_imag * mkr)
            return carry

        lax.fori_loop(0, count, per_source, 0)
        return carry

    lax.fori_loop(0, count, step, 0)


def sweep(spec_sw, var_sw, frames):
    _, count, bins, length = spec_sw.shape
    lanes = 128
    vmem = pl.BlockSpec(memory_space=pltpu.VMEM)
    return pl.pallas_call(
        functools.partial(sweep_kernel, frames),
        out_shape=(
            jax.ShapeDtypeStruct((count, bins, lanes), jnp.float32),
            jax.ShapeDtypeStruct((count, bins, lanes), jnp.float32),
        ),
        in_specs=[vmem, vmem],
        out_specs=(vmem, vmem),
        scratch_shapes=[
            pltpu.VMEM((count, bins, length), jnp.float32),
            pltpu.VMEM((count, bins, length), jnp.float32),
            pltpu.VMEM((count, bins, length), jnp.float32),
            pltpu.VMEM((bins, length), jnp.float32),
            pltpu.VMEM((bins, length), jnp.float32),
            pltpu.VMEM((bins, length), jnp.float32),
        ],
        compiler_params=pltpu.CompilerParams(vmem_limit_bytes=60 * 1024 * 1024),
    )(spec_sw, var_sw)


def on_device(spectra, norm_gain, w_in, b_in, w_mid, b_mid, w_out, b_out):
    count = spectra.shape[1]
    frames = spectra.shape[3] * lax.axis_size("frame")
    variances = source_model(spectra, norm_gain, w_in, b_in, w_mid, b_mid, w_out, b_out)

    spec_sw = lax.all_to_all(spectra, "frame", split_axis=2, concat_axis=3, tiled=True)
    var_sw = lax.all_to_all(variances, "frame", split_axis=1, concat_axis=2, tiled=True)
    mix_real, mix_imag = sweep(spec_sw, var_sw, frames)
    mix = jnp.stack([mix_real[:, :, :count], mix_imag[:, :, :count]])
    mix = lax.all_gather(mix, "frame", axis=2, tiled=True)
    mix_real, mix_imag = mix[0], mix[1]
    top = jnp.concatenate([mix_real, -mix_imag], axis=2)
    bottom = jnp.concatenate([mix_imag, mix_real], axis=2)
    mix = jnp.concatenate([top, bottom], axis=0)
    stacked = spectra.reshape(2 * count, spectra.shape[2], spectra.shape[3]).astype(jnp.float32)
    demixed = jnp.einsum(
        "jfa,aft->jft", mix, stacked, precision=lax.Precision.HIGHEST,
        preferred_element_type=jnp.float32,
    )
    return (demixed.reshape(spectra.shape), variances)


def solution(mesh):
    in_specs = (P(None, None, "freq", "frame"), P(), P(), P(), P(), P(), P(), P())
    out_specs = (P(None, None, "freq", "frame"), P(None, "freq", "frame"))
    return jax.shard_map(
        on_device, mesh=mesh, in_specs=in_specs, out_specs=out_specs, check_vma=False
    )
```

time: 533 us -> 355 us (0.67)
  other arithmetic: 293 us -> 9.36 us
  Pallas kernels: 0 us -> 105 us
  local copies, waits for them, and re-layouts: 61.3 us -> 76 us
  blocking collectives: 74.6 us -> 63.1 us
    sub x48 -> x0, other arithmetic: 143 us -> none  [the longest x24 140 us: sweep(): new_imag = demix_imag - (coef_real * pick_imag + coef_imag * pick_real)]
    reduce_sum x24 -> x0, other arithmetic: 110 us -> none  [sweep(): jnp.sum(weight * (demix_real * pick_real + demix_imag * pick_imag), axis=2)]
    pallas_call x0 -> x1, Pallas kernels: none -> 105 us  [sweep(): pl.pallas_call(functools.partial(sweep_kernel, frames), out_shape=(jax.Sh...]
    mul x24 -> x0, other arithmetic: 22.5 us -> none  [sweep(): weight * (pick_real * pick_real + pick_imag * pick_imag)]
    all_gather x2 -> x1, blocking collectives: 48.6 us -> 37.1 us  [on_device(): mix = lax.all_gather(mix, 'frame', axis=2, tiled=True)]
    all_to_all x0 -> x2, local copies, waits for them, and re-layouts: none -> 7.58 us  [the longest x1 4.65 us: on_device(): lax.all_to_all(spectra, 'frame', split_axis=2, concat_axis=3, tiled=True)]
    squeeze x0 -> x3, local copies, waits for them, and re-layouts: none -> 7.05 us  [on_device(): mix_real, mix_imag = (mix[0], mix[1])]
    unnamed x23 -> x21, local copies, waits for them, and re-layouts: 34.3 us -> 35.3 us
  transfers between devices with their start and end apart: 3 -> 3, of which waited for: 3 -> 3; matrix products, arithmetic and copies ran while one was open for 5% -> 8% of each run, Pallas kernels for 0% -> 0%
where the time goes in v2:
time: 355 us; the launch traced here: 354 us
  Pallas kernels  105 us (30%)
  local copies, waits for them, and re-layouts  76 us (21%)
  blocking collectives  63.1 us (18%)
  waiting for transfers between devices  62.2 us (18%)
  matrix products  20 us (6%)
  starting transfers between devices  17.2 us (5%)
  other arithmetic  9.36 us (3%)
    pallas_call x1, Pallas kernels, sweep(): pl.pallas_call(functools.partial(sweep_kernel, frames), out_shape=(jax.Sh...  105 us
    all_gather x1, blocking collectives, on_device(): mix = lax.all_gather(mix, 'frame', axis=2, tiled=True)  37.1 us
    unnamed x21, local copies, waits for them, and re-layouts  35.3 us
    all_to_all x1, waiting for transfers between devices, on_device(): lax.all_to_all(spectra, 'frame', split_axis=2, concat_axis=3, tiled=True)  29 us
    all_to_all x1, blocking collectives, source_model(): lax.all_to_all(logpower, 'freq', split_axis=2, concat_axis=1, tiled=True)  26 us
    all_to_all x1, waiting for transfers between devices, source_model(): lax.all_to_all(frame_variances, 'freq', split_axis=1, concat_axis=2, tile...  17.9 us
    all_to_all x1, waiting for transfers between devices, on_device(): lax.all_to_all(variances, 'frame', split_axis=1, concat_axis=2, tiled=True)  15.2 us
    all_to_all x2, local copies, waits for them, and re-layouts, source_model(): lax.all_to_all(frame_variances, 'freq', split_axis=1, concat_axis=2, tile...  10.1 us
  transfers between devices with their start and end apart: 3, of which 3 were waited for; matrix products, arithmetic and copies ran while one was open for 8% of the time, Pallas kernels for 0%

profile of v2, /device:TPU:0, one launch (start us, length us, event | category | flops | bytes accessed | tf_op | source)
XLA Modules:
  0.0 354.0 jit_solution(15910812970390306471)
XLA Ops:
  0.6 4.0 %fusion.41 = (bf16[1,24,128,256]{3,2,1,0:T(8,128)(2,1)}, bf16[1,24,128,256]{3,2,1,0:T(8,128)(2,1)}) fusion(bf16[2,24,128,256]{3,2,1,0:T(8,128)(2,1)} %param.8), kind=kLoop, calls=%fused_computation.47 | loop fusion | bytes 6291456 | tf_op jit(solution)/shard_map/slice | solution.py:16
  4.7 2.8 copy.70
  7.5 2.7 copy.71
  10.2 2.8 fusion.21
  13.0 26.0 %all_to_all.63 = bf16[24,128,256]{1,0,2:T(8,128)(2,1)S(1)} all-to-all(bf16[24,128,256]{1,0,2:T(8,128)(2,1)S(1)} %fusion.21), channel_id=1, replica_groups=mesh['freq'=8,'frame'=16] {'freq'}, dimensions={2} | all-to-all | bytes 3145728 | tf_op jit(solution)/shard_map/all_to_all | solution.py:21
  39.0 2.2 fusion.42
  42.1 7.7 %fusion.17 = f32[24,32,1024]{2,1,0:T(8,128)} fusion(bf16[1024,1024]{1,0:T(8,128)(2,1)S(1)} %copy-done, f32[1024]{0:T(1024)S(1)} %copy-done.3, bf16[1024,1024]{1,0:T(8,128)(2,1)} %param.10, f32[24,8,4,8,128]{4,3,2,1,0:T(8,128)} %get-tuple-element.21, f32[1024]{0:T(1024)S(1)} %copy-done.4, f32[24,32]{1,0:T(8,128)S(1)} %add_rsqrt_fusion, ...), kind=kOutput, calls=%fused_computation.26 | convolution fusion | flops 3229089792 | bytes 10500096 | tf_op jit(solution)/shard_map/nth,hg->ntg/dot_general | solution.py:32
  49.8 5.9 %fusion.5 = bf16[24,1024,32]{1,2,0:T(8,128)(2,1)S(1)} fusion(f32[1024]{0:T(1024)S(1)} %copy-done.5, bf16[1024,1024]{1,0:T(8,128)(2,1)} %param.14, f32[24,32,1024]{2,1,0:T(8,128)} %fusion.17, f32[1024]{0:T(1024)S(1)} %copy-done.6), kind=kOutput, calls=%fused_computation.8 | convolution fusion | flops 1622409216 | bytes 6823936 | tf_op jit(solution)/shard_map/nth,hf->nft/dot_general | solution.py:35
  55.7 5.9 %copy.55 = bf16[24,1024,32]{2,0,1:T(8,128)(2,1)} copy(bf16[24,1024,32]{1,2,0:T(8,128)(2,1)S(1)} %fusion.5) | data formatting | bytes 3145728 | tf_op jit(solution)/shard_map/convert_element_type | solution.py:38
  61.5 9.5 %reshape.49 = bf16[8,2,49152]{2,1,0:T(2,128)(2,1)} reshape(bf16[1024,24,32]{2,1,0:T(8,128)(2,1)} %bitcast.94) | data formatting | bytes 3145728
  71.0 4.7 %all-to-all-start.2 = ((bf16[8,2,49152]{2,1,0:T(2,128)(2,1)}), bf16[8,2,49152]{2,1,0:T(2,128)(2,1)}, u32[]{:S(2)}, u32[]{:S(2)}) async-start(bf16[8,2,49152]{2,1,0:T(2,128)(2,1)} %reshape.49), calls=%async_computation.2 | async-start | bytes 3145728 | tf_op jit(solution)/shard_map/all_to_all | solution.py:39
  75.8 3.4 copy.49
  79.2 17.9 %all-to-all-done.2 = bf16[8,2,49152]{2,1,0:T(2,128)(2,1)} async-done(((bf16[8,2,49152]{2,1,0:T(2,128)(2,1)}), bf16[8,2,49152]{2,1,0:T(2,128)(2,1)}, u32[]{:S(2)}, u32[]{:S(2)}) %all-to-all-start.2) | async-done | bytes 1572896 | tf_op jit(solution)/shard_map/all_to_all | solution.py:39
  97.2 8.1 %all-to-all-start = ((bf16[2,24,128,256]{3,1,0,2:T(8,128)(2,1)}), bf16[2,24,128,256]{3,1,0,2:T(8,128)(2,1)}, u32[]{:S(2)}, u32[]{:S(2)}) async-start(bf16[2,24,128,256]{3,1,0,2:T(8,128)(2,1)} %copy.49), calls=%async_computation | async-start | bytes 6291456 | tf_op jit(solution)/shard_map/all_to_all | solution.py:130
  105.3 7.9 %reshape.50 = bf16[1024,24,32]{2,1,0:T(8,128)(2,1)} reshape(bf16[8,2,49152]{2,1,0:T(2,128)(2,1)} %all-to-all-done.2) | data formatting | bytes 3145728
  113.1 7.3 %copy.57 = bf16[24,128,8,32]{1,3,2,0:T(8,128)(2,1)} copy(bf16[24,128,8,32]{3,0,1,2:T(8,128)(2,1)} %bitcast.95) | data formatting | bytes 3145728 | tf_op jit(solution)/shard_map/all_to_all | solution.py:39
  120.5 2.8 copy.58
  123.3 29.0 %all-to-all-done = bf16[2,24,128,256]{3,1,0,2:T(8,128)(2,1)} async-done(((bf16[2,24,128,256]{3,1,0,2:T(8,128)(2,1)}), bf16[2,24,128,256]{3,1,0,2:T(8,128)(2,1)}, u32[]{:S(2)}, u32[]{:S(2)}) %all-to-all-start) | async-done | bytes 3145760 | tf_op jit(solution)/shard_map/all_to_all | solution.py:130
  152.3 4.4 %all-to-all-start.3 = ((bf16[24,128,256]{2,0,1:T(8,128)(2,1)}), bf16[24,128,256]{2,0,1:T(8,128)(2,1)}, u32[]{:S(2)}, u32[]{:S(2)}) async-start(bf16[24,128,256]{2,0,1:T(8,128)(2,1)} %copy.58), calls=%async_computation.3 | async-start | bytes 3145728 | tf_op jit(solution)/shard_map/all_to_all | solution.py:131
  156.7 2.6 copy.67
  159.3 4.6 %copy.50 = bf16[2,24,16,8,256]{4,3,2,1,0:T(8,128)(2,1)} copy(bf16[2,24,16,8,256]{4,1,0,3,2:T(8,128)(2,1)} %bitcast) | data formatting | bytes 6291456 | tf_op jit(solution)/shard_map/all_to_all | solution.py:130
  163.9 15.2 %all-to-all-done.3 = bf16[24,128,256]{2,0,1:T(8,128)(2,1)} async-done(((bf16[24,128,256]{2,0,1:T(8,128)(2,1)}), bf16[24,128,256]{2,0,1:T(8,128)(2,1)}, u32[]{:S(2)}, u32[]{:S(2)}) %all-to-all-start.3) | async-done | bytes 1572896 | tf_op jit(solution)/shard_map/all_to_all | solution.py:131
  179.2 2.9 copy.59
  182.1 105.3 %shard_map.95 = (f32[24,8,128]{2,1,0:T(8,128)}, f32[24,8,128]{2,1,0:T(8,128)}) custom-call(bf16[2,24,8,4096]{3,2,1,0:T(8,128)(2,1)} %bitcast.100, bf16[24,8,4096]{2,1,0:T(8,128)(2,1)} %bitcast.101), custom_call_target="tpu_custom_call" | custom-call | tf_op jit(solution)/shard_map/pallas_call | solution.py:105
  288.4 37.1 %all_gather.3 = f32[2,24,128,24]{3,2,1,0:T(8,128)S(1)} all-gather(f32[2,24,8,24]{3,2,1,0:T(8,128)S(1)} %pad_maximum_fusion), channel_id=1, replica_groups=mesh['freq'=8,'frame'=16] {'frame'}, dimensions={2}, use_global_device_ids=true | all-gather | bytes 626688 | tf_op jit(solution)/shard_map/all_gather | solution.py:134
  326.8 1.9 slice_bitcast_fusion
  330.5 2.6 copy.62
  333.1 2.6 copy.60
  335.7 2.3 maximum_maximum_fusion
  337.9 3.2 copy.64
  341.1 6.5 %fusion.13 = f32[128,48,256]{2,1,0:T(8,128)S(1)} fusion(f32[48,128,48]{2,0,1:T(8,128)} %copy.64, bf16[48,128,256]{2,1,0:T(8,128)(2,1)S(1)} %bitcast.92), kind=kOutput, calls=%fused_computation.19 | convolution fusion | flops 905969664 | bytes 10616832 | tf_op jit(solution)/shard_map/jfa,aft->jft/dot_general | solution.py:140
  347.6 6.3 %copy.66 = f32[2,24,128,256]{3,2,1,0:T(8,128)} copy(f32[2,24,128,256]{3,1,0,2:T(8,128)S(1)} %bitcast.93) | data formatting | bytes 12582912
  (22 shorter events, 5.0 us)
Async XLA Ops:
  0.6 41.4 %copy-start = (bf16[1024,1024]{1,0:T(8,128)(2,1)S(1)}, bf16[1024,1024]{1,0:T(8,128)(2,1)}, u32[]{:S(2)}) copy-start(bf16[1024,1024]{1,0:T(8,128)(2,1)} %param.12) | copy-start | bytes 6291460
  41.2 0.9 copy-start.3
  41.2 0.9 copy-start.4
  42.1 7.7 %copy-start.5 = (f32[1024]{0:T(1024)S(1)}, f32[1024]{0:T(1024)}, u32[]{:S(2)}) copy-start(f32[1024]{0:T(1024)} %param.15) | copy-start | bytes 12292
  42.1 7.7 %copy-start.6 = (f32[1024]{0:T(1024)S(1)}, f32[1024]{0:T(1024)}, u32[]{:S(2)}) copy-start(f32[1024]{0:T(1024)} %param.13) | copy-start | bytes 12292
  71.0 4.7 %copy-start.2 = (bf16[2,24,128,256]{3,2,1,0:T(8,128)(2,1)S(1)}, bf16[2,24,128,256]{3,2,1,0:T(8,128)(2,1)}, u32[]{:S(2)}) copy-start(bf16[2,24,128,256]{3,2,1,0:T(8,128)(2,1)} %param.8) | copy-start | bytes 9437188
  71.0 26.1 %all-to-all-start.2 = ((bf16[8,2,49152]{2,1,0:T(2,128)(2,1)}), bf16[8,2,49152]{2,1,0:T(2,128)(2,1)}, u32[]{:S(2)}, u32[]{:S(2)}) async-start(bf16[8,2,49152]{2,1,0:T(2,128)(2,1)} %reshape.49), calls=%async_computation.2 | async-start | bytes 3145728 | tf_op jit(solution)/shard_map/all_to_all | solution.py:39
  97.2 55.1 %all-to-all-start = ((bf16[2,24,128,256]{3,1,0,2:T(8,128)(2,1)}), bf16[2,24,128,256]{3,1,0,2:T(8,128)(2,1)}, u32[]{:S(2)}, u32[]{:S(2)}) async-start(bf16[2,24,128,256]{3,1,0,2:T(8,128)(2,1)} %copy.49), calls=%async_computation | async-start | bytes 6291456 | tf_op jit(solution)/shard_map/all_to_all | solution.py:130
  152.3 26.9 %all-to-all-start.3 = ((bf16[24,128,256]{2,0,1:T(8,128)(2,1)}), bf16[24,128,256]{2,0,1:T(8,128)(2,1)}, u32[]{:S(2)}, u32[]{:S(2)}) async-start(bf16[24,128,256]{2,0,1:T(8,128)(2,1)} %copy.58), calls=%async_computation.3 | async-start | bytes 3145728 | tf_op jit(solution)/shard_map/all_to_all | solution.py:131
  347.6 6.4 %copy-start.1 = (bf16[1024,1024]{1,0:T(8,128)(2,1)S(1)}, bf16[1024,1024]{1,0:T(8,128)(2,1)}, u32[]{:S(2)}) copy-start(bf16[1024,1024]{1,0:T(8,128)(2,1)} %param.12) | copy-start | bytes 6291460

commit v3 on v2

--- a/solution.py
+++ b/solution.py
@@ -127,8 +127,9 @@
     frames = spectra.shape[3] * lax.axis_size("frame")
     variances = source_model(spectra, norm_gain, w_in, b_in, w_mid, b_mid, w_out, b_out)
 
-    spec_sw = lax.all_to_all(spectra, "frame", split_axis=2, concat_axis=3, tiled=True)
-    var_sw = lax.all_to_all(variances, "frame", split_axis=1, concat_axis=2, tiled=True)
+    both = jnp.concatenate([spectra, variances[None]], axis=0)
+    both = lax.all_to_all(both, "frame", split_axis=2, concat_axis=3, tiled=True)
+    spec_sw, var_sw = both[:2], both[2]
     mix_real, mix_imag = sweep(spec_sw, var_sw, frames)
     mix = jnp.stack([mix_real[:, :, :count], mix_imag[:, :, :count]])
     mix = lax.all_gather(mix, "frame", axis=2, tiled=True)

time: 355 us -> 380 us (1.070)
  waiting for transfers between devices: 62.2 us -> 85.9 us
  other arithmetic: 9.36 us -> 14.3 us
  starting transfers between devices: 17.2 us -> 12.8 us
    all_to_all x2 -> x1, waiting for transfers between devices: 44.3 us -> 67.9 us  [on_device(): lax.all_to_all(both, 'frame', split_axis=2, concat_axis=3, tiled=True)]
    concatenate x0 -> x1, other arithmetic: none -> 4.96 us  [on_device(): both = jnp.concatenate([spectra, variances[None]], axis=0)]
    all_to_all x2 -> x1, starting transfers between devices: 12.5 us -> 8.09 us  [on_device(): lax.all_to_all(both, 'frame', split_axis=2, concat_axis=3, tiled=True)]
    all_to_all x2 -> x1, local copies, waits for them, and re-layouts: 7.58 us -> 3.46 us  [on_device(): lax.all_to_all(both, 'frame', split_axis=2, concat_axis=3, tiled=True)]
    all_to_all x2 -> x1, local copies, waits for them, and re-layouts: 10.1 us -> 7.32 us  [source_model(): lax.all_to_all(frame_variances, 'freq', split_axis=1, concat_axis=2, tile...]
  transfers between devices with their start and end apart: 3 -> 2, of which waited for: 3 -> 2; matrix products, arithmetic and copies ran while one was open for 8% -> 2% of each run, Pallas kernels for 0% -> 0%
where the time goes in v3:
time: 380 us; the launch traced here: 379 us
  Pallas kernels  105 us (28%)
  waiting for transfers between devices  85.9 us (23%)
  local copies, waits for them, and re-layouts  74.8 us (20%)
  blocking collectives  65.4 us (17%)
  matrix products  20 us (5%)
  other arithmetic  14.3 us (4%)
  starting transfers between devices  12.8 us (3%)
    pallas_call x1, Pallas kernels, sweep(): pl.pallas_call(functools.partial(sweep_kernel, frames), out_shape=(jax.Sh...  105 us
    all_to_all x1, waiting for transfers between devices, on_device(): lax.all_to_all(both, 'frame', split_axis=2, concat_axis=3, tiled=True)  67.9 us
    all_gather x1, blocking collectives, on_device(): mix = lax.all_gather(mix, 'frame', axis=2, tiled=True)  39.4 us
    unnamed x21, local copies, waits for them, and re-layouts  35.3 us
    all_to_all x1, blocking collectives, source_model(): lax.all_to_all(logpower, 'freq', split_axis=2, concat_axis=1, tiled=True)  26 us
    all_to_all x1, waiting for transfers between devices, source_model(): lax.all_to_all(frame_variances, 'freq', split_axis=1, concat_axis=2, tile...  18 us
    all_to_all x1, starting transfers between devices, on_device(): lax.all_to_all(both, 'frame', split_axis=2, concat_axis=3, tiled=True)  8.09 us
    dot_general x1, matrix products, source_model(): jnp.einsum('nth,hg->ntg', hidden_one, w_mid, preferred_element_type=jnp.f...  7.68 us
  transfers between devices with their start and end apart: 2, of which 2 were waited for; matrix products, arithmetic and copies ran while one was open for 2% of the time, Pallas kernels for 0%

profile of v3, /device:TPU:0, one launch (start us, length us, event | category | flops | bytes accessed | tf_op | source)
XLA Modules:
  0.0 379.4 jit_solution(9511525382331380163)
XLA Ops:
  0.6 4.0 %fusion.41 = (bf16[1,24,128,256]{3,2,1,0:T(8,128)(2,1)}, bf16[1,24,128,256]{3,2,1,0:T(8,128)(2,1)}) fusion(bf16[2,24,128,256]{3,2,1,0:T(8,128)(2,1)} %param.8), kind=kLoop, calls=%fused_computation.49 | loop fusion | bytes 6291456 | tf_op jit(solution)/shard_map/slice | solution.py:16
  4.7 2.8 copy.71
  7.5 2.7 copy.72
  10.2 2.8 fusion.21
  13.0 26.0 %all_to_all.42 = bf16[24,128,256]{1,0,2:T(8,128)(2,1)S(1)} all-to-all(bf16[24,128,256]{1,0,2:T(8,128)(2,1)S(1)} %fusion.21), channel_id=1, replica_groups=mesh['freq'=8,'frame'=16] {'freq'}, dimensions={2} | all-to-all | bytes 3145728 | tf_op jit(solution)/shard_map/all_to_all | solution.py:21
  39.0 2.2 fusion.42
  42.1 7.7 %fusion.17 = f32[24,32,1024]{2,1,0:T(8,128)} fusion(bf16[1024,1024]{1,0:T(8,128)(2,1)S(1)} %copy-done, f32[1024]{0:T(1024)S(1)} %copy-done.3, bf16[1024,1024]{1,0:T(8,128)(2,1)} %param.10, f32[24,8,4,8,128]{4,3,2,1,0:T(8,128)} %get-tuple-element.21, f32[1024]{0:T(1024)S(1)} %copy-done.4, f32[24,32]{1,0:T(8,128)S(1)} %add_rsqrt_fusion, ...), kind=kOutput, calls=%fused_computation.28 | convolution fusion | flops 3229089792 | bytes 10500096 | tf_op jit(solution)/shard_map/nth,hg->ntg/dot_general | solution.py:32
  49.8 5.9 %fusion.5 = bf16[24,1024,32]{1,2,0:T(8,128)(2,1)S(1)} fusion(f32[1024]{0:T(1024)S(1)} %copy-done.5, bf16[1024,1024]{1,0:T(8,128)(2,1)} %param.14, f32[24,32,1024]{2,1,0:T(8,128)} %fusion.17, f32[1024]{0:T(1024)S(1)} %copy-done.6), kind=kOutput, calls=%fused_computation.10 | convolution fusion | flops 1622409216 | bytes 6823936 | tf_op jit(solution)/shard_map/nth,hf->nft/dot_general | solution.py:35
  55.7 5.9 %copy.53 = bf16[24,1024,32]{2,0,1:T(8,128)(2,1)} copy(bf16[24,1024,32]{1,2,0:T(8,128)(2,1)S(1)} %fusion.5) | data formatting | bytes 3145728 | tf_op jit(solution)/shard_map/convert_element_type | solution.py:38
  61.6 9.5 %reshape.53 = bf16[8,2,49152]{2,1,0:T(2,128)(2,1)} reshape(bf16[1024,24,32]{2,1,0:T(8,128)(2,1)} %bitcast.93) | data formatting | bytes 3145728
  71.1 4.7 %all-to-all-start.1 = ((bf16[8,2,49152]{2,1,0:T(2,128)(2,1)}), bf16[8,2,49152]{2,1,0:T(2,128)(2,1)}, u32[]{:S(2)}, u32[]{:S(2)}) async-start(bf16[8,2,49152]{2,1,0:T(2,128)(2,1)} %reshape.53), calls=%async_computation.1 | async-start | bytes 3145728 | tf_op jit(solution)/shard_map/all_to_all | solution.py:39
  75.8 3.4 copy.56
  79.2 18.0 %all-to-all-done.1 = bf16[8,2,49152]{2,1,0:T(2,128)(2,1)} async-done(((bf16[8,2,49152]{2,1,0:T(2,128)(2,1)}), bf16[8,2,49152]{2,1,0:T(2,128)(2,1)}, u32[]{:S(2)}, u32[]{:S(2)}) %all-to-all-start.1) | async-done | bytes 1572896 | tf_op jit(solution)/shard_map/all_to_all | solution.py:39
  97.2 7.9 %reshape.54 = bf16[1024,24,32]{2,1,0:T(8,128)(2,1)} reshape(bf16[8,2,49152]{2,1,0:T(2,128)(2,1)} %all-to-all-done.1) | data formatting | bytes 3145728
  105.1 7.3 %copy.55 = bf16[24,128,8,32]{1,3,2,0:T(8,128)(2,1)} copy(bf16[24,128,8,32]{3,0,1,2:T(8,128)(2,1)} %bitcast.94) | data formatting | bytes 3145728 | tf_op jit(solution)/shard_map/all_to_all | solution.py:39
  112.4 2.8 copy.57
  115.1 5.0 %pad_maximum_fusion = bf16[3,24,128,256]{3,1,0,2:T(8,128)(2,1)} fusion(bf16[1,24,128,256]{3,1,0,2:T(8,128)(2,1)} %copy.57, bf16[2,24,128,256]{3,1,0,2:T(8,128)(2,1)} %copy.56), kind=kLoop, calls=%fused_computation.1 | loop fusion | flops 2359296 | bytes 9437184 | tf_op jit(solution)/shard_map/concatenate | solution.py:130
  120.1 8.1 %all-to-all-start.2 = ((bf16[3,24,128,256]{3,1,0,2:T(8,128)(2,1)}), bf16[3,24,128,256]{3,1,0,2:T(8,128)(2,1)}, u32[]{:S(2)}, u32[]{:S(2)}) async-start(bf16[3,24,128,256]{3,1,0,2:T(8,128)(2,1)} %pad_maximum_fusion), calls=%async_computation.2 | async-start | bytes 9437184 | tf_op jit(solution)/shard_map/all_to_all | solution.py:131
  128.2 2.6 copy.67
  130.8 67.9 %all-to-all-done.2 = bf16[3,24,128,256]{3,1,0,2:T(8,128)(2,1)} async-done(((bf16[3,24,128,256]{3,1,0,2:T(8,128)(2,1)}), bf16[3,24,128,256]{3,1,0,2:T(8,128)(2,1)}, u32[]{:S(2)}, u32[]{:S(2)}) %all-to-all-start.2) | async-done | bytes 4718624 | tf_op jit(solution)/shard_map/all_to_all | solution.py:131
  198.7 3.5 copy.85
  203.4 1.9 slice.37
  205.3 105.3 %shard_map.95 = (f32[24,8,128]{2,1,0:T(8,128)}, f32[24,8,128]{2,1,0:T(8,128)}) custom-call(bf16[2,24,8,4096]{3,2,1,0:T(8,128)(2,1)} %bitcast.101, bf16[24,8,4096]{2,1,0:T(8,128)(2,1)} %bitcast.102), custom_call_target="tpu_custom_call" | custom-call | tf_op jit(solution)/shard_map/pallas_call | solution.py:105
  311.5 39.4 %all_gather.3 = f32[2,24,128,24]{3,2,1,0:T(8,128)S(1)} all-gather(f32[2,24,8,24]{3,2,1,0:T(8,128)S(1)} %pad_maximum_fusion.1), channel_id=1, replica_groups=mesh['freq'=8,'frame'=16] {'frame'}, dimensions={2}, use_global_device_ids=true | all-gather | bytes 626688 | tf_op jit(solution)/shard_map/all_gather | solution.py:135
  352.3 1.9 slice_bitcast_fusion
  354.1 1.8 copy.60
  356.0 2.6 copy.61
  358.5 2.6 copy.59
  361.1 2.2 maximum_maximum_fusion
  363.4 3.2 copy.63
  366.6 6.5 %fusion.13 = f32[128,48,256]{2,1,0:T(8,128)S(1)} fusion(f32[48,128,48]{2,0,1:T(8,128)} %copy.63, bf16[48,128,256]{2,1,0:T(8,128)(2,1)S(1)} %bitcast.91), kind=kOutput, calls=%fused_computation.21 | convolution fusion | flops 905969664 | bytes 10616832 | tf_op jit(solution)/shard_map/jfa,aft->jft/dot_general | solution.py:141
  373.0 6.3 %copy.66 = f32[2,24,128,256]{3,2,1,0:T(8,128)} copy(f32[2,24,128,256]{3,1,0,2:T(8,128)S(1)} %bitcast.92) | data formatting | bytes 12582912
  (22 shorter events, 4.4 us)
Async XLA Ops:
  0.6 41.4 %copy-start = (bf16[1024,1024]{1,0:T(8,128)(2,1)S(1)}, bf16[1024,1024]{1,0:T(8,128)(2,1)}, u32[]{:S(2)}) copy-start(bf16[1024,1024]{1,0:T(8,128)(2,1)} %param.12) | copy-start | bytes 6291460
  41.2 0.9 copy-start.3
  41.2 0.9 copy-start.4
  42.1 7.7 %copy-start.5 = (f32[1024]{0:T(1024)S(1)}, f32[1024]{0:T(1024)}, u32[]{:S(2)}) copy-start(f32[1024]{0:T(1024)} %param.15) | copy-start | bytes 12292
  42.1 7.7 %copy-start.6 = (f32[1024]{0:T(1024)S(1)}, f32[1024]{0:T(1024)}, u32[]{:S(2)}) copy-start(f32[1024]{0:T(1024)} %param.13) | copy-start | bytes 12292
  71.1 4.8 %copy-start.2 = (bf16[2,24,128,256]{3,2,1,0:T(8,128)(2,1)S(1)}, bf16[2,24,128,256]{3,2,1,0:T(8,128)(2,1)}, u32[]{:S(2)}) copy-start(bf16[2,24,128,256]{3,2,1,0:T(8,128)(2,1)} %param.8) | copy-start | bytes 9437188
  71.1 26.2 %all-to-all-start.1 = ((bf16[8,2,49152]{2,1,0:T(2,128)(2,1)}), bf16[8,2,49152]{2,1,0:T(2,128)(2,1)}, u32[]{:S(2)}, u32[]{:S(2)}) async-start(bf16[8,2,49152]{2,1,0:T(2,128)(2,1)} %reshape.53), calls=%async_computation.1 | async-start | bytes 3145728 | tf_op jit(solution)/shard_map/all_to_all | solution.py:39
  120.1 78.6 %all-to-all-start.2 = ((bf16[3,24,128,256]{3,1,0,2:T(8,128)(2,1)}), bf16[3,24,128,256]{3,1,0,2:T(8,128)(2,1)}, u32[]{:S(2)}, u32[]{:S(2)}) async-start(bf16[3,24,128,256]{3,1,0,2:T(8,128)(2,1)} %pad_maximum_fusion), calls=%async_computation.2 | async-start | bytes 9437184 | tf_op jit(solution)/shard_map/all_to_all | solution.py:131
  373.0 6.4 %copy-start.1 = (bf16[1024,1024]{1,0:T(8,128)(2,1)S(1)}, bf16[1024,1024]{1,0:T(8,128)(2,1)}, u32[]{:S(2)}) copy-start(bf16[1024,1024]{1,0:T(8,128)(2,1)} %param.12) | copy-start | bytes 6291460

commit v4 on v2

--- a/solution.py
+++ b/solution.py
@@ -122,6 +122,53 @@
     )(spec_sw, var_sw)
 
 
+def gather_kernel(x_ref, o_ref, send_sem, recv_sem, local_sem):
+    n = o_ref.shape[0]
+    me = lax.axis_index("frame")
+    fq = lax.axis_index("freq")
+    barrier = pltpu.get_barrier_semaphore()
+    for d in range(1, n):
+        peer = lax.rem(me + d, n)
+        pl.semaphore_signal(barrier, inc=1, device_id=(fq, peer), device_id_type=pl.DeviceIdType.MESH)
+    pl.semaphore_wait(barrier, n - 1)
+    local = pltpu.make_async_copy(x_ref, o_ref.at[me], local_sem)
+    local.start()
+    copies = []
+    for d in range(1, n):
+        peer = lax.rem(me + d, n)
+        copy = pltpu.make_async_remote_copy(
+            src_ref=x_ref, dst_ref=o_ref.at[me], send_sem=send_sem.at[d], recv_sem=recv_sem.at[d],
+            device_id=(fq, peer), device_id_type=pl.DeviceIdType.MESH,
+        )
+        copy.start()
+        copies.append(copy)
+    for d in range(1, n):
+        source = lax.rem(me + n - d, n)
+        copies[d - 1].wait_send()
+        incoming = pltpu.make_async_remote_copy(
+            src_ref=x_ref, dst_ref=o_ref.at[source], send_sem=send_sem.at[d], recv_sem=recv_sem.at[d],
+            device_id=(fq, source), device_id_type=pl.DeviceIdType.MESH,
+        )
+        incoming.wait_recv()
+    local.wait()
+
+
+def frame_gather(x, n):
+    vmem = pl.BlockSpec(memory_space=pltpu.VMEM)
+    return pl.pallas_call(
+        gather_kernel,
+        out_shape=jax.ShapeDtypeStruct((n,) + x.shape, x.dtype),
+        in_specs=[vmem],
+        out_specs=vmem,
+        scratch_shapes=[
+            pltpu.SemaphoreType.DMA((n,)),
+            pltpu.SemaphoreType.DMA((n,)),
+            pltpu.SemaphoreType.DMA,
+        ],
+        compiler_params=pltpu.CompilerParams(collective_id=0, has_side_effects=True),
+    )(x)
+
+
 def on_device(spectra, norm_gain, w_in, b_in, w_mid, b_mid, w_out, b_out):
     count = spectra.shape[1]
     frames = spectra.shape[3] * lax.axis_size("frame")
@@ -131,7 +178,11 @@
     var_sw = lax.all_to_all(variances, "frame", split_axis=1, concat_axis=2, tiled=True)
     mix_real, mix_imag = sweep(spec_sw, var_sw, frames)
     mix = jnp.stack([mix_real[:, :, :count], mix_imag[:, :, :count]])
-    mix = lax.all_gather(mix, "frame", axis=2, tiled=True)
+    peers = lax.axis_size("frame")
+    bins = mix.shape[2]
+    mix = frame_gather(mix.reshape(-1, 128), peers)
+    mix = mix.reshape(peers, 2, count, bins, count).transpose(1, 2, 0, 3, 4)
+    mix = mix.reshape(2, count, peers * bins, count)
     mix_real, mix_imag = mix[0], mix[1]
     top = jnp.concatenate([mix_real, -mix_imag], axis=2)
     bottom = jnp.concatenate([mix_imag, mix_real], axis=2)

time: 355 us -> 338 us (0.952)
  blocking collectives: 63.1 us -> 26 us
  Pallas kernels: 105 us -> 117 us
  local copies, waits for them, and re-layouts: 76 us -> 83.1 us
    all_gather x1 -> x0, blocking collectives: 37.1 us -> none  [on_device(): mix = lax.all_gather(mix, 'frame', axis=2, tiled=True)]
    pallas_call x0 -> x1, Pallas kernels: none -> 11.9 us  [frame_gather(): pl.pallas_call(gather_kernel, out_shape=jax.ShapeDtypeStruct((n,) + x.sha...]
    reshape x0 -> x3, local copies, waits for them, and re-layouts: none -> 7.12 us  [the longest x2 6.36 us: on_device(): mix = mix.reshape(peers, 2, count, bins, count).transpose(1, 2, 0, 3, 4)]
  transfers between devices with their start and end apart: 3 -> 3, of which waited for: 3 -> 3; matrix products, arithmetic and copies ran while one was open for 8% -> 9% of each run, Pallas kernels for 0% -> 0%
where the time goes in v4:
time: 338 us; the launch traced here: 336 us
  Pallas kernels  117 us (35%)
  local copies, waits for them, and re-layouts  83.1 us (25%)
  waiting for transfers between devices  62.2 us (18%)
  blocking collectives  26 us (8%)
  matrix products  20 us (6%)
  starting transfers between devices  17.2 us (5%)
  other arithmetic  9.37 us (3%)
    pallas_call x1, Pallas kernels, sweep(): pl.pallas_call(functools.partial(sweep_kernel, frames), out_shape=(jax.Sh...  105 us
    unnamed x21, local copies, waits for them, and re-layouts  35.3 us
    all_to_all x1, waiting for transfers between devices, on_device(): lax.all_to_all(spectra, 'frame', split_axis=2, concat_axis=3, tiled=True)  29 us
    all_to_all x1, blocking collectives, source_model(): lax.all_to_all(logpower, 'freq', split_axis=2, concat_axis=1, tiled=True)  26 us
    all_to_all x1, waiting for transfers between devices, source_model(): lax.all_to_all(frame_variances, 'freq', split_axis=1, concat_axis=2, tile...  17.9 us
    all_to_all x1, waiting for transfers between devices, on_device(): lax.all_to_all(variances, 'frame', split_axis=1, concat_axis=2, tiled=True)  15.2 us
    pallas_call x1, Pallas kernels, frame_gather(): pl.pallas_call(gather_kernel, out_shape=jax.ShapeDtypeStruct((n,) + x.sha...  11.9 us
    all_to_all x2, local copies, waits for them, and re-layouts, source_model(): lax.all_to_all(frame_variances, 'freq', split_axis=1, concat_axis=2, tile...  10.1 us
  transfers between devices with their start and end apart: 3, of which 3 were waited for; matrix products, arithmetic and copies ran while one was open for 9% of the time, Pallas kernels for 0%

profile of v4, /device:TPU:0, one launch (start us, length us, event | category | flops | bytes accessed | tf_op | source)
XLA Modules:
  0.0 335.9 jit_solution(17380874311591759771)
XLA Ops:
  0.6 4.0 %fusion.41 = (bf16[1,24,128,256]{3,2,1,0:T(8,128)(2,1)}, bf16[1,24,128,256]{3,2,1,0:T(8,128)(2,1)}) fusion(bf16[2,24,128,256]{3,2,1,0:T(8,128)(2,1)} %param.8), kind=kLoop, calls=%fused_computation.48 | loop fusion | bytes 6291456 | tf_op jit(solution)/shard_map/slice | solution.py:16
  4.7 2.8 copy.72
  7.5 2.7 copy.73
  10.2 2.8 fusion.21
  13.0 26.0 %all_to_all.63 = bf16[24,128,256]{1,0,2:T(8,128)(2,1)S(1)} all-to-all(bf16[24,128,256]{1,0,2:T(8,128)(2,1)S(1)} %fusion.21), channel_id=1, replica_groups=mesh['freq'=8,'frame'=16] {'freq'}, dimensions={2} | all-to-all | bytes 3145728 | tf_op jit(solution)/shard_map/all_to_all | solution.py:21
  42.1 7.7 %fusion.17 = f32[24,32,1024]{2,1,0:T(8,128)} fusion(bf16[1024,1024]{1,0:T(8,128)(2,1)S(1)} %copy-done, f32[1024]{0:T(1024)S(1)} %copy-done.3, bf16[1024,1024]{1,0:T(8,128)(2,1)} %param.10, f32[24,8,4,8,128]{4,3,2,1,0:T(8,128)} %get-tuple-element.21, f32[1024]{0:T(1024)S(1)} %copy-done.4, f32[24,32]{1,0:T(8,128)S(1)} %add_rsqrt_fusion, ...), kind=kOutput, calls=%fused_computation.27 | convolution fusion | flops 3229089792 | bytes 10500096 | tf_op jit(solution)/shard_map/nth,hg->ntg/dot_general | solution.py:32
  49.8 5.9 %fusion.5 = bf16[24,1024,32]{1,2,0:T(8,128)(2,1)S(1)} fusion(f32[1024]{0:T(1024)S(1)} %copy-done.5, bf16[1024,1024]{1,0:T(8,128)(2,1)} %param.14, f32[24,32,1024]{2,1,0:T(8,128)} %fusion.17, f32[1024]{0:T(1024)S(1)} %copy-done.6), kind=kOutput, calls=%fused_computation.8 | convolution fusion | flops 1622409216 | bytes 6823936 | tf_op jit(solution)/shard_map/nth,hf->nft/dot_general | solution.py:35
  55.7 5.9 %copy.56 = bf16[24,1024,32]{2,0,1:T(8,128)(2,1)} copy(bf16[24,1024,32]{1,2,0:T(8,128)(2,1)S(1)} %fusion.5) | data formatting | bytes 3145728 | tf_op jit(solution)/shard_map/convert_element_type | solution.py:38
  61.5 9.5 %reshape.62 = bf16[8,2,49152]{2,1,0:T(2,128)(2,1)} reshape(bf16[1024,24,32]{2,1,0:T(8,128)(2,1)} %bitcast.99) | data formatting | bytes 3145728
  71.0 4.7 %all-to-all-start.2 = ((bf16[8,2,49152]{2,1,0:T(2,128)(2,1)}), bf16[8,2,49152]{2,1,0:T(2,128)(2,1)}, u32[]{:S(2)}, u32[]{:S(2)}) async-start(bf16[8,2,49152]{2,1,0:T(2,128)(2,1)} %reshape.62), calls=%async_computation.2 | async-start | bytes 3145728 | tf_op jit(solution)/shard_map/all_to_all | solution.py:39
  75.8 3.4 %copy.50 = bf16[2,24,128,256]{3,1,0,2:T(8,128)(2,1)} copy(bf16[2,24,128,256]{3,2,1,0:T(8,128)(2,1)S(1)} %copy-done.2) | data formatting | bytes 6291456 | tf_op args[0]
  79.2 17.9 %all-to-all-done.2 = bf16[8,2,49152]{2,1,0:T(2,128)(2,1)} async-done(((bf16[8,2,49152]{2,1,0:T(2,128)(2,1)}), bf16[8,2,49152]{2,1,0:T(2,128)(2,1)}, u32[]{:S(2)}, u32[]{:S(2)}) %all-to-all-start.2) | async-done | bytes 1572896 | tf_op jit(solution)/shard_map/all_to_all | solution.py:39
  97.2 8.1 %all-to-all-start = ((bf16[2,24,128,256]{3,1,0,2:T(8,128)(2,1)}), bf16[2,24,128,256]{3,1,0,2:T(8,128)(2,1)}, u32[]{:S(2)}, u32[]{:S(2)}) async-start(bf16[2,24,128,256]{3,1,0,2:T(8,128)(2,1)} %copy.50), calls=%async_computation | async-start | bytes 6291456 | tf_op jit(solution)/shard_map/all_to_all | solution.py:177
  105.3 7.9 %reshape.63 = bf16[1024,24,32]{2,1,0:T(8,128)(2,1)} reshape(bf16[8,2,49152]{2,1,0:T(2,128)(2,1)} %all-to-all-done.2) | data formatting | bytes 3145728
  113.1 7.3 %copy.58 = bf16[24,128,8,32]{1,3,2,0:T(8,128)(2,1)} copy(bf16[24,128,8,32]{3,0,1,2:T(8,128)(2,1)} %bitcast.100) | data formatting | bytes 3145728 | tf_op jit(solution)/shard_map/all_to_all | solution.py:39
  120.5 2.8 copy.59
  123.3 29.0 %all-to-all-done = bf16[2,24,128,256]{3,1,0,2:T(8,128)(2,1)} async-done(((bf16[2,24,128,256]{3,1,0,2:T(8,128)(2,1)}), bf16[2,24,128,256]{3,1,0,2:T(8,128)(2,1)}, u32[]{:S(2)}, u32[]{:S(2)}) %all-to-all-start) | async-done | bytes 3145760 | tf_op jit(solution)/shard_map/all_to_all | solution.py:177
  152.3 4.4 %all-to-all-start.3 = ((bf16[24,128,256]{2,0,1:T(8,128)(2,1)}), bf16[24,128,256]{2,0,1:T(8,128)(2,1)}, u32[]{:S(2)}, u32[]{:S(2)}) async-start(bf16[24,128,256]{2,0,1:T(8,128)(2,1)} %copy.59), calls=%async_computation.3 | async-start | bytes 3145728 | tf_op jit(solution)/shard_map/all_to_all | solution.py:178
  156.7 2.6 copy.69
  159.3 4.6 %copy.51 = bf16[2,24,16,8,256]{4,3,2,1,0:T(8,128)(2,1)} copy(bf16[2,24,16,8,256]{4,1,0,3,2:T(8,128)(2,1)} %bitcast) | data formatting | bytes 6291456 | tf_op jit(solution)/shard_map/all_to_all | solution.py:177
  163.9 15.2 %all-to-all-done.3 = bf16[24,128,256]{2,0,1:T(8,128)(2,1)} async-done(((bf16[24,128,256]{2,0,1:T(8,128)(2,1)}), bf16[24,128,256]{2,0,1:T(8,128)(2,1)}, u32[]{:S(2)}, u32[]{:S(2)}) %all-to-all-start.3) | async-done | bytes 1572896 | tf_op jit(solution)/shard_map/all_to_all | solution.py:178
  179.2 2.9 copy.60
  182.1 105.3 %shard_map.95 = (f32[24,8,128]{2,1,0:T(8,128)}, f32[24,8,128]{2,1,0:T(8,128)}) custom-call(bf16[2,24,8,4096]{3,2,1,0:T(8,128)(2,1)} %bitcast.107, bf16[24,8,4096]{2,1,0:T(8,128)(2,1)} %bitcast.108), custom_call_target="tpu_custom_call" | custom-call | tf_op jit(solution)/shard_map/pallas_call | solution.py:105
  289.2 11.9 %shard_map.96 = f32[16,72,128]{2,1,0:T(8,128)} custom-call(f32[72,128]{1,0:T(8,128)} %reshape.50.x_ref), custom_call_target="tpu_custom_call" | custom-call | tf_op jit(solution)/shard_map/pallas_call | solution.py:158
  301.1 4.1 %reshape.51 = f32[16,2,24,8,24]{4,3,2,1,0:T(8,128)} reshape(f32[16,72,128]{2,1,0:T(8,128)} %shard_map.96) | data formatting | bytes 1179648 | tf_op jit(solution)/shard_map/reshape | solution.py:184
  305.2 2.3 copy.86
  312.5 2.6 copy.64
  315.1 2.6 copy.62
  317.6 2.3 maximum_maximum_fusion
  319.9 3.2 copy.66
  323.1 6.5 %fusion.13 = f32[128,48,256]{2,1,0:T(8,128)S(1)} fusion(f32[48,128,48]{2,0,1:T(8,128)} %copy.66, bf16[48,128,256]{2,1,0:T(8,128)(2,1)S(1)} %bitcast.97), kind=kOutput, calls=%fused_computation.19 | convolution fusion | flops 905969664 | bytes 10616832 | tf_op jit(solution)/shard_map/jfa,aft->jft/dot_general | solution.py:191
  329.6 6.3 %copy.68 = f32[2,24,128,256]{3,2,1,0:T(8,128)} copy(f32[2,24,128,256]{3,1,0,2:T(8,128)S(1)} %bitcast.98) | data formatting | bytes 12582912
  (25 shorter events, 9.8 us)
Async XLA Ops:
  0.6 41.4 %copy-start = (bf16[1024,1024]{1,0:T(8,128)(2,1)S(1)}, bf16[1024,1024]{1,0:T(8,128)(2,1)}, u32[]{:S(2)}) copy-start(bf16[1024,1024]{1,0:T(8,128)(2,1)} %param.12) | copy-start | bytes 6291460
  41.2 0.9 copy-start.3
  41.2 0.9 copy-start.4
  42.1 7.7 %copy-start.5 = (f32[1024]{0:T(1024)S(1)}, f32[1024]{0:T(1024)}, u32[]{:S(2)}) copy-start(f32[1024]{0:T(1024)} %param.15) | copy-start | bytes 12292
  42.1 7.7 %copy-start.6 = (f32[1024]{0:T(1024)S(1)}, f32[1024]{0:T(1024)}, u32[]{:S(2)}) copy-start(f32[1024]{0:T(1024)} %param.13) | copy-start | bytes 12292
  71.0 4.7 %copy-start.2 = (bf16[2,24,128,256]{3,2,1,0:T(8,128)(2,1)S(1)}, bf16[2,24,128,256]{3,2,1,0:T(8,128)(2,1)}, u32[]{:S(2)}) copy-start(bf16[2,24,128,256]{3,2,1,0:T(8,128)(2,1)} %param.8) | copy-start | bytes 9437188
  71.0 26.1 %all-to-all-start.2 = ((bf16[8,2,49152]{2,1,0:T(2,128)(2,1)}), bf16[8,2,49152]{2,1,0:T(2,128)(2,1)}, u32[]{:S(2)}, u32[]{:S(2)}) async-start(bf16[8,2,49152]{2,1,0:T(2,128)(2,1)} %reshape.62), calls=%async_computation.2 | async-start | bytes 3145728 | tf_op jit(solution)/shard_map/all_to_all | solution.py:39
  97.2 55.1 %all-to-all-start = ((bf16[2,24,128,256]{3,1,0,2:T(8,128)(2,1)}), bf16[2,24,128,256]{3,1,0,2:T(8,128)(2,1)}, u32[]{:S(2)}, u32[]{:S(2)}) async-start(bf16[2,24,128,256]{3,1,0,2:T(8,128)(2,1)} %copy.50), calls=%async_computation | async-start | bytes 6291456 | tf_op jit(solution)/shard_map/all_to_all | solution.py:177
  152.3 26.9 %all-to-all-start.3 = ((bf16[24,128,256]{2,0,1:T(8,128)(2,1)}), bf16[24,128,256]{2,0,1:T(8,128)(2,1)}, u32[]{:S(2)}, u32[]{:S(2)}) async-start(bf16[24,128,256]{2,0,1:T(8,128)(2,1)} %copy.59), calls=%async_computation.3 | async-start | bytes 3145728 | tf_op jit(solution)/shard_map/all_to_all | solution.py:178
  329.5 6.4 %copy-start.1 = (bf16[1024,1024]{1,0:T(8,128)(2,1)S(1)}, bf16[1024,1024]{1,0:T(8,128)(2,1)}, u32[]{:S(2)}) copy-start(bf16[1024,1024]{1,0:T(8,128)(2,1)} %param.12) | copy-start | bytes 6291460

commit v5 on v4

--- a/solution.py
+++ b/solution.py
@@ -39,21 +39,79 @@
     return lax.all_to_all(frame_variances, "freq", split_axis=1, concat_axis=2, tiled=True)
 
 
-def sweep_kernel(frames, spec_ref, var_ref, mr_ref, mi_ref, yr, yi, w, pr, pi, pp):
+def sweep_kernel(frames, spec_hbm, var_hbm, mr_ref, mi_ref, spec_in, var_in, yr, yi, w, pr, pi, pp, sems):
     count, bins, length = yr.shape
+    peers, _, _, span = spec_in.shape
     chunk = 512
     chunks = length // chunk
-
-    def init(j, carry):
-        yr[j] = spec_ref[0, j].astype(jnp.float32)
-        yi[j] = spec_ref[1, j].astype(jnp.float32)
-        w[j] = 1.0 / var_ref[j].astype(jnp.float32)
+    me = lax.axis_index("frame")
+    fq = lax.axis_index("freq")
+    mesh_id = pl.DeviceIdType.MESH
+
+    barrier = pltpu.get_barrier_semaphore()
+    for d in range(1, peers):
+        peer = lax.rem(me + d, peers)
+        pl.semaphore_signal(barrier, inc=1, device_id=(fq, peer), device_id_type=mesh_id)
+    pl.semaphore_wait(barrier, peers - 1)
+
+    def exchange(src, dst, d, kind):
+        peer = lax.rem(me + d, peers)
+        return pltpu.make_async_remote_copy(
+            src_ref=src.at[peer], dst_ref=dst.at[me], send_sem=sems.at[kind, 0, d],
+            recv_sem=sems.at[kind, 1, d], device_id=(fq, peer), device_id_type=mesh_id,
+        )
+
+    def incoming(src, dst, d, kind):
+        source = lax.rem(me + peers - d, peers)
+        return pltpu.make_async_remote_copy(
+            src_ref=src.at[source], dst_ref=dst.at[source], send_sem=sems.at[kind, 0, d],
+            recv_sem=sems.at[kind, 1, d], device_id=(fq, source), device_id_type=mesh_id,
+        )
+
+    local_spec = pltpu.make_async_copy(spec_hbm.at[me], spec_in.at[me], sems.at[0, 0, 0])
+    local_var = pltpu.make_async_copy(var_hbm.at[me], var_in.at[me], sems.at[1, 0, 0])
+    local_spec.start()
+    local_var.start()
+    sends = []
+    for d in range(1, peers):
+        for kind, (src, dst) in enumerate(((spec_hbm, spec_in), (var_hbm, var_in))):
+            copy = exchange(src, dst, d, kind)
+            copy.start()
+            sends.append(copy)
+    for copy in sends:
+        copy.wait_send()
+    for d in range(1, peers):
+        incoming(spec_hbm, spec_in, d, 0).wait_recv()
+        incoming(var_hbm, var_in, d, 1).wait_recv()
+    local_spec.wait()
+    local_var.wait()
+
+    def init(s, carry):
+        cols = pl.ds(pl.multiple_of(s * span, span), span)
+
+        def per_pair(p, carry):
+            block = var_in[s, p].astype(jnp.float32)
+            w[2 * p, :, cols] = 1.0 / block[:bins]
+            w[2 * p + 1, :, cols] = 1.0 / block[bins:]
+            for half in range(2):
+                j = 2 * p + half
+                spec = spec_in[s, j].astype(jnp.float32)
+                yr[j, :, cols] = spec[:bins]
+                yi[j, :, cols] = spec[bins:]
+            return carry
+
+        lax.fori_loop(0, count // 2, per_pair, 0)
+        return carry
+
+    lax.fori_loop(0, peers, init, 0)
+
+    def init_mix(j, carry):
         lane = lax.broadcasted_iota(jnp.int32, (bins, mr_ref.shape[2]), 1)
         mr_ref[j] = jnp.where(lane == j, 1.0, 0.0).astype(jnp.float32)
         mi_ref[j] = jnp.zeros((bins, mr_ref.shape[2]), jnp.float32)
         return carry
 
-    lax.fori_loop(0, count, init, 0)
+    lax.fori_loop(0, count, init_mix, 0)
 
     def step(k, carry):
         pr[...] = yr[k]
@@ -98,28 +156,40 @@
     lax.fori_loop(0, count, step, 0)
 
 
-def sweep(spec_sw, var_sw, frames):
-    _, count, bins, length = spec_sw.shape
+def sweep(spectra, variances, frames):
+    _, count, freq, span = spectra.shape
+    peers = frames // span
+    bins = freq // peers
+    spec_send = spectra.reshape(2, count, peers, bins, span).transpose(2, 1, 0, 3, 4)
+    spec_send = spec_send.reshape(peers, count, 2 * bins, span)
+    var_send = variances.reshape(count // 2, 2, peers, bins, span).transpose(2, 0, 1, 3, 4)
+    var_send = var_send.reshape(peers, count // 2, 2 * bins, span)
     lanes = 128
     vmem = pl.BlockSpec(memory_space=pltpu.VMEM)
+    anywhere = pl.BlockSpec(memory_space=pl.ANY)
     return pl.pallas_call(
         functools.partial(sweep_kernel, frames),
         out_shape=(
             jax.ShapeDtypeStruct((count, bins, lanes), jnp.float32),
             jax.ShapeDtypeStruct((count, bins, lanes), jnp.float32),
         ),
-        in_specs=[vmem, vmem],
+        in_specs=[anywhere, anywhere],
         out_specs=(vmem, vmem),
         scratch_shapes=[
-            pltpu.VMEM((count, bins, length), jnp.float32),
-            pltpu.VMEM((count, bins, length), jnp.float32),
-            pltpu.VMEM((count, bins, length), jnp.float32),
-            pltpu.VMEM((bins, length), jnp.float32),
-            pltpu.VMEM((bins, length), jnp.float32),
-            pltpu.VMEM((bins, length), jnp.float32),
+            pltpu.VMEM((peers, count, 2 * bins, span), spectra.dtype),
+            pltpu.VMEM((peers, count // 2, 2 * bins, span), variances.dtype),
+            pltpu.VMEM((count, bins, frames), jnp.float32),
+            pltpu.VMEM((count, bins, frames), jnp.float32),
+            pltpu.VMEM((count, bins, frames), jnp.float32),
+            pltpu.VMEM((bins, frames), jnp.float32),
+            pltpu.VMEM((bins, frames), jnp.float32),
+            pltpu.VMEM((bins, frames), jnp.float32),
+            pltpu.SemaphoreType.DMA((2, 2, peers)),
         ],
-        compiler_params=pltpu.CompilerParams(vmem_limit_bytes=60 * 1024 * 1024),
-    )(spec_sw, var_sw)
+        compiler_params=pltpu.CompilerParams(
+            collective_id=1, has_side_effects=True, vmem_limit_bytes=60 * 1024 * 1024
+        ),
+    )(spec_send, var_send)
 
 
 def gather_kernel(x_ref, o_ref, send_sem, recv_sem, local_sem):
@@ -174,9 +244,7 @@
     frames = spectra.shape[3] * lax.axis_size("frame")
     variances = source_model(spectra, norm_gain, w_in, b_in, w_mid, b_mid, w_out, b_out)
 
-    spec_sw = lax.all_to_all(spectra, "frame", split_axis=2, concat_axis=3, tiled=True)
-    var_sw = lax.all_to_all(variances, "frame", split_axis=1, concat_axis=2, tiled=True)
-    mix_real, mix_imag = sweep(spec_sw, var_sw, frames)
+    mix_real, mix_imag = sweep(spectra, variances, frames)
     mix = jnp.stack([mix_real[:, :, :count], mix_imag[:, :, :count]])
     peers = lax.axis_size("frame")
     bins = mix.shape[2]

time: 338 us -> 360 us (1.065)
  Pallas kernels: 117 us -> 198 us
  waiting for transfers between devices: 62.2 us -> 17.4 us
  starting transfers between devices: 17.2 us -> 3.76 us
    pallas_call x1, Pallas kernels: 105 us -> 185 us  [sweep(): pl.pallas_call(functools.partial(sweep_kernel, frames), out_shape=(jax.Sh...]
    all_to_all x2 -> x0, waiting for transfers between devices: 44.3 us -> none  [the longest x1 29 us: on_device(): lax.all_to_all(spectra, 'frame', split_axis=2, concat_axis=3, tiled=True)]
    reshape x0 -> x3, local copies, waits for them, and re-layouts: none -> 12.7 us  [the longest x1 7.51 us: sweep(): variances.reshape(count // 2, 2, peers, bins, span).transpose(2, 0, 1, 3, 4)]
    all_to_all x2 -> x0, starting transfers between devices: 12.5 us -> none  [the longest x1 8.09 us: on_device(): lax.all_to_all(spectra, 'frame', split_axis=2, concat_axis=3, tiled=True)]
    all_to_all x2 -> x0, local copies, waits for them, and re-layouts: 7.58 us -> none  [the longest x1 4.65 us: on_device(): lax.all_to_all(spectra, 'frame', split_axis=2, concat_axis=3, tiled=True)]
    all_to_all x2, local copies, waits for them, and re-layouts: 10.1 us -> 16.8 us  [source_model(): lax.all_to_all(frame_variances, 'freq', split_axis=1, concat_axis=2, tile...]
    unnamed x21 -> x18, local copies, waits for them, and re-layouts: 35.3 us -> 29.3 us
  transfers between devices with their start and end apart: 3 -> 1, of which waited for: 3 -> 1; matrix products, arithmetic and copies ran while one was open for 9% -> 1% of each run, Pallas kernels for 0% -> 0%
where the time goes in v5:
time: 360 us; the launch traced here: 358 us
  Pallas kernels  198 us (55%)
  local copies, waits for them, and re-layouts  85 us (24%)
  blocking collectives  26 us (7%)
  matrix products  20.9 us (6%)
  waiting for transfers between devices  17.4 us (5%)
  other arithmetic  6.05 us (2%)
  starting transfers between devices  3.76 us (1%)
    pallas_call x1, Pallas kernels, sweep(): pl.pallas_call(functools.partial(sweep_kernel, frames), out_shape=(jax.Sh...  185 us
    unnamed x18, local copies, waits for them, and re-layouts  29.3 us
    all_to_all x1, blocking collectives, source_model(): lax.all_to_all(logpower, 'freq', split_axis=2, concat_axis=1, tiled=True)  26 us
    all_to_all x1, waiting for transfers between devices, source_model(): lax.all_to_all(frame_variances, 'freq', split_axis=1, concat_axis=2, tile...  17.4 us
    all_to_all x2, local copies, waits for them, and re-layouts, source_model(): lax.all_to_all(frame_variances, 'freq', split_axis=1, concat_axis=2, tile...  16.8 us
    pallas_call x1, Pallas kernels, frame_gather(): pl.pallas_call(gather_kernel, out_shape=jax.ShapeDtypeStruct((n,) + x.sha...  13.2 us
    dot_general x1, matrix products, source_model(): jnp.einsum('nth,hg->ntg', hidden_one, w_mid, preferred_element_type=jnp.f...  7.69 us
    reshape x1, local copies, waits for them, and re-layouts, sweep(): variances.reshape(count // 2, 2, peers, bins, span).transpose(2, 0, 1, 3, 4)  7.51 us
  transfers between devices with their start and end apart: 1, of which 1 were waited for; matrix products, arithmetic and copies ran while one was open for 1% of the time, Pallas kernels for 0%

profile of v5, /device:TPU:0, one launch (start us, length us, event | category | flops | bytes accessed | tf_op | source)
XLA Modules:
  0.0 358.0 jit_solution(591551771874339361)
XLA Ops:
  0.6 4.0 %fusion.41 = (bf16[1,24,128,256]{3,2,1,0:T(8,128)(2,1)}, bf16[1,24,128,256]{3,2,1,0:T(8,128)(2,1)}) fusion(bf16[2,24,128,256]{3,2,1,0:T(8,128)(2,1)} %param.8), kind=kLoop, calls=%fused_computation.50 | loop fusion | bytes 6291456 | tf_op jit(solution)/shard_map/slice | solution.py:16
  4.7 2.8 copy.76
  7.5 2.7 copy.77
  10.2 2.8 fusion.21
  13.0 26.0 %all_to_all.27 = bf16[24,128,256]{1,0,2:T(8,128)(2,1)S(1)} all-to-all(bf16[24,128,256]{1,0,2:T(8,128)(2,1)S(1)} %fusion.21), channel_id=1, replica_groups=mesh['freq'=8,'frame'=16] {'freq'}, dimensions={2} | all-to-all | bytes 3145728 | tf_op jit(solution)/shard_map/all_to_all | solution.py:21
  39.0 2.2 fusion.42
  41.5 0.6 fusion.3
  42.1 7.7 %fusion.17 = f32[24,32,1024]{2,1,0:T(8,128)} fusion(bf16[1024,1024]{1,0:T(8,128)(2,1)S(1)} %copy-done, f32[1024]{0:T(1024)S(1)} %copy-done.2, bf16[1024,1024]{1,0:T(8,128)(2,1)} %param.10, f32[24,8,4,8,128]{4,3,2,1,0:T(8,128)} %get-tuple-element.21, f32[1024]{0:T(1024)S(1)} %copy-done.3, f32[24,32]{1,0:T(8,128)S(1)} %add_rsqrt_fusion, ...), kind=kOutput, calls=%fused_computation.28 | convolution fusion | flops 3229089792 | bytes 10500096 | tf_op jit(solution)/shard_map/nth,hg->ntg/dot_general | solution.py:32
  49.8 5.9 %fusion.5 = bf16[24,1024,32]{1,2,0:T(8,128)(2,1)S(1)} fusion(f32[1024]{0:T(1024)S(1)} %copy-done.4, bf16[1024,1024]{1,0:T(8,128)(2,1)} %param.14, f32[24,32,1024]{2,1,0:T(8,128)} %fusion.17, f32[1024]{0:T(1024)S(1)} %copy-done.5), kind=kOutput, calls=%fused_computation.8 | convolution fusion | flops 1622409216 | bytes 6823936 | tf_op jit(solution)/shard_map/nth,hf->nft/dot_general | solution.py:35
  55.7 5.9 %copy.59 = bf16[24,1024,32]{2,0,1:T(8,128)(2,1)} copy(bf16[24,1024,32]{1,2,0:T(8,128)(2,1)S(1)} %fusion.5) | data formatting | bytes 3145728 | tf_op jit(solution)/shard_map/convert_element_type | solution.py:38
  61.5 9.5 %reshape.79 = bf16[8,2,49152]{2,1,0:T(2,128)(2,1)} reshape(bf16[1024,24,32]{2,1,0:T(8,128)(2,1)} %bitcast.107) | data formatting | bytes 3145728
  71.0 3.8 %all-to-all-start.1 = ((bf16[8,2,49152]{2,1,0:T(2,128)(2,1)}), bf16[8,2,49152]{2,1,0:T(2,128)(2,1)S(1)}, u32[]{:S(2)}, u32[]{:S(2)}) async-start(bf16[8,2,49152]{2,1,0:T(2,128)(2,1)} %reshape.79), calls=%async_computation.1 | async-start | bytes 3145728 | tf_op jit(solution)/shard_map/all_to_all | solution.py:39
  74.8 3.9 %copy_bitcast_fusion.1.spec_hbm = bf16[16,24,16,256]{3,2,1,0:T(8,128)(2,1)} fusion(bf16[2,24,128,256]{3,2,1,0:T(8,128)(2,1)} %param.8), kind=kLoop, calls=%fused_computation.22 | loop fusion | bytes 6291456 | tf_op jit(solution)/shard_map/reshape | solution.py:164
  78.7 17.4 %all-to-all-done.1 = bf16[8,2,49152]{2,1,0:T(2,128)(2,1)S(1)} async-done(((bf16[8,2,49152]{2,1,0:T(2,128)(2,1)}), bf16[8,2,49152]{2,1,0:T(2,128)(2,1)S(1)}, u32[]{:S(2)}, u32[]{:S(2)}) %all-to-all-start.1) | async-done | bytes 1572896 | tf_op jit(solution)/shard_map/all_to_all | solution.py:39
  96.1 5.3 %reshape.80 = bf16[1024,24,32]{2,1,0:T(8,128)(2,1)} reshape(bf16[8,2,49152]{2,1,0:T(2,128)(2,1)S(1)} %all-to-all-done.1) | data formatting | bytes 3145728
  101.5 7.3 %copy.70 = bf16[24,128,8,32]{1,3,2,0:T(8,128)(2,1)} copy(bf16[24,128,8,32]{3,0,1,2:T(8,128)(2,1)} %bitcast.103) | data formatting | bytes 3145728 | tf_op jit(solution)/shard_map/all_to_all | solution.py:39
  108.8 9.5 %copy.61 = bf16[24,128,8,32]{3,2,1,0:T(8,128)(2,1)} copy(bf16[24,128,8,32]{3,0,1,2:T(8,128)(2,1)} %bitcast.104) | data formatting | bytes 3145728 | tf_op jit(solution)/shard_map/all_to_all | solution.py:39
  118.3 7.5 %reshape.65 = bf16[12,2,16,8,256]{4,3,2,1,0:T(8,128)(2,1)S(1)} reshape(bf16[24,128,8,32]{3,2,1,0:T(8,128)(2,1)} %copy.61) | data formatting | bytes 3145728 | tf_op jit(solution)/shard_map/reshape | solution.py:165
  125.8 1.3 copy_bitcast_fusion.2.var_hbm
  127.1 184.8 %shard_map.95 = (f32[24,8,128]{2,1,0:T(8,128)}, f32[24,8,128]{2,1,0:T(8,128)}) custom-call(bf16[16,24,16,256]{3,2,1,0:T(8,128)(2,1)} %copy_bitcast_fusion.1.spec_hbm, bf16[16,12,16,256]{3,2,1,0:T(8,128)(2,1)} %copy_bitcast_fusion.2.var_hbm), custom_call_target="tpu_custom_call" | custom-call | tf_op jit(solution)/shard_map/pallas_call | solution.py:170
  311.9 1.0 slice_bitcast_fusion.2
  312.9 0.8 reshape.67.x_ref
  313.6 13.2 %shard_map.96 = f32[16,72,128]{2,1,0:T(8,128)} custom-call(f32[72,128]{1,0:T(8,128)} %reshape.67.x_ref), custom_call_target="tpu_custom_call" | custom-call | tf_op jit(solution)/shard_map/pallas_call | solution.py:228
  326.9 4.1 %reshape.68 = f32[16,2,24,8,24]{4,3,2,1,0:T(8,128)} reshape(f32[16,72,128]{2,1,0:T(8,128)} %shard_map.96) | data formatting | bytes 1179648 | tf_op jit(solution)/shard_map/reshape | solution.py:252
  331.0 2.3 copy.92
  333.4 1.9 slice_bitcast_fusion
  335.2 2.6 copy.72
  338.3 1.9 copy.66
  340.1 1.9 copy.64
  342.0 2.2 copy.68
  344.3 7.3 %fusion.13 = f32[128,48,256]{2,1,0:T(8,128)S(1)} fusion(f32[48,128,48]{2,0,1:T(8,128)} %copy.68, bf16[48,128,256]{2,1,0:T(8,128)(2,1)} %bitcast.105), kind=kOutput, calls=%fused_computation.19 | convolution fusion | flops 905969664 | bytes 10616832 | tf_op jit(solution)/shard_map/jfa,aft->jft/dot_general | solution.py:259
  351.6 6.3 %copy.71 = f32[2,24,128,256]{3,2,1,0:T(8,128)} copy(f32[2,24,128,256]{3,1,0,2:T(8,128)S(1)} %bitcast.106) | data formatting | bytes 12582912
  (19 shorter events, 1.0 us)
Async XLA Ops:
  0.6 41.4 %copy-start = (bf16[1024,1024]{1,0:T(8,128)(2,1)S(1)}, bf16[1024,1024]{1,0:T(8,128)(2,1)}, u32[]{:S(2)}) copy-start(bf16[1024,1024]{1,0:T(8,128)(2,1)} %param.12) | copy-start | bytes 6291460
  41.2 0.9 copy-start.2
  41.2 0.9 copy-start.3
  42.1 7.7 %copy-start.4 = (f32[1024]{0:T(1024)S(1)}, f32[1024]{0:T(1024)}, u32[]{:S(2)}) copy-start(f32[1024]{0:T(1024)} %param.15) | copy-start | bytes 12292
  42.1 7.7 %copy-start.5 = (f32[1024]{0:T(1024)S(1)}, f32[1024]{0:T(1024)}, u32[]{:S(2)}) copy-start(f32[1024]{0:T(1024)} %param.13) | copy-start | bytes 12292
  71.0 25.1 %all-to-all-start.1 = ((bf16[8,2,49152]{2,1,0:T(2,128)(2,1)}), bf16[8,2,49152]{2,1,0:T(2,128)(2,1)S(1)}, u32[]{:S(2)}, u32[]{:S(2)}) async-start(bf16[8,2,49152]{2,1,0:T(2,128)(2,1)} %reshape.79), calls=%async_computation.1 | async-start | bytes 3145728 | tf_op jit(solution)/shard_map/all_to_all | solution.py:39
  351.6 6.4 %copy-start.1 = (bf16[1024,1024]{1,0:T(8,128)(2,1)S(1)}, bf16[1024,1024]{1,0:T(8,128)(2,1)}, u32[]{:S(2)}) copy-start(bf16[1024,1024]{1,0:T(8,128)(2,1)} %param.12) | copy-start | bytes 6291460

commit v6 on v4

--- a/solution.py
+++ b/solution.py
@@ -39,14 +39,24 @@
     return lax.all_to_all(frame_variances, "freq", split_axis=1, concat_axis=2, tiled=True)
 
 
-def sweep_kernel(frames, spec_ref, var_ref, mr_ref, mi_ref, yr, yi, w, pr, pi, pp):
+def sweep_kernel(frames, *refs):
+    peers = len(refs) - 9
+    pieces = refs[:peers]
+    var_ref, mr_ref, mi_ref, yr, yi, w, pr, pi, pp = refs[peers:]
     count, bins, length = yr.shape
     chunk = 512
     chunks = length // chunk
 
+    me = lax.axis_index("frame")
+    span = pieces[0].shape[2]
+
     def init(j, carry):
-        yr[j] = spec_ref[0, j].astype(jnp.float32)
-        yi[j] = spec_ref[1, j].astype(jnp.float32)
+        for d in range(peers):
+            source = lax.rem(me + peers - d, peers)
+            cols = pl.ds(pl.multiple_of(source * span, span), span)
+            spec = pieces[d][j].astype(jnp.float32)
+            yr[j, :, cols] = spec[:bins]
+            yi[j, :, cols] = spec[bins:]
         w[j] = 1.0 / var_ref[j].astype(jnp.float32)
         lane = lax.broadcasted_iota(jnp.int32, (bins, mr_ref.shape[2]), 1)
         mr_ref[j] = jnp.where(lane == j, 1.0, 0.0).astype(jnp.float32)
@@ -98,8 +108,8 @@
     lax.fori_loop(0, count, step, 0)
 
 
-def sweep(spec_sw, var_sw, frames):
-    _, count, bins, length = spec_sw.shape
+def sweep(pieces, var_sw, frames):
+    count, bins, length = var_sw.shape
     lanes = 128
     vmem = pl.BlockSpec(memory_space=pltpu.VMEM)
     return pl.pallas_call(
@@ -108,7 +118,7 @@
             jax.ShapeDtypeStruct((count, bins, lanes), jnp.float32),
             jax.ShapeDtypeStruct((count, bins, lanes), jnp.float32),
         ),
-        in_specs=[vmem, vmem],
+        in_specs=[vmem] * (len(pieces) + 1),
         out_specs=(vmem, vmem),
         scratch_shapes=[
             pltpu.VMEM((count, bins, length), jnp.float32),
@@ -119,7 +129,7 @@
             pltpu.VMEM((bins, length), jnp.float32),
         ],
         compiler_params=pltpu.CompilerParams(vmem_limit_bytes=60 * 1024 * 1024),
-    )(spec_sw, var_sw)
+    )(*pieces, var_sw)
 
 
 def gather_kernel(x_ref, o_ref, send_sem, recv_sem, local_sem):
@@ -172,11 +182,21 @@
 def on_device(spectra, norm_gain, w_in, b_in, w_mid, b_mid, w_out, b_out):
     count = spectra.shape[1]
     frames = spectra.shape[3] * lax.axis_size("frame")
+    peers = lax.axis_size("frame")
+    me = lax.axis_index("frame")
+    span = spectra.shape[3]
+    bins = spectra.shape[2] // peers
+    send = spectra.reshape(2, count, peers, bins, span).transpose(2, 1, 0, 3, 4)
+    send = send.reshape(peers, count, 2 * bins, span)
+    pieces = []
+    for d in range(peers):
+        piece = lax.dynamic_index_in_dim(send, lax.rem(me + d, peers), 0, keepdims=False)
+        if d:
+            piece = lax.ppermute(piece, "frame", [(i, (i + d) % peers) for i in range(peers)])
+        pieces.append(piece)
     variances = source_model(spectra, norm_gain, w_in, b_in, w_mid, b_mid, w_out, b_out)
-
-    spec_sw = lax.all_to_all(spectra, "frame", split_axis=2, concat_axis=3, tiled=True)
     var_sw = lax.all_to_all(variances, "frame", split_axis=1, concat_axis=2, tiled=True)
-    mix_real, mix_imag = sweep(spec_sw, var_sw, frames)
+    mix_real, mix_imag = sweep(pieces, var_sw, frames)
     mix = jnp.stack([mix_real[:, :, :count], mix_imag[:, :, :count]])
     peers = lax.axis_size("frame")
     bins = mix.shape[2]

time: 338 us -> 356 us (1.053)
  starting transfers between devices: 17.2 us -> 50.3 us
  waiting for transfers between devices: 62.2 us -> 31.2 us
  blocking collectives: 26 us -> 50.2 us
  local copies, waits for them, and re-layouts: 83.1 us -> 73.7 us
    all_to_all x2 -> x0, waiting for transfers between devices: 47 us -> none  [the longest x1 29 us: on_device(): lax.all_to_all(spectra, 'frame', split_axis=2, concat_axis=3, tiled=True)]
    ppermute x0 -> x15, starting transfers between devices: none -> 42.2 us  [on_device(): lax.ppermute(piece, 'frame', [(i, (i + d) % peers) for i in range(peers)])]
    ppermute x0 -> x15, waiting for transfers between devices: none -> 31.2 us  [on_device(): lax.ppermute(piece, 'frame', [(i, (i + d) % peers) for i in range(peers)])]
    all_to_all x0 -> x1, blocking collectives: none -> 24.2 us  [source_model(): lax.all_to_all(frame_variances, 'freq', split_axis=1, concat_axis=2, tile...]
    all_to_all x1, waiting for transfers between devices: 15.2 us -> 0.01 us  [on_device(): lax.all_to_all(variances, 'frame', split_axis=1, concat_axis=2, tiled=True)]
    all_to_all x2 -> x0, starting transfers between devices: 12.8 us -> none  [the longest x1 8.09 us: on_device(): lax.all_to_all(spectra, 'frame', split_axis=2, concat_axis=3, tiled=True)]
    unnamed x21 -> x40, local copies, waits for them, and re-layouts: 35.3 us -> 29.1 us
    all_to_all x1 -> x0, local copies, waits for them, and re-layouts: 4.65 us -> none  [on_device(): lax.all_to_all(spectra, 'frame', split_axis=2, concat_axis=3, tiled=True)]
  transfers between devices with their start and end apart: 3 -> 16, of which waited for: 3 -> 5; matrix products, arithmetic and copies ran while one was open for 9% -> 2% of each run, Pallas kernels for 0% -> 0%
where the time goes in v6:
time: 356 us; the launch traced here: 355 us
  Pallas kernels  119 us (33%)
  local copies, waits for them, and re-layouts  73.7 us (21%)
  starting transfers between devices  50.3 us (14%)
  blocking collectives  50.2 us (14%)
  waiting for transfers between devices  31.2 us (9%)
  matrix products  20 us (6%)
  other arithmetic  9.38 us (3%)
    pallas_call x1, Pallas kernels, sweep(): pl.pallas_call(functools.partial(sweep_kernel, frames), out_shape=(jax.Sh...  106 us
    ppermute x15, starting transfers between devices, on_device(): lax.ppermute(piece, 'frame', [(i, (i + d) % peers) for i in range(peers)])  42.2 us
    ppermute x15, waiting for transfers between devices, on_device(): lax.ppermute(piece, 'frame', [(i, (i + d) % peers) for i in range(peers)])  31.2 us
    unnamed x40, local copies, waits for them, and re-layouts  29.1 us
    all_to_all x1, blocking collectives, source_model(): lax.all_to_all(logpower, 'freq', split_axis=2, concat_axis=1, tiled=True)  26 us
    all_to_all x1, blocking collectives, source_model(): lax.all_to_all(frame_variances, 'freq', split_axis=1, concat_axis=2, tile...  24.2 us
    pallas_call x1, Pallas kernels, frame_gather(): pl.pallas_call(gather_kernel, out_shape=jax.ShapeDtypeStruct((n,) + x.sha...  12.2 us
    all_to_all x2, local copies, waits for them, and re-layouts, source_model(): lax.all_to_all(frame_variances, 'freq', split_axis=1, concat_axis=2, tile...  10.2 us
  transfers between devices with their start and end apart: 16, of which 5 were waited for; matrix products, arithmetic and copies ran while one was open for 2% of the time, Pallas kernels for 0%

profile of v6, /device:TPU:0, one launch (start us, length us, event | category | flops | bytes accessed | tf_op | source)
XLA Modules:
  0.0 354.6 jit_solution(17073457532379123342)
XLA Ops:
  0.6 4.0 %fusion.41 = (bf16[1,24,128,256]{3,2,1,0:T(8,128)(2,1)}, bf16[1,24,128,256]{3,2,1,0:T(8,128)(2,1)}) fusion(bf16[2,24,128,256]{3,2,1,0:T(8,128)(2,1)} %param.8), kind=kLoop, calls=%fused_computation.65 | loop fusion | bytes 6291456 | tf_op jit(solution)/shard_map/slice | solution.py:16
  4.7 2.8 copy.73
  7.5 2.7 copy.74
  10.2 2.8 fusion.21
  13.0 26.0 %all_to_all.45 = bf16[24,128,256]{1,0,2:T(8,128)(2,1)S(1)} all-to-all(bf16[24,128,256]{1,0,2:T(8,128)(2,1)S(1)} %fusion.21), channel_id=1, replica_groups=mesh['freq'=8,'frame'=16] {'freq'}, dimensions={2} | all-to-all | bytes 3145728 | tf_op jit(solution)/shard_map/all_to_all | solution.py:21
  42.1 7.7 %fusion.17 = f32[24,32,1024]{2,1,0:T(8,128)} fusion(bf16[1024,1024]{1,0:T(8,128)(2,1)S(1)} %copy-done, f32[1024]{0:T(1024)S(1)} %copy-done.13, bf16[1024,1024]{1,0:T(8,128)(2,1)} %param.10, f32[24,8,4,8,128]{4,3,2,1,0:T(8,128)} %get-tuple-element.37, f32[1024]{0:T(1024)S(1)} %copy-done.14, f32[24,32]{1,0:T(8,128)S(1)} %add_rsqrt_fusion, ...), kind=kOutput, calls=%fused_computation.28 | convolution fusion | flops 3229089792 | bytes 10500096 | tf_op jit(solution)/shard_map/nth,hg->ntg/dot_general | solution.py:32
  49.8 5.9 %fusion.5 = bf16[24,1024,32]{1,2,0:T(8,128)(2,1)S(1)} fusion(f32[1024]{0:T(1024)S(1)} %copy-done.15, bf16[1024,1024]{1,0:T(8,128)(2,1)} %param.14, f32[24,32,1024]{2,1,0:T(8,128)} %fusion.17, f32[1024]{0:T(1024)S(1)} %copy-done.16), kind=kOutput, calls=%fused_computation.8 | convolution fusion | flops 1622409216 | bytes 6823936 | tf_op jit(solution)/shard_map/nth,hf->nft/dot_general | solution.py:35
  55.7 5.9 %copy.57 = bf16[24,1024,32]{2,0,1:T(8,128)(2,1)} copy(bf16[24,1024,32]{1,2,0:T(8,128)(2,1)S(1)} %fusion.5) | data formatting | bytes 3145728 | tf_op jit(solution)/shard_map/convert_element_type | solution.py:38
  61.5 8.6 %reshape.70 = bf16[8,2,49152]{2,1,0:T(2,128)(2,1)S(1)} reshape(bf16[1024,24,32]{2,1,0:T(8,128)(2,1)} %bitcast.134) | data formatting | bytes 3145728
  70.2 24.2 %all_to_all.46 = bf16[8,2,49152]{2,1,0:T(2,128)(2,1)S(1)} all-to-all(bf16[8,2,49152]{2,1,0:T(2,128)(2,1)S(1)} %reshape.70), channel_id=1, replica_groups=mesh['freq'=8,'frame'=16] {'freq'}, dimensions={0} | all-to-all | bytes 3145728 | tf_op jit(solution)/shard_map/all_to_all | solution.py:39
  94.4 5.3 %reshape.71 = bf16[1024,24,32]{2,1,0:T(8,128)(2,1)} reshape(bf16[8,2,49152]{2,1,0:T(2,128)(2,1)S(1)} %all_to_all.46) | data formatting | bytes 3145728
  99.7 7.3 %copy.59 = bf16[24,128,8,32]{1,3,2,0:T(8,128)(2,1)} copy(bf16[24,128,8,32]{3,0,1,2:T(8,128)(2,1)} %bitcast.135) | data formatting | bytes 3145728 | tf_op jit(solution)/shard_map/all_to_all | solution.py:39
  107.0 2.9 copy.60
  109.9 8.1 %all-to-all-start.2 = ((bf16[24,128,256]{2,0,1:T(8,128)(2,1)}), bf16[24,128,256]{2,0,1:T(8,128)(2,1)}, u32[]{:S(2)}, u32[]{:S(2)}) async-start(bf16[24,128,256]{2,0,1:T(8,128)(2,1)} %copy.60), calls=%async_computation.2 | async-start | bytes 3145728 | tf_op jit(solution)/shard_map/all_to_all | solution.py:198
  119.6 5.1 %collective-permute-start.14 = (bf16[24,16,256]{2,1,0:T(8,128)(2,1)S(1)}, bf16[24,16,256]{2,1,0:T(8,128)(2,1)S(1)}, u32[]{:S(2)}, u32[]{:S(2)}) collective-permute-start(bf16[24,16,256]{2,1,0:T(8,128)(2,1)S(1)} %get-tuple-element.20), channel_id=1, source_target_pairs={{0,15},{1,0},{2,1},{3,2},{4,3},{5,4},{6,5},{7,6},{8,7},{9,8},{10,9... | collective-permute-start | bytes 589832 | tf_op jit(solution)/shard_map/ppermute | solution.py:195
  129.6 19.3 %collective-permute-done.14.refs_15_ = bf16[24,16,256]{2,1,0:T(8,128)(2,1)S(1)} collective-permute-done((bf16[24,16,256]{2,1,0:T(8,128)(2,1)S(1)}, bf16[24,16,256]{2,1,0:T(8,128)(2,1)S(1)}, u32[]{:S(2)}, u32[]{:S(2)}) %collective-permute-start.14) | collective-permute-done | bytes 196640 | tf_op jit(solution)/shard_map/ppermute | solution.py:195
  149.0 12.2 %collective-permute-start.8 = (bf16[24,16,256]{2,1,0:T(8,128)(2,1)S(1)}, bf16[24,16,256]{2,1,0:T(8,128)(2,1)S(1)}, u32[]{:S(2)}, u32[]{:S(2)}) collective-permute-start(bf16[24,16,256]{2,1,0:T(8,128)(2,1)S(1)} %get-tuple-element.26), channel_id=1, source_target_pairs={{0,9},{1,10},{2,11},{3,12},{4,13},{5,14},{6,15},{7,0},{8,1},{9,2},... | collective-permute-start | bytes 589832 | tf_op jit(solution)/shard_map/ppermute | solution.py:195
  161.2 9.1 %collective-permute-start.6 = (bf16[24,16,256]{2,1,0:T(8,128)(2,1)S(1)}, bf16[24,16,256]{2,1,0:T(8,128)(2,1)S(1)}, u32[]{:S(2)}, u32[]{:S(2)}) collective-permute-start(bf16[24,16,256]{2,1,0:T(8,128)(2,1)S(1)} %get-tuple-element.28), channel_id=1, source_target_pairs={{0,7},{1,8},{2,9},{3,10},{4,11},{5,12},{6,13},{7,14},{8,15},{9,0},... | collective-permute-start | bytes 589832 | tf_op jit(solution)/shard_map/ppermute | solution.py:195
  172.5 3.6 %collective-permute-start.2 = (bf16[24,16,256]{2,1,0:T(8,128)(2,1)}, bf16[24,16,256]{2,1,0:T(8,128)(2,1)}, u32[]{:S(2)}, u32[]{:S(2)}) collective-permute-start(bf16[24,16,256]{2,1,0:T(8,128)(2,1)} %get-tuple-element.32), channel_id=1, source_target_pairs={{0,3},{1,4},{2,5},{3,6},{4,7},{5,8},{6,9},{7,10},{8,11},{9,12},{10... | collective-permute-start | bytes 589832 | tf_op jit(solution)/shard_map/ppermute | solution.py:195
  176.2 4.5 %collective-permute-done.6.refs_7_ = bf16[24,16,256]{2,1,0:T(8,128)(2,1)S(1)} collective-permute-done((bf16[24,16,256]{2,1,0:T(8,128)(2,1)S(1)}, bf16[24,16,256]{2,1,0:T(8,128)(2,1)S(1)}, u32[]{:S(2)}, u32[]{:S(2)}) %collective-permute-start.6) | collective-permute-done | bytes 196640 | tf_op jit(solution)/shard_map/ppermute | solution.py:195
  180.7 2.8 collective-permute-start.1
  187.2 2.6 copy.70
  189.8 2.9 copy.61
  194.6 4.6 %collective-permute-done.3.refs_4_ = bf16[24,16,256]{2,1,0:T(8,128)(2,1)} collective-permute-done((bf16[24,16,256]{2,1,0:T(8,128)(2,1)}, bf16[24,16,256]{2,1,0:T(8,128)(2,1)}, u32[]{:S(2)}, u32[]{:S(2)}) %collective-permute-start.3) | collective-permute-done | bytes 196640 | tf_op jit(solution)/shard_map/ppermute | solution.py:195
  199.3 106.5 %shard_map.95 = (f32[24,8,128]{2,1,0:T(8,128)}, f32[24,8,128]{2,1,0:T(8,128)}) custom-call(bf16[24,16,256]{2,1,0:T(8,128)(2,1)} %get-tuple-element.35.refs_0_, bf16[24,16,256]{2,1,0:T(8,128)(2,1)} %collective-permute-done.refs_1_, bf16[24,16,256]{2,1,0:T(8,128)(2,1)} %collective-permute-done.1.refs_2_, bf16[24,16,256]{2,1,0:T(8,128)(2,1)} %collective-permute-done.2.refs_3_, ...), custom_call_target="tpu_custom_call" | custom-call | tf_op jit(solution)/shard_map/pallas_call | solution.py:115
  307.5 12.2 %shard_map.96 = f32[16,72,128]{2,1,0:T(8,128)} custom-call(f32[72,128]{1,0:T(8,128)} %reshape.58.x_ref), custom_call_target="tpu_custom_call" | custom-call | tf_op jit(solution)/shard_map/pallas_call | solution.py:168
  319.7 4.1 %reshape.59 = f32[16,2,24,8,24]{4,3,2,1,0:T(8,128)} reshape(f32[16,72,128]{2,1,0:T(8,128)} %shard_map.96) | data formatting | bytes 1179648 | tf_op jit(solution)/shard_map/reshape | solution.py:204
  331.1 2.6 copy.65
  333.7 2.6 copy.63
  338.6 3.2 copy.67
  341.8 6.5 %fusion.13 = f32[128,48,256]{2,1,0:T(8,128)S(1)} fusion(f32[48,128,48]{2,0,1:T(8,128)} %copy.67, bf16[48,128,256]{2,1,0:T(8,128)(2,1)S(1)} %bitcast.132), kind=kOutput, calls=%fused_computation.19 | convolution fusion | flops 905969664 | bytes 10616832 | tf_op jit(solution)/shard_map/jfa,aft->jft/dot_general | solution.py:211
  348.2 6.3 %copy.69 = f32[2,24,128,256]{3,2,1,0:T(8,128)} copy(f32[2,24,128,256]{3,1,0,2:T(8,128)S(1)} %bitcast.133) | data formatting | bytes 12582912
  (72 shorter events, 28.7 us)
Async XLA Ops:
  0.6 41.4 %copy-start = (bf16[1024,1024]{1,0:T(8,128)(2,1)S(1)}, bf16[1024,1024]{1,0:T(8,128)(2,1)}, u32[]{:S(2)}) copy-start(bf16[1024,1024]{1,0:T(8,128)(2,1)} %param.12) | copy-start | bytes 6291460
  41.2 0.9 copy-start.13
  41.2 0.9 copy-start.14
  42.1 7.7 %copy-start.15 = (f32[1024]{0:T(1024)S(1)}, f32[1024]{0:T(1024)}, u32[]{:S(2)}) copy-start(f32[1024]{0:T(1024)} %param.15) | copy-start | bytes 12292
  42.1 7.7 %copy-start.16 = (f32[1024]{0:T(1024)S(1)}, f32[1024]{0:T(1024)}, u32[]{:S(2)}) copy-start(f32[1024]{0:T(1024)} %param.13) | copy-start | bytes 12292
  107.0 11.1 %copy-start.2 = (bf16[2,24,128,256]{3,2,1,0:T(8,128)(2,1)S(1)}, bf16[2,24,128,256]{3,2,1,0:T(8,128)(2,1)}, u32[]{:S(2)}) copy-start(bf16[2,24,128,256]{3,2,1,0:T(8,128)(2,1)} %param.8) | copy-start | bytes 9437188
  109.9 79.9 %all-to-all-start.2 = ((bf16[24,128,256]{2,0,1:T(8,128)(2,1)}), bf16[24,128,256]{2,0,1:T(8,128)(2,1)}, u32[]{:S(2)}, u32[]{:S(2)}) async-start(bf16[24,128,256]{2,0,1:T(8,128)(2,1)} %copy.60), calls=%async_computation.2 | async-start | bytes 3145728 | tf_op jit(solution)/shard_map/all_to_all | solution.py:198
  119.6 29.4 %collective-permute-start.14 = (bf16[24,16,256]{2,1,0:T(8,128)(2,1)S(1)}, bf16[24,16,256]{2,1,0:T(8,128)(2,1)S(1)}, u32[]{:S(2)}, u32[]{:S(2)}) collective-permute-start(bf16[24,16,256]{2,1,0:T(8,128)(2,1)S(1)} %get-tuple-element.20), channel_id=1, source_target_pairs={{0,15},{1,0},{2,1},{3,2},{4,3},{5,4},{6,5},{7,6},{8,7},{9,8},{10,9... | collective-permute-start | bytes 589832 | tf_op jit(solution)/shard_map/ppermute | solution.py:195
  124.7 24.3 %collective-permute-start.13 = (bf16[24,16,256]{2,1,0:T(8,128)(2,1)S(1)}, bf16[24,16,256]{2,1,0:T(8,128)(2,1)S(1)}, u32[]{:S(2)}, u32[]{:S(2)}) collective-permute-start(bf16[24,16,256]{2,1,0:T(8,128)(2,1)S(1)} %get-tuple-element.21), channel_id=1, source_target_pairs={{0,14},{1,15},{2,0},{3,1},{4,2},{5,3},{6,4},{7,5},{8,6},{9,7},{10,... | collective-permute-start | bytes 589832 | tf_op jit(solution)/shard_map/ppermute | solution.py:195
  125.5 35.6 %collective-permute-start.12 = (bf16[24,16,256]{2,1,0:T(8,128)(2,1)S(1)}, bf16[24,16,256]{2,1,0:T(8,128)(2,1)S(1)}, u32[]{:S(2)}, u32[]{:S(2)}) collective-permute-start(bf16[24,16,256]{2,1,0:T(8,128)(2,1)S(1)} %get-tuple-element.22), channel_id=1, source_target_pairs={{0,13},{1,14},{2,15},{3,0},{4,1},{5,2},{6,3},{7,4},{8,5},{9,6},{10... | collective-permute-start | bytes 589832 | tf_op jit(solution)/shard_map/ppermute | solution.py:195
  126.7 34.4 %collective-permute-start.11 = (bf16[24,16,256]{2,1,0:T(8,128)(2,1)S(1)}, bf16[24,16,256]{2,1,0:T(8,128)(2,1)S(1)}, u32[]{:S(2)}, u32[]{:S(2)}) collective-permute-start(bf16[24,16,256]{2,1,0:T(8,128)(2,1)S(1)} %get-tuple-element.23), channel_id=1, source_target_pairs={{0,12},{1,13},{2,14},{3,15},{4,0},{5,1},{6,2},{7,3},{8,4},{9,5},{1... | collective-permute-start | bytes 589832 | tf_op jit(solution)/shard_map/ppermute | solution.py:195
  127.3 43.0 %collective-permute-start.10 = (bf16[24,16,256]{2,1,0:T(8,128)(2,1)S(1)}, bf16[24,16,256]{2,1,0:T(8,128)(2,1)S(1)}, u32[]{:S(2)}, u32[]{:S(2)}) collective-permute-start(bf16[24,16,256]{2,1,0:T(8,128)(2,1)S(1)} %get-tuple-element.24), channel_id=1, source_target_pairs={{0,11},{1,12},{2,13},{3,14},{4,15},{5,0},{6,1},{7,2},{8,3},{9,4},{... | collective-permute-start | bytes 589832 | tf_op jit(solution)/shard_map/ppermute | solution.py:195
  148.9 35.3 %copy-start.3 = (bf16[24,16,256]{2,1,0:T(8,128)(2,1)}, bf16[24,16,256]{2,1,0:T(8,128)(2,1)S(1)}, u32[]{:S(2)}) copy-start(bf16[24,16,256]{2,1,0:T(8,128)(2,1)S(1)} %collective-permute-done.14.refs_15_) | copy-start | bytes 589828
  148.9 21.3 %collective-permute-start.9 = (bf16[24,16,256]{2,1,0:T(8,128)(2,1)S(1)}, bf16[24,16,256]{2,1,0:T(8,128)(2,1)S(1)}, u32[]{:S(2)}, u32[]{:S(2)}) collective-permute-start(bf16[24,16,256]{2,1,0:T(8,128)(2,1)S(1)} %get-tuple-element.25), channel_id=1, source_target_pairs={{0,10},{1,11},{2,12},{3,13},{4,14},{5,15},{6,0},{7,1},{8,2},{9,3},... | collective-permute-start | bytes 589832 | tf_op jit(solution)/shard_map/ppermute | solution.py:195
  149.0 35.3 %copy-start.4 = (bf16[24,16,256]{2,1,0:T(8,128)(2,1)}, bf16[24,16,256]{2,1,0:T(8,128)(2,1)S(1)}, u32[]{:S(2)}) copy-start(bf16[24,16,256]{2,1,0:T(8,128)(2,1)S(1)} %collective-permute-done.13.refs_14_) | copy-start | bytes 589828
  149.0 23.5 %collective-permute-start.8 = (bf16[24,16,256]{2,1,0:T(8,128)(2,1)S(1)}, bf16[24,16,256]{2,1,0:T(8,128)(2,1)S(1)}, u32[]{:S(2)}, u32[]{:S(2)}) collective-permute-start(bf16[24,16,256]{2,1,0:T(8,128)(2,1)S(1)} %get-tuple-element.26), channel_id=1, source_target_pairs={{0,9},{1,10},{2,11},{3,12},{4,13},{5,14},{6,15},{7,0},{8,1},{9,2},... | collective-permute-start | bytes 589832 | tf_op jit(solution)/shard_map/ppermute | solution.py:195
  161.1 23.1 %copy-start.5 = (bf16[24,16,256]{2,1,0:T(8,128)(2,1)}, bf16[24,16,256]{2,1,0:T(8,128)(2,1)S(1)}, u32[]{:S(2)}) copy-start(bf16[24,16,256]{2,1,0:T(8,128)(2,1)S(1)} %collective-permute-done.12.refs_13_) | copy-start | bytes 589828
  161.1 11.4 %collective-permute-start.7 = (bf16[24,16,256]{2,1,0:T(8,128)(2,1)S(1)}, bf16[24,16,256]{2,1,0:T(8,128)(2,1)S(1)}, u32[]{:S(2)}, u32[]{:S(2)}) collective-permute-start(bf16[24,16,256]{2,1,0:T(8,128)(2,1)S(1)} %get-tuple-element.27), channel_id=1, source_target_pairs={{0,8},{1,9},{2,10},{3,11},{4,12},{5,13},{6,14},{7,15},{8,0},{9,1},... | collective-permute-start | bytes 589832 | tf_op jit(solution)/shard_map/ppermute | solution.py:195
  161.2 23.1 %copy-start.6 = (bf16[24,16,256]{2,1,0:T(8,128)(2,1)}, bf16[24,16,256]{2,1,0:T(8,128)(2,1)S(1)}, u32[]{:S(2)}) copy-start(bf16[24,16,256]{2,1,0:T(8,128)(2,1)S(1)} %collective-permute-done.11.refs_12_) | copy-start | bytes 589828
  161.2 19.5 %collective-permute-start.6 = (bf16[24,16,256]{2,1,0:T(8,128)(2,1)S(1)}, bf16[24,16,256]{2,1,0:T(8,128)(2,1)S(1)}, u32[]{:S(2)}, u32[]{:S(2)}) collective-permute-start(bf16[24,16,256]{2,1,0:T(8,128)(2,1)S(1)} %get-tuple-element.28), channel_id=1, source_target_pairs={{0,7},{1,8},{2,9},{3,10},{4,11},{5,12},{6,13},{7,14},{8,15},{9,0},... | collective-permute-start | bytes 589832 | tf_op jit(solution)/shard_map/ppermute | solution.py:195
  170.2 14.1 %copy-start.7 = (bf16[24,16,256]{2,1,0:T(8,128)(2,1)}, bf16[24,16,256]{2,1,0:T(8,128)(2,1)S(1)}, u32[]{:S(2)}) copy-start(bf16[24,16,256]{2,1,0:T(8,128)(2,1)S(1)} %collective-permute-done.10.refs_11_) | copy-start | bytes 589828
  170.2 14.0 %collective-permute-start.5 = (bf16[24,16,256]{2,1,0:T(8,128)(2,1)S(1)}, bf16[24,16,256]{2,1,0:T(8,128)(2,1)S(1)}, u32[]{:S(2)}, u32[]{:S(2)}) collective-permute-start(bf16[24,16,256]{2,1,0:T(8,128)(2,1)S(1)} %get-tuple-element.29), channel_id=1, source_target_pairs={{0,6},{1,7},{2,8},{3,9},{4,10},{5,11},{6,12},{7,13},{8,14},{9,15},... | collective-permute-start | bytes 589832 | tf_op jit(solution)/shard_map/ppermute | solution.py:195
  170.3 14.0 %copy-start.8 = (bf16[24,16,256]{2,1,0:T(8,128)(2,1)}, bf16[24,16,256]{2,1,0:T(8,128)(2,1)S(1)}, u32[]{:S(2)}) copy-start(bf16[24,16,256]{2,1,0:T(8,128)(2,1)S(1)} %collective-permute-done.9.refs_10_) | copy-start | bytes 589828
  170.3 24.4 %collective-permute-start.4 = (bf16[24,16,256]{2,1,0:T(8,128)(2,1)}, bf16[24,16,256]{2,1,0:T(8,128)(2,1)}, u32[]{:S(2)}, u32[]{:S(2)}) collective-permute-start(bf16[24,16,256]{2,1,0:T(8,128)(2,1)} %get-tuple-element.30), channel_id=1, source_target_pairs={{0,5},{1,6},{2,7},{3,8},{4,9},{5,10},{6,11},{7,12},{8,13},{9,14},{... | collective-permute-start | bytes 589832 | tf_op jit(solution)/shard_map/ppermute | solution.py:195
  172.5 11.8 %copy-start.9 = (bf16[24,16,256]{2,1,0:T(8,128)(2,1)}, bf16[24,16,256]{2,1,0:T(8,128)(2,1)S(1)}, u32[]{:S(2)}) copy-start(bf16[24,16,256]{2,1,0:T(8,128)(2,1)S(1)} %collective-permute-done.8.refs_9_) | copy-start | bytes 589828
  172.5 26.8 %collective-permute-start.3 = (bf16[24,16,256]{2,1,0:T(8,128)(2,1)}, bf16[24,16,256]{2,1,0:T(8,128)(2,1)}, u32[]{:S(2)}, u32[]{:S(2)}) collective-permute-start(bf16[24,16,256]{2,1,0:T(8,128)(2,1)} %get-tuple-element.31), channel_id=1, source_target_pairs={{0,4},{1,5},{2,6},{3,7},{4,8},{5,9},{6,10},{7,11},{8,12},{9,13},{1... | collective-permute-start | bytes 589832 | tf_op jit(solution)/shard_map/ppermute | solution.py:195
  172.5 11.8 %copy-start.10 = (bf16[24,16,256]{2,1,0:T(8,128)(2,1)}, bf16[24,16,256]{2,1,0:T(8,128)(2,1)S(1)}, u32[]{:S(2)}) copy-start(bf16[24,16,256]{2,1,0:T(8,128)(2,1)S(1)} %collective-permute-done.7.refs_8_) | copy-start | bytes 589828
  172.5 26.8 %collective-permute-start.2 = (bf16[24,16,256]{2,1,0:T(8,128)(2,1)}, bf16[24,16,256]{2,1,0:T(8,128)(2,1)}, u32[]{:S(2)}, u32[]{:S(2)}) collective-permute-start(bf16[24,16,256]{2,1,0:T(8,128)(2,1)} %get-tuple-element.32), channel_id=1, source_target_pairs={{0,3},{1,4},{2,5},{3,6},{4,7},{5,8},{6,9},{7,10},{8,11},{9,12},{10... | collective-permute-start | bytes 589832 | tf_op jit(solution)/shard_map/ppermute | solution.py:195
  180.7 3.7 %copy-start.11 = (bf16[24,16,256]{2,1,0:T(8,128)(2,1)}, bf16[24,16,256]{2,1,0:T(8,128)(2,1)S(1)}, u32[]{:S(2)}) copy-start(bf16[24,16,256]{2,1,0:T(8,128)(2,1)S(1)} %collective-permute-done.6.refs_7_) | copy-start | bytes 589828
  180.7 18.6 %collective-permute-start.1 = (bf16[24,16,256]{2,1,0:T(8,128)(2,1)S(1)}, bf16[24,16,256]{2,1,0:T(8,128)(2,1)}, u32[]{:S(2)}, u32[]{:S(2)}) collective-permute-start(bf16[24,16,256]{2,1,0:T(8,128)(2,1)S(1)} %get-tuple-element.33), channel_id=1, source_target_pairs={{0,2},{1,3},{2,4},{3,5},{4,6},{5,7},{6,8},{7,9},{8,10},{9,11},{10,... | collective-permute-start | bytes 589832 | tf_op jit(solution)/shard_map/ppermute | solution.py:195
  185.0 14.3 %collective-permute-start = (bf16[24,16,256]{2,1,0:T(8,128)(2,1)S(1)}, bf16[24,16,256]{2,1,0:T(8,128)(2,1)}, u32[]{:S(2)}, u32[]{:S(2)}) collective-permute-start(bf16[24,16,256]{2,1,0:T(8,128)(2,1)S(1)} %get-tuple-element.34), channel_id=1, source_target_pairs={{0,1},{1,2},{2,3},{3,4},{4,5},{5,6},{6,7},{7,8},{8,9},{9,10},{10,1... | collective-permute-start | bytes 589832 | tf_op jit(solution)/shard_map/ppermute | solution.py:195
  348.2 6.4 %copy-start.1 = (bf16[1024,1024]{1,0:T(8,128)(2,1)S(1)}, bf16[1024,1024]{1,0:T(8,128)(2,1)}, u32[]{:S(2)}) copy-start(bf16[1024,1024]{1,0:T(8,128)(2,1)} %param.12) | copy-start | bytes 6291460
  (1 other events, 0.7 us)

commit v7 on v4

--- a/solution.py
+++ b/solution.py
@@ -39,21 +39,38 @@
     return lax.all_to_all(frame_variances, "freq", split_axis=1, concat_axis=2, tiled=True)
 
 
-def sweep_kernel(frames, spec_ref, var_ref, mr_ref, mi_ref, yr, yi, w, pr, pi, pp):
+def sweep_kernel(frames, spec_in, var_in, mr_ref, mi_ref, yr, yi, w, pr, pi, pp):
     count, bins, length = yr.shape
+    peers, _, _, span = spec_in.shape
     chunk = 512
     chunks = length // chunk
 
-    def init(j, carry):
-        yr[j] = spec_ref[0, j].astype(jnp.float32)
-        yi[j] = spec_ref[1, j].astype(jnp.float32)
-        w[j] = 1.0 / var_ref[j].astype(jnp.float32)
+    def init(s, carry):
+        cols = pl.ds(pl.multiple_of(s * span, span), span)
+
+        def per_pair(p, carry):
+            block = var_in[s, p].astype(jnp.float32)
+            w[2 * p, :, cols] = 1.0 / block[:bins]
+            w[2 * p + 1, :, cols] = 1.0 / block[bins:]
+            for half in range(2):
+                j = 2 * p + half
+                spec = spec_in[s, j].astype(jnp.float32)
+                yr[j, :, cols] = spec[:bins]
+                yi[j, :, cols] = spec[bins:]
+            return carry
+
+        lax.fori_loop(0, count // 2, per_pair, 0)
+        return carry
+
+    lax.fori_loop(0, peers, init, 0)
+
+    def init_mix(j, carry):
         lane = lax.broadcasted_iota(jnp.int32, (bins, mr_ref.shape[2]), 1)
         mr_ref[j] = jnp.where(lane == j, 1.0, 0.0).astype(jnp.float32)
         mi_ref[j] = jnp.zeros((bins, mr_ref.shape[2]), jnp.float32)
         return carry
 
-    lax.fori_loop(0, count, init, 0)
+    lax.fori_loop(0, count, init_mix, 0)
 
     def step(k, carry):
         pr[...] = yr[k]
@@ -98,8 +115,9 @@
     lax.fori_loop(0, count, step, 0)
 
 
-def sweep(spec_sw, var_sw, frames):
-    _, count, bins, length = spec_sw.shape
+def sweep(spec_in, var_in, frames):
+    _, count, rows, _ = spec_in.shape
+    bins, length = rows // 2, frames
     lanes = 128
     vmem = pl.BlockSpec(memory_space=pltpu.VMEM)
     return pl.pallas_call(
@@ -119,7 +137,7 @@
             pltpu.VMEM((bins, length), jnp.float32),
         ],
         compiler_params=pltpu.CompilerParams(vmem_limit_bytes=60 * 1024 * 1024),
-    )(spec_sw, var_sw)
+    )(spec_in, var_in)
 
 
 def gather_kernel(x_ref, o_ref, send_sem, recv_sem, local_sem):
@@ -174,9 +192,16 @@
     frames = spectra.shape[3] * lax.axis_size("frame")
     variances = source_model(spectra, norm_gain, w_in, b_in, w_mid, b_mid, w_out, b_out)
 
-    spec_sw = lax.all_to_all(spectra, "frame", split_axis=2, concat_axis=3, tiled=True)
-    var_sw = lax.all_to_all(variances, "frame", split_axis=1, concat_axis=2, tiled=True)
-    mix_real, mix_imag = sweep(spec_sw, var_sw, frames)
+    peers = lax.axis_size("frame")
+    _, _, freq, span = spectra.shape
+    bins = freq // peers
+    spec_send = spectra.reshape(2, count, peers, bins, span).transpose(2, 1, 0, 3, 4)
+    spec_send = spec_send.reshape(peers, count, 2 * bins, span)
+    var_send = variances.reshape(count // 2, 2, peers, bins, span).transpose(2, 0, 1, 3, 4)
+    var_send = var_send.reshape(peers, count // 2, 2 * bins, span)
+    spec_in = lax.all_to_all(spec_send, "frame", split_axis=0, concat_axis=0, tiled=True)
+    var_in = lax.all_to_all(var_send, "frame", split_axis=0, concat_axis=0, tiled=True)
+    mix_real, mix_imag = sweep(spec_in, var_in, frames)
     mix = jnp.stack([mix_real[:, :, :count], mix_imag[:, :, :count]])
     peers = lax.axis_size("frame")
     bins = mix.shape[2]

time: 338 us -> 330 us (0.976)
  waiting for transfers between devices: 62.2 us -> 53.2 us
    reshape x0 -> x3, local copies, waits for them, and re-layouts: none -> 12.7 us  [the longest x1 7.51 us: on_device(): variances.reshape(count // 2, 2, peers, bins, span).transpose(2, 0, 1, 3, 4)]
    all_to_all x2, waiting for transfers between devices: 44.3 us -> 35.6 us  [the longest x1 23.3 us: on_device(): lax.all_to_all(spec_send, 'frame', split_axis=0, concat_axis=0, tiled=True)]
    all_to_all x2 -> x0, local copies, waits for them, and re-layouts: 7.58 us -> none  [the longest x1 4.65 us: on_device(): lax.all_to_all(spectra, 'frame', split_axis=2, concat_axis=3, tiled=True)]
    all_to_all x2, local copies, waits for them, and re-layouts: 10.1 us -> 16.8 us  [source_model(): lax.all_to_all(frame_variances, 'freq', split_axis=1, concat_axis=2, tile...]
    unnamed x21 -> x20, local copies, waits for them, and re-layouts: 35.3 us -> 30.5 us
  transfers between devices with their start and end apart: 3 -> 3, of which waited for: 3 -> 3; matrix products, arithmetic and copies ran while one was open for 9% -> 11% of each run, Pallas kernels for 0% -> 0%
where the time goes in v7:
time: 330 us; the launch traced here: 328 us
  Pallas kernels  119 us (36%)
  local copies, waits for them, and re-layouts  86.2 us (26%)
  waiting for transfers between devices  53.2 us (16%)
  blocking collectives  26 us (8%)
  matrix products  20.9 us (6%)
  starting transfers between devices  15.8 us (5%)
  other arithmetic  6.05 us (2%)
    pallas_call x1, Pallas kernels, sweep(): pl.pallas_call(functools.partial(sweep_kernel, frames), out_shape=(jax.Sh...  107 us
    unnamed x20, local copies, waits for them, and re-layouts  30.5 us
    all_to_all x1, blocking collectives, source_model(): lax.all_to_all(logpower, 'freq', split_axis=2, concat_axis=1, tiled=True)  26 us
    all_to_all x1, waiting for transfers between devices, on_device(): lax.all_to_all(spec_send, 'frame', split_axis=0, concat_axis=0, tiled=True)  23.3 us
    all_to_all x1, waiting for transfers between devices, source_model(): lax.all_to_all(frame_variances, 'freq', split_axis=1, concat_axis=2, tile...  17.6 us
    all_to_all x2, local copies, waits for them, and re-layouts, source_model(): lax.all_to_all(frame_variances, 'freq', split_axis=1, concat_axis=2, tile...  16.8 us
    all_to_all x1, waiting for transfers between devices, on_device(): lax.all_to_all(var_send, 'frame', split_axis=0, concat_axis=0, tiled=True)  12.2 us
    pallas_call x1, Pallas kernels, frame_gather(): pl.pallas_call(gather_kernel, out_shape=jax.ShapeDtypeStruct((n,) + x.sha...  11.7 us
  transfers between devices with their start and end apart: 3, of which 3 were waited for; matrix products, arithmetic and copies ran while one was open for 11% of the time, Pallas kernels for 0%

profile of v7, /device:TPU:0, one launch (start us, length us, event | category | flops | bytes accessed | tf_op | source)
XLA Modules:
  0.0 327.8 jit_solution(17949524226006264677)
XLA Ops:
  0.6 4.0 %fusion.41 = (bf16[1,24,128,256]{3,2,1,0:T(8,128)(2,1)}, bf16[1,24,128,256]{3,2,1,0:T(8,128)(2,1)}) fusion(bf16[2,24,128,256]{3,2,1,0:T(8,128)(2,1)} %param.8), kind=kLoop, calls=%fused_computation.50 | loop fusion | bytes 6291456 | tf_op jit(solution)/shard_map/slice | solution.py:16
  4.7 2.8 copy.76
  7.5 2.7 copy.77
  10.2 2.8 fusion.21
  13.0 26.0 %all_to_all.37 = bf16[24,128,256]{1,0,2:T(8,128)(2,1)S(1)} all-to-all(bf16[24,128,256]{1,0,2:T(8,128)(2,1)S(1)} %fusion.21), channel_id=1, replica_groups=mesh['freq'=8,'frame'=16] {'freq'}, dimensions={2} | all-to-all | bytes 3145728 | tf_op jit(solution)/shard_map/all_to_all | solution.py:21
  39.0 2.2 fusion.42
  42.1 7.7 %fusion.17 = f32[24,32,1024]{2,1,0:T(8,128)} fusion(bf16[1024,1024]{1,0:T(8,128)(2,1)S(1)} %copy-done, f32[1024]{0:T(1024)S(1)} %copy-done.3, bf16[1024,1024]{1,0:T(8,128)(2,1)} %param.10, f32[24,8,4,8,128]{4,3,2,1,0:T(8,128)} %get-tuple-element.21, f32[1024]{0:T(1024)S(1)} %copy-done.4, f32[24,32]{1,0:T(8,128)S(1)} %add_rsqrt_fusion, ...), kind=kOutput, calls=%fused_computation.28 | convolution fusion | flops 3229089792 | bytes 10500096 | tf_op jit(solution)/shard_map/nth,hg->ntg/dot_general | solution.py:32
  49.8 5.9 %fusion.5 = bf16[24,1024,32]{1,2,0:T(8,128)(2,1)S(1)} fusion(f32[1024]{0:T(1024)S(1)} %copy-done.5, bf16[1024,1024]{1,0:T(8,128)(2,1)} %param.14, f32[24,32,1024]{2,1,0:T(8,128)} %fusion.17, f32[1024]{0:T(1024)S(1)} %copy-done.6), kind=kOutput, calls=%fused_computation.8 | convolution fusion | flops 1622409216 | bytes 6823936 | tf_op jit(solution)/shard_map/nth,hf->nft/dot_general | solution.py:35
  55.7 5.9 %copy.59 = bf16[24,1024,32]{2,0,1:T(8,128)(2,1)} copy(bf16[24,1024,32]{1,2,0:T(8,128)(2,1)S(1)} %fusion.5) | data formatting | bytes 3145728 | tf_op jit(solution)/shard_map/convert_element_type | solution.py:38
  61.5 9.5 %reshape.79 = bf16[8,2,49152]{2,1,0:T(2,128)(2,1)} reshape(bf16[1024,24,32]{2,1,0:T(8,128)(2,1)} %bitcast.107) | data formatting | bytes 3145728
  71.0 3.6 %all-to-all-start.2 = ((bf16[8,2,49152]{2,1,0:T(2,128)(2,1)}), bf16[8,2,49152]{2,1,0:T(2,128)(2,1)S(1)}, u32[]{:S(2)}, u32[]{:S(2)}) async-start(bf16[8,2,49152]{2,1,0:T(2,128)(2,1)} %reshape.79), calls=%async_computation.2 | async-start | bytes 3145728 | tf_op jit(solution)/shard_map/all_to_all | solution.py:39
  74.6 3.9 %copy_bitcast_fusion.1 = bf16[16,24,16,256]{3,2,1,0:T(8,128)(2,1)} fusion(bf16[2,24,128,256]{3,2,1,0:T(8,128)(2,1)} %param.8), kind=kLoop, calls=%fused_computation.22 | loop fusion | bytes 6291456 | tf_op jit(solution)/shard_map/reshape | solution.py:199
  78.5 17.6 %all-to-all-done.2 = bf16[8,2,49152]{2,1,0:T(2,128)(2,1)S(1)} async-done(((bf16[8,2,49152]{2,1,0:T(2,128)(2,1)}), bf16[8,2,49152]{2,1,0:T(2,128)(2,1)S(1)}, u32[]{:S(2)}, u32[]{:S(2)}) %all-to-all-start.2) | async-done | bytes 1572896 | tf_op jit(solution)/shard_map/all_to_all | solution.py:39
  96.1 8.1 %all-to-all-start = ((bf16[16,24,16,256]{3,2,1,0:T(8,128)(2,1)}), bf16[16,24,16,256]{3,2,1,0:T(8,128)(2,1)}, u32[]{:S(2)}, u32[]{:S(2)}) async-start(bf16[16,24,16,256]{3,2,1,0:T(8,128)(2,1)} %copy_bitcast_fusion.1), calls=%async_computation | async-start | bytes 6291456 | tf_op jit(solution)/shard_map/all_to_all | solution.py:202
  104.2 5.4 %reshape.80 = bf16[1024,24,32]{2,1,0:T(8,128)(2,1)} reshape(bf16[8,2,49152]{2,1,0:T(2,128)(2,1)S(1)} %all-to-all-done.2) | data formatting | bytes 3145728
  109.6 9.5 %copy.61 = bf16[24,128,8,32]{3,2,1,0:T(8,128)(2,1)} copy(bf16[24,128,8,32]{3,0,1,2:T(8,128)(2,1)} %bitcast.103) | data formatting | bytes 3145728 | tf_op jit(solution)/shard_map/all_to_all | solution.py:39
  119.1 7.5 %reshape.65 = bf16[12,2,16,8,256]{4,3,2,1,0:T(8,128)(2,1)S(1)} reshape(bf16[24,128,8,32]{3,2,1,0:T(8,128)(2,1)} %copy.61) | data formatting | bytes 3145728 | tf_op jit(solution)/shard_map/reshape | solution.py:200
  127.9 23.3 %all-to-all-done.spec_in = bf16[16,24,16,256]{3,2,1,0:T(8,128)(2,1)} async-done(((bf16[16,24,16,256]{3,2,1,0:T(8,128)(2,1)}), bf16[16,24,16,256]{3,2,1,0:T(8,128)(2,1)}, u32[]{:S(2)}, u32[]{:S(2)}) %all-to-all-start) | async-done | bytes 3145760 | tf_op jit(solution)/shard_map/all_to_all | solution.py:202
  151.2 4.1 %all-to-all-start.3 = ((bf16[16,12,16,256]{3,2,1,0:T(8,128)(2,1)}), bf16[16,12,16,256]{3,2,1,0:T(8,128)(2,1)S(1)}, u32[]{:S(2)}, u32[]{:S(2)}) async-start(bf16[16,12,16,256]{3,2,1,0:T(8,128)(2,1)} %copy_bitcast_fusion.2), calls=%async_computation.3 | async-start | bytes 3145728 | tf_op jit(solution)/shard_map/all_to_all | solution.py:203
  155.4 7.3 %copy.70 = bf16[24,128,8,32]{1,3,2,0:T(8,128)(2,1)} copy(bf16[24,128,8,32]{3,0,1,2:T(8,128)(2,1)} %bitcast.104) | data formatting | bytes 3145728 | tf_op jit(solution)/shard_map/all_to_all | solution.py:39
  162.7 2.6 copy.72
  165.3 12.2 %all-to-all-done.3.var_in = bf16[16,12,16,256]{3,2,1,0:T(8,128)(2,1)S(1)} async-done(((bf16[16,12,16,256]{3,2,1,0:T(8,128)(2,1)}), bf16[16,12,16,256]{3,2,1,0:T(8,128)(2,1)S(1)}, u32[]{:S(2)}, u32[]{:S(2)}) %all-to-all-start.3) | async-done | bytes 1572896 | tf_op jit(solution)/shard_map/all_to_all | solution.py:203
  178.6 107.1 %shard_map.95 = (f32[24,8,128]{2,1,0:T(8,128)}, f32[24,8,128]{2,1,0:T(8,128)}) custom-call(bf16[16,24,16,256]{3,2,1,0:T(8,128)(2,1)} %all-to-all-done.spec_in, bf16[16,12,16,256]{3,2,1,0:T(8,128)(2,1)} %copy-done.2), custom_call_target="tpu_custom_call" | custom-call | tf_op jit(solution)/shard_map/pallas_call | solution.py:123
  287.5 11.7 %shard_map.96 = f32[16,72,128]{2,1,0:T(8,128)} custom-call(f32[72,128]{1,0:T(8,128)} %reshape.67.x_ref), custom_call_target="tpu_custom_call" | custom-call | tf_op jit(solution)/shard_map/pallas_call | solution.py:176
  299.2 4.1 %reshape.68 = f32[16,2,24,8,24]{4,3,2,1,0:T(8,128)} reshape(f32[16,72,128]{2,1,0:T(8,128)} %shard_map.96) | data formatting | bytes 1179648 | tf_op jit(solution)/shard_map/reshape | solution.py:209
  303.3 2.3 copy.92
  305.7 1.9 slice_bitcast_fusion
  308.1 1.9 copy.66
  309.9 1.9 copy.64
  311.8 2.2 copy.68
  314.1 7.3 %fusion.13 = f32[128,48,256]{2,1,0:T(8,128)S(1)} fusion(f32[48,128,48]{2,0,1:T(8,128)} %copy.68, bf16[48,128,256]{2,1,0:T(8,128)(2,1)} %bitcast.105), kind=kOutput, calls=%fused_computation.19 | convolution fusion | flops 905969664 | bytes 10616832 | tf_op jit(solution)/shard_map/jfa,aft->jft/dot_general | solution.py:216
  321.4 6.3 %copy.71 = f32[2,24,128,256]{3,2,1,0:T(8,128)} copy(f32[2,24,128,256]{3,1,0,2:T(8,128)S(1)} %bitcast.106) | data formatting | bytes 12582912
  (25 shorter events, 5.7 us)
Async XLA Ops:
  0.6 41.4 %copy-start = (bf16[1024,1024]{1,0:T(8,128)(2,1)S(1)}, bf16[1024,1024]{1,0:T(8,128)(2,1)}, u32[]{:S(2)}) copy-start(bf16[1024,1024]{1,0:T(8,128)(2,1)} %param.12) | copy-start | bytes 6291460
  41.2 0.9 copy-start.3
  41.2 0.9 copy-start.4
  42.1 7.7 %copy-start.5 = (f32[1024]{0:T(1024)S(1)}, f32[1024]{0:T(1024)}, u32[]{:S(2)}) copy-start(f32[1024]{0:T(1024)} %param.15) | copy-start | bytes 12292
  42.1 7.7 %copy-start.6 = (f32[1024]{0:T(1024)S(1)}, f32[1024]{0:T(1024)}, u32[]{:S(2)}) copy-start(f32[1024]{0:T(1024)} %param.13) | copy-start | bytes 12292
  71.0 25.1 %all-to-all-start.2 = ((bf16[8,2,49152]{2,1,0:T(2,128)(2,1)}), bf16[8,2,49152]{2,1,0:T(2,128)(2,1)S(1)}, u32[]{:S(2)}, u32[]{:S(2)}) async-start(bf16[8,2,49152]{2,1,0:T(2,128)(2,1)} %reshape.79), calls=%async_computation.2 | async-start | bytes 3145728 | tf_op jit(solution)/shard_map/all_to_all | solution.py:39
  96.1 55.1 %all-to-all-start = ((bf16[16,24,16,256]{3,2,1,0:T(8,128)(2,1)}), bf16[16,24,16,256]{3,2,1,0:T(8,128)(2,1)}, u32[]{:S(2)}, u32[]{:S(2)}) async-start(bf16[16,24,16,256]{3,2,1,0:T(8,128)(2,1)} %copy_bitcast_fusion.1), calls=%async_computation | async-start | bytes 6291456 | tf_op jit(solution)/shard_map/all_to_all | solution.py:202
  151.2 26.3 %all-to-all-start.3 = ((bf16[16,12,16,256]{3,2,1,0:T(8,128)(2,1)}), bf16[16,12,16,256]{3,2,1,0:T(8,128)(2,1)S(1)}, u32[]{:S(2)}, u32[]{:S(2)}) async-start(bf16[16,12,16,256]{3,2,1,0:T(8,128)(2,1)} %copy_bitcast_fusion.2), calls=%async_computation.3 | async-start | bytes 3145728 | tf_op jit(solution)/shard_map/all_to_all | solution.py:203
  177.5 1.1 copy-start.2
  321.4 6.4 %copy-start.1 = (bf16[1024,1024]{1,0:T(8,128)(2,1)S(1)}, bf16[1024,1024]{1,0:T(8,128)(2,1)}, u32[]{:S(2)}) copy-start(bf16[1024,1024]{1,0:T(8,128)(2,1)} %param.12) | copy-start | bytes 6291460

commit v8 on v7

--- a/solution.py
+++ b/solution.py
@@ -18,25 +18,29 @@
     logpower = jnp.log(real_part * real_part + imag_part * imag_part + power_floor).astype(
         jnp.bfloat16
     )
-    values = lax.all_to_all(logpower, "freq", split_axis=2, concat_axis=1, tiled=True).astype(
-        jnp.float32
-    )
-    average = jnp.mean(values, axis=1, keepdims=True)
+    count, freq, span = logpower.shape
+    shards = lax.axis_size("freq")
+    rows = span // shards
+    send = logpower.transpose(0, 2, 1).reshape(count, shards, rows, freq).transpose(1, 0, 2, 3)
+    received = lax.all_to_all(send, "freq", split_axis=0, concat_axis=0, tiled=True)
+    values = received.transpose(1, 2, 0, 3).reshape(count, rows, shards * freq).astype(jnp.float32)
+    average = jnp.mean(values, axis=2, keepdims=True)
     centred = values - average
-    spread = jnp.mean(centred * centred, axis=1, keepdims=True)
-    normed = (centred * lax.rsqrt(spread + epsilon) * norm_gain[None, :, None]).astype(jnp.bfloat16)
+    spread = jnp.mean(centred * centred, axis=2, keepdims=True)
+    normed = (centred * lax.rsqrt(spread + epsilon) * norm_gain).astype(jnp.bfloat16)
     hidden_one = jax.nn.silu(
-        jnp.einsum("nft,fh->nth", normed, w_in, preferred_element_type=jnp.float32) + b_in
+        jnp.einsum("ntf,fh->nth", normed, w_in, preferred_element_type=jnp.float32) + b_in
     ).astype(jnp.bfloat16)
     hidden_two = jax.nn.silu(
         jnp.einsum("nth,hg->ntg", hidden_one, w_mid, preferred_element_type=jnp.float32) + b_mid
     ).astype(jnp.bfloat16)
     output_pre = (
-        jnp.einsum("nth,hf->nft", hidden_two, w_out, preferred_element_type=jnp.float32)
-        + b_out[None, :, None]
+        jnp.einsum("nth,hf->ntf", hidden_two, w_out, preferred_element_type=jnp.float32) + b_out
     )
     frame_variances = (jax.nn.softplus(output_pre) + variance_floor).astype(jnp.bfloat16)
-    return lax.all_to_all(frame_variances, "freq", split_axis=1, concat_axis=2, tiled=True)
+    send = frame_variances.reshape(count, rows, shards, freq).transpose(2, 0, 1, 3)
+    received = lax.all_to_all(send, "freq", split_axis=0, concat_axis=0, tiled=True)
+    return received.transpose(1, 3, 0, 2).reshape(count, freq, span)
 
 
 def sweep_kernel(frames, spec_in, var_in, mr_ref, mi_ref, yr, yi, w, pr, pi, pp):

time: 330 us -> 321 us (0.973)
  local copies, waits for them, and re-layouts: 86.2 us -> 63.6 us
  waiting for transfers between devices: 53.2 us -> 65.6 us
    unnamed x20, local copies, waits for them, and re-layouts: 30.5 us -> 15 us
    all_to_all x2 -> x1, local copies, waits for them, and re-layouts: 16.8 us -> 3.03 us  [source_model(): lax.all_to_all(send, 'freq', split_axis=0, concat_axis=0, tiled=True)]
    another operation x0 -> x1, local copies, waits for them, and re-layouts: none -> 8.41 us  [on_device(): variances.reshape(count // 2, 2, peers, bins, span).transpose(2, 0, 1, 3, 4)]
    transpose x0 -> x2, local copies, waits for them, and re-layouts: none -> 6.88 us  [the longest x1 6.6 us: source_model(): return received.transpose(1, 3, 0, 2).reshape(count, freq, span)]
    reshape x1, local copies, waits for them, and re-layouts: 7.51 us -> 1.44 us  [source_model(): frame_variances.reshape(count, rows, shards, freq).transpose(2, 0, 1, 3)]
    all_to_all x1, waiting for transfers between devices: 23.3 us -> 29.3 us  [on_device(): lax.all_to_all(spec_send, 'frame', split_axis=0, concat_axis=0, tiled=True)]
    convert_element_type x1 -> x0, local copies, waits for them, and re-layouts: 5.85 us -> none  [source_model(): (jax.nn.softplus(output_pre) + variance_floor).astype(jnp.bfloat16)]
    all_to_all x1, waiting for transfers between devices: 12.2 us -> 16.7 us  [on_device(): lax.all_to_all(var_send, 'frame', split_axis=0, concat_axis=0, tiled=True)]
  transfers between devices with their start and end apart: 3 -> 3, of which waited for: 3 -> 3; matrix products, arithmetic and copies ran while one was open for 11% -> 8% of each run, Pallas kernels for 0% -> 0%
where the time goes in v8:
time: 321 us; the launch traced here: 319 us
  Pallas kernels  119 us (37%)
  waiting for transfers between devices  65.6 us (20%)
  local copies, waits for them, and re-layouts  63.6 us (20%)
  blocking collectives  26 us (8%)
  matrix products  19.6 us (6%)
  starting transfers between devices  17.1 us (5%)
  other arithmetic  7.21 us (2%)
    pallas_call x1, Pallas kernels, sweep(): pl.pallas_call(functools.partial(sweep_kernel, frames), out_shape=(jax.Sh...  107 us
    all_to_all x1, waiting for transfers between devices, on_device(): lax.all_to_all(spec_send, 'frame', split_axis=0, concat_axis=0, tiled=True)  29.3 us
    all_to_all x1, blocking collectives, source_model(): lax.all_to_all(send, 'freq', split_axis=0, concat_axis=0, tiled=True)  26 us
    all_to_all x1, waiting for transfers between devices, source_model(): lax.all_to_all(send, 'freq', split_axis=0, concat_axis=0, tiled=True)  19.6 us
    all_to_all x1, waiting for transfers between devices, on_device(): lax.all_to_all(var_send, 'frame', split_axis=0, concat_axis=0, tiled=True)  16.7 us
    unnamed x20, local copies, waits for them, and re-layouts  15 us
    pallas_call x1, Pallas kernels, frame_gather(): pl.pallas_call(gather_kernel, out_shape=jax.ShapeDtypeStruct((n,) + x.sha...  11.9 us
    another operation x1, local copies, waits for them, and re-layouts, on_device(): variances.reshape(count // 2, 2, peers, bins, span).transpose(2, 0, 1, 3, 4)  8.41 us
  transfers between devices with their start and end apart: 3, of which 3 were waited for; matrix products, arithmetic and copies ran while one was open for 8% of the time, Pallas kernels for 0%

profile of v8, /device:TPU:0, one launch (start us, length us, event | category | flops | bytes accessed | tf_op | source)
XLA Modules:
  0.0 319.0 jit_solution(13118298441034376899)
XLA Ops:
  0.6 4.0 %fusion.37 = (bf16[1,24,128,256]{3,2,1,0:T(8,128)(2,1)}, bf16[1,24,128,256]{3,2,1,0:T(8,128)(2,1)}) fusion(bf16[2,24,128,256]{3,2,1,0:T(8,128)(2,1)} %param.8), kind=kLoop, calls=%fused_computation.45 | loop fusion | bytes 6291456 | tf_op jit(solution)/shard_map/slice | solution.py:16
  4.7 2.6 copy.74
  7.3 2.6 copy.75
  9.9 2.8 log_convert_fusion
  13.0 26.0 %all_to_all.20 = bf16[8,24,32,128]{3,2,1,0:T(8,128)(2,1)S(1)} all-to-all(bf16[8,24,32,128]{3,2,1,0:T(8,128)(2,1)S(1)} %copy.58), channel_id=1, replica_groups=mesh['freq'=8,'frame'=16] {'freq'}, dimensions={0} | all-to-all | bytes 3145728 | tf_op jit(solution)/shard_map/all_to_all | solution.py:25
  40.8 7.2 %fusion.13 = f32[24,32,1024]{2,1,0:T(8,128)} fusion(bf16[1024,1024]{1,0:T(8,128)(2,1)S(1)} %copy-done, f32[1024]{0:T(1024)S(1)} %copy-done.4, bf16[1024,1024]{1,0:T(8,128)(2,1)} %param.10, f32[1024]{0:T(1024)S(1)} %copy-done.5, f32[24,32]{1,0:T(8,128)S(1)} %add_rsqrt_fusion, f32[24,32]{1,0:T(8,128)S(1)} %broadcast_multiply_fusion, ...), kind=kOutput, calls=%fused_computation.22 | convolution fusion | flops 3229876224 | bytes 8927232 | tf_op jit(solution)/shard_map/nth,hg->ntg/dot_general | solution.py:35
  48.0 5.9 %fusion.23 = bf16[24,4,8,8,128]{4,3,2,1,0:T(8,128)(2,1)S(1)} fusion(f32[1024]{0:T(1024)S(1)} %copy-done.6, bf16[1024,1024]{1,0:T(8,128)(2,1)} %param.14, f32[24,32,1024]{2,1,0:T(8,128)} %fusion.13, f32[1024]{0:T(1024)S(1)} %copy-done.7), kind=kOutput, calls=%fused_computation.35 | convolution fusion | flops 1622409216 | bytes 6823936 | tf_op jit(solution)/shard_map/nth,hf->ntf/dot_general | solution.py:38
  53.9 1.4 copy.91
  55.4 4.4 %all-to-all-start.2 = ((bf16[8,24,32,128]{3,2,1,0:T(8,128)(2,1)}), bf16[8,24,32,128]{3,2,1,0:T(8,128)(2,1)}, u32[]{:S(2)}, u32[]{:S(2)}) async-start(bf16[8,24,32,128]{3,2,1,0:T(8,128)(2,1)} %bitcast.100), calls=%async_computation.2 | async-start | bytes 3145728 | tf_op jit(solution)/shard_map/all_to_all | solution.py:42
  59.8 2.0 copy_bitcast_fusion.1
  61.8 19.6 %all-to-all-done.2 = bf16[8,24,32,128]{3,2,1,0:T(8,128)(2,1)} async-done(((bf16[8,24,32,128]{3,2,1,0:T(8,128)(2,1)}), bf16[8,24,32,128]{3,2,1,0:T(8,128)(2,1)}, u32[]{:S(2)}, u32[]{:S(2)}) %all-to-all-start.2) | async-done | bytes 1572896 | tf_op jit(solution)/shard_map/all_to_all | solution.py:42
  81.4 8.1 %all-to-all-start = ((bf16[16,24,16,256]{3,2,1,0:T(8,128)(2,1)}), bf16[16,24,16,256]{3,2,1,0:T(8,128)(2,1)}, u32[]{:S(2)}, u32[]{:S(2)}) async-start(bf16[16,24,16,256]{3,2,1,0:T(8,128)(2,1)} %copy_bitcast_fusion.1), calls=%async_computation | async-start | bytes 6291456 | tf_op jit(solution)/shard_map/all_to_all | solution.py:206
  89.5 6.6 %copy.62 = bf16[24,128,8,32]{3,2,1,0:T(8,128)(2,1)} copy(bf16[24,128,8,32]{1,3,0,2:T(8,128)(2,1)} %bitcast.13) | data formatting | bytes 3145728 | tf_op jit(solution)/shard_map/transpose | solution.py:43
  96.1 8.4 %reshape_reshape.3 = bf16[12,2,16,8,256]{4,3,2,1,0:T(8,128)(2,1)} reshape(bf16[24,128,8,32]{3,2,1,0:T(8,128)(2,1)} %copy.62) | data formatting | bytes 3145728 | tf_op jit(solution)/shard_map/reshape;reshape | solution.py:204
  104.5 2.7 copy_bitcast_fusion.2
  107.2 29.3 %all-to-all-done.spec_in = bf16[16,24,16,256]{3,2,1,0:T(8,128)(2,1)} async-done(((bf16[16,24,16,256]{3,2,1,0:T(8,128)(2,1)}), bf16[16,24,16,256]{3,2,1,0:T(8,128)(2,1)}, u32[]{:S(2)}, u32[]{:S(2)}) %all-to-all-start) | async-done | bytes 3145760 | tf_op jit(solution)/shard_map/all_to_all | solution.py:206
  136.5 4.6 %all-to-all-start.3 = ((bf16[16,12,16,256]{3,2,1,0:T(8,128)(2,1)}), bf16[16,12,16,256]{3,2,1,0:T(8,128)(2,1)}, u32[]{:S(2)}, u32[]{:S(2)}) async-start(bf16[16,12,16,256]{3,2,1,0:T(8,128)(2,1)} %copy_bitcast_fusion.2), calls=%async_computation.3 | async-start | bytes 3145728 | tf_op jit(solution)/shard_map/all_to_all | solution.py:207
  141.1 3.0 copy.61
  144.2 2.6 copy.72
  146.7 16.7 %all-to-all-done.3.var_in = bf16[16,12,16,256]{3,2,1,0:T(8,128)(2,1)} async-done(((bf16[16,12,16,256]{3,2,1,0:T(8,128)(2,1)}), bf16[16,12,16,256]{3,2,1,0:T(8,128)(2,1)}, u32[]{:S(2)}, u32[]{:S(2)}) %all-to-all-start.3) | async-done | bytes 1572896 | tf_op jit(solution)/shard_map/all_to_all | solution.py:207
  163.4 107.1 %shard_map.95 = (f32[24,8,128]{2,1,0:T(8,128)}, f32[24,8,128]{2,1,0:T(8,128)}) custom-call(bf16[16,24,16,256]{3,2,1,0:T(8,128)(2,1)} %all-to-all-done.spec_in, bf16[16,12,16,256]{3,2,1,0:T(8,128)(2,1)} %all-to-all-done.3.var_in), custom_call_target="tpu_custom_call" | custom-call | tf_op jit(solution)/shard_map/pallas_call | solution.py:127
  272.3 11.9 %shard_map.96 = f32[16,72,128]{2,1,0:T(8,128)} custom-call(f32[72,128]{1,0:T(8,128)} %reshape.70.x_ref), custom_call_target="tpu_custom_call" | custom-call | tf_op jit(solution)/shard_map/pallas_call | solution.py:180
  284.2 4.1 %reshape.71 = f32[16,2,24,8,24]{4,3,2,1,0:T(8,128)} reshape(f32[16,72,128]{2,1,0:T(8,128)} %shard_map.96) | data formatting | bytes 1179648 | tf_op jit(solution)/shard_map/reshape | solution.py:213
  288.3 2.3 copy.90
  291.8 1.9 slice_bitcast_fusion
  293.7 1.8 copy.66
  295.6 2.6 copy.67
  298.1 2.6 copy.65
  300.7 2.3 maximum_maximum_fusion
  303.0 3.2 %copy.69 = f32[48,128,48]{2,0,1:T(8,128)} copy(f32[48,128,48]{1,2,0:T(8,128)} %maximum_maximum_fusion) | data formatting | bytes 2359296 | tf_op jit(solution)/shard_map/concatenate | solution.py:218
  306.2 6.5 %fusion.9 = f32[128,48,256]{2,1,0:T(8,128)S(1)} fusion(f32[48,128,48]{2,0,1:T(8,128)} %copy.69, bf16[48,128,256]{2,1,0:T(8,128)(2,1)S(1)} %bitcast.96), kind=kOutput, calls=%fused_computation.13 | convolution fusion | flops 905969664 | bytes 10616832 | tf_op jit(solution)/shard_map/jfa,aft->jft/dot_general | solution.py:220
  312.7 6.3 %copy.71 = f32[2,24,128,256]{3,2,1,0:T(8,128)} copy(f32[2,24,128,256]{3,1,0,2:T(8,128)S(1)} %bitcast.97) | data formatting | bytes 12582912
  (25 shorter events, 5.0 us)
Async XLA Ops:
  0.6 40.1 %copy-start = (bf16[1024,1024]{1,0:T(8,128)(2,1)S(1)}, bf16[1024,1024]{1,0:T(8,128)(2,1)}, u32[]{:S(2)}) copy-start(bf16[1024,1024]{1,0:T(8,128)(2,1)} %param.12) | copy-start | bytes 6291460
  13.0 27.8 %copy-start.4 = (f32[1024]{0:T(1024)S(1)}, f32[1024]{0:T(1024)}, u32[]{:S(2)}) copy-start(f32[1024]{0:T(1024)} %param.11) | copy-start | bytes 12292
  13.0 27.8 %copy-start.5 = (f32[1024]{0:T(1024)S(1)}, f32[1024]{0:T(1024)}, u32[]{:S(2)}) copy-start(f32[1024]{0:T(1024)} %param.9) | copy-start | bytes 12292
  39.0 1.1 copy-start.3
  40.7 7.3 %copy-start.6 = (f32[1024]{0:T(1024)S(1)}, f32[1024]{0:T(1024)}, u32[]{:S(2)}) copy-start(f32[1024]{0:T(1024)} %param.15) | copy-start | bytes 12292
  40.7 7.2 %copy-start.7 = (f32[1024]{0:T(1024)S(1)}, f32[1024]{0:T(1024)}, u32[]{:S(2)}) copy-start(f32[1024]{0:T(1024)} %param.13) | copy-start | bytes 12292
  53.9 5.9 %copy-start.2 = (bf16[2,24,128,256]{3,2,1,0:T(8,128)(2,1)S(1)}, bf16[2,24,128,256]{3,2,1,0:T(8,128)(2,1)}, u32[]{:S(2)}) copy-start(bf16[2,24,128,256]{3,2,1,0:T(8,128)(2,1)} %param.8) | copy-start | bytes 9437188
  55.4 26.0 %all-to-all-start.2 = ((bf16[8,24,32,128]{3,2,1,0:T(8,128)(2,1)}), bf16[8,24,32,128]{3,2,1,0:T(8,128)(2,1)}, u32[]{:S(2)}, u32[]{:S(2)}) async-start(bf16[8,24,32,128]{3,2,1,0:T(8,128)(2,1)} %bitcast.100), calls=%async_computation.2 | async-start | bytes 3145728 | tf_op jit(solution)/shard_map/all_to_all | solution.py:42
  81.4 55.1 %all-to-all-start = ((bf16[16,24,16,256]{3,2,1,0:T(8,128)(2,1)}), bf16[16,24,16,256]{3,2,1,0:T(8,128)(2,1)}, u32[]{:S(2)}, u32[]{:S(2)}) async-start(bf16[16,24,16,256]{3,2,1,0:T(8,128)(2,1)} %copy_bitcast_fusion.1), calls=%async_computation | async-start | bytes 6291456 | tf_op jit(solution)/shard_map/all_to_all | solution.py:206
  136.5 26.9 %all-to-all-start.3 = ((bf16[16,12,16,256]{3,2,1,0:T(8,128)(2,1)}), bf16[16,12,16,256]{3,2,1,0:T(8,128)(2,1)}, u32[]{:S(2)}, u32[]{:S(2)}) async-start(bf16[16,12,16,256]{3,2,1,0:T(8,128)(2,1)} %copy_bitcast_fusion.2), calls=%async_computation.3 | async-start | bytes 3145728 | tf_op jit(solution)/shard_map/all_to_all | solution.py:207
  312.6 6.4 %copy-start.1 = (bf16[1024,1024]{1,0:T(8,128)(2,1)S(1)}, bf16[1024,1024]{1,0:T(8,128)(2,1)}, u32[]{:S(2)}) copy-start(bf16[1024,1024]{1,0:T(8,128)(2,1)} %param.12) | copy-start | bytes 6291460

commit v9 on v8

--- a/solution.py
+++ b/solution.py
@@ -40,7 +40,7 @@
     frame_variances = (jax.nn.softplus(output_pre) + variance_floor).astype(jnp.bfloat16)
     send = frame_variances.reshape(count, rows, shards, freq).transpose(2, 0, 1, 3)
     received = lax.all_to_all(send, "freq", split_axis=0, concat_axis=0, tiled=True)
-    return received.transpose(1, 3, 0, 2).reshape(count, freq, span)
+    return received.transpose(1, 3, 0, 2).reshape(count, freq, span), received
 
 
 def sweep_kernel(frames, spec_in, var_in, mr_ref, mi_ref, yr, yi, w, pr, pi, pp):
@@ -194,15 +194,16 @@
 def on_device(spectra, norm_gain, w_in, b_in, w_mid, b_mid, w_out, b_out):
     count = spectra.shape[1]
     frames = spectra.shape[3] * lax.axis_size("frame")
-    variances = source_model(spectra, norm_gain, w_in, b_in, w_mid, b_mid, w_out, b_out)
+    variances, received = source_model(spectra, norm_gain, w_in, b_in, w_mid, b_mid, w_out, b_out)
 
     peers = lax.axis_size("frame")
     _, _, freq, span = spectra.shape
     bins = freq // peers
     spec_send = spectra.reshape(2, count, peers, bins, span).transpose(2, 1, 0, 3, 4)
     spec_send = spec_send.reshape(peers, count, 2 * bins, span)
-    var_send = variances.reshape(count // 2, 2, peers, bins, span).transpose(2, 0, 1, 3, 4)
-    var_send = var_send.reshape(peers, count // 2, 2 * bins, span)
+    shards, rows = received.shape[0], received.shape[2]
+    var_send = received.reshape(shards, count // 2, 2, rows, peers, bins)
+    var_send = var_send.transpose(4, 1, 2, 5, 0, 3).reshape(peers, count // 2, 2 * bins, span)
     spec_in = lax.all_to_all(spec_send, "frame", split_axis=0, concat_axis=0, tiled=True)
     var_in = lax.all_to_all(var_send, "frame", split_axis=0, concat_axis=0, tiled=True)
     mix_real, mix_imag = sweep(spec_in, var_in, frames)

time: 321 us -> 321 us (level)
  local copies, waits for them, and re-layouts: 63.6 us -> 73.3 us
  waiting for transfers between devices: 65.6 us -> 55.9 us
    all_to_all x1, waiting for transfers between devices: 29.3 us -> 19.6 us  [on_device(): lax.all_to_all(spec_send, 'frame', split_axis=0, concat_axis=0, tiled=True)]
    another operation x1 -> x0, local copies, waits for them, and re-layouts: 8.41 us -> none  [on_device(): variances.reshape(count // 2, 2, peers, bins, span).transpose(2, 0, 1, 3, 4)]
    all_to_all x1 -> x2, local copies, waits for them, and re-layouts: 3.03 us -> 9.28 us  [source_model(): lax.all_to_all(send, 'freq', split_axis=0, concat_axis=0, tiled=True)]
    transpose x1, local copies, waits for them, and re-layouts: 6.6 us -> 12.7 us  [on_device(): var_send.transpose(4, 1, 2, 5, 0, 3)]
    reshape x1, local copies, waits for them, and re-layouts: 2.71 us -> 8.41 us  [on_device(): var_send.transpose(4, 1, 2, 5, 0, 3)]
  transfers between devices with their start and end apart: 3 -> 3, of which waited for: 3 -> 3; matrix products, arithmetic and copies ran while one was open for 8% -> 11% of each run, Pallas kernels for 0% -> 0%
where the time goes in v9:
time: 321 us; the launch traced here: 319 us
  Pallas kernels  119 us (37%)
  local copies, waits for them, and re-layouts  73.3 us (23%)
  waiting for transfers between devices  55.9 us (17%)
  blocking collectives  26 us (8%)
  matrix products  19.6 us (6%)
  starting transfers between devices  17.2 us (5%)
  other arithmetic  7.12 us (2%)
    pallas_call x1, Pallas kernels, sweep(): pl.pallas_call(functools.partial(sweep_kernel, frames), out_shape=(jax.Sh...  107 us
    all_to_all x1, blocking collectives, source_model(): lax.all_to_all(send, 'freq', split_axis=0, concat_axis=0, tiled=True)  26 us
    all_to_all x1, waiting for transfers between devices, on_device(): lax.all_to_all(spec_send, 'frame', split_axis=0, concat_axis=0, tiled=True)  19.6 us
    all_to_all x1, waiting for transfers between devices, source_model(): lax.all_to_all(send, 'freq', split_axis=0, concat_axis=0, tiled=True)  19.6 us
    all_to_all x1, waiting for transfers between devices, on_device(): lax.all_to_all(var_send, 'frame', split_axis=0, concat_axis=0, tiled=True)  16.7 us
    unnamed x20, local copies, waits for them, and re-layouts  15 us
    transpose x1, local copies, waits for them, and re-layouts, on_device(): var_send.transpose(4, 1, 2, 5, 0, 3)  12.7 us
    pallas_call x1, Pallas kernels, frame_gather(): pl.pallas_call(gather_kernel, out_shape=jax.ShapeDtypeStruct((n,) + x.sha...  11.9 us
  transfers between devices with their start and end apart: 3, of which 3 were waited for; matrix products, arithmetic and copies ran while one was open for 11% of the time, Pallas kernels for 0%

profile of v9, /device:TPU:0, one launch (start us, length us, event | category | flops | bytes accessed | tf_op | source)
XLA Modules:
  0.0 318.9 jit_solution(15441655055486572811)
XLA Ops:
  0.6 4.0 %fusion.37 = (bf16[1,24,128,256]{3,2,1,0:T(8,128)(2,1)}, bf16[1,24,128,256]{3,2,1,0:T(8,128)(2,1)}) fusion(bf16[2,24,128,256]{3,2,1,0:T(8,128)(2,1)} %param.8), kind=kLoop, calls=%fused_computation.44 | loop fusion | bytes 6291456 | tf_op jit(solution)/shard_map/slice | solution.py:16
  4.7 2.6 copy.73
  7.3 2.6 copy.74
  9.9 2.8 log_convert_fusion
  13.0 26.0 %all_to_all.20 = bf16[8,24,32,128]{3,2,1,0:T(8,128)(2,1)S(1)} all-to-all(bf16[8,24,32,128]{3,2,1,0:T(8,128)(2,1)S(1)} %copy.58), channel_id=1, replica_groups=mesh['freq'=8,'frame'=16] {'freq'}, dimensions={0} | all-to-all | bytes 3145728 | tf_op jit(solution)/shard_map/all_to_all | solution.py:25
  40.8 7.2 %fusion.13 = f32[24,32,1024]{2,1,0:T(8,128)} fusion(bf16[1024,1024]{1,0:T(8,128)(2,1)S(1)} %copy-done, f32[1024]{0:T(1024)S(1)} %copy-done.4, bf16[1024,1024]{1,0:T(8,128)(2,1)} %param.10, f32[1024]{0:T(1024)S(1)} %copy-done.5, f32[24,32]{1,0:T(8,128)S(1)} %add_rsqrt_fusion, f32[24,32]{1,0:T(8,128)S(1)} %broadcast_multiply_fusion, ...), kind=kOutput, calls=%fused_computation.22 | convolution fusion | flops 3229876224 | bytes 8927232 | tf_op jit(solution)/shard_map/nth,hg->ntg/dot_general | solution.py:35
  48.0 5.9 %fusion.23 = bf16[24,4,8,8,128]{4,3,2,1,0:T(8,128)(2,1)S(1)} fusion(f32[1024]{0:T(1024)S(1)} %copy-done.6, bf16[1024,1024]{1,0:T(8,128)(2,1)} %param.14, f32[24,32,1024]{2,1,0:T(8,128)} %fusion.13, f32[1024]{0:T(1024)S(1)} %copy-done.7), kind=kOutput, calls=%fused_computation.34 | convolution fusion | flops 1622409216 | bytes 6823936 | tf_op jit(solution)/shard_map/nth,hf->ntf/dot_general | solution.py:38
  53.9 1.4 copy.89
  55.4 4.4 %all-to-all-start.2 = ((bf16[8,24,32,128]{3,2,1,0:T(8,128)(2,1)}), bf16[8,24,32,128]{3,2,1,0:T(8,128)(2,1)}, u32[]{:S(2)}, u32[]{:S(2)}) async-start(bf16[8,24,32,128]{3,2,1,0:T(8,128)(2,1)} %bitcast.98), calls=%async_computation.2 | async-start | bytes 3145728 | tf_op jit(solution)/shard_map/all_to_all | solution.py:42
  59.8 2.0 copy_bitcast_fusion.1
  61.8 19.6 %all-to-all-done.2 = bf16[8,24,32,128]{3,2,1,0:T(8,128)(2,1)} async-done(((bf16[8,24,32,128]{3,2,1,0:T(8,128)(2,1)}), bf16[8,24,32,128]{3,2,1,0:T(8,128)(2,1)}, u32[]{:S(2)}, u32[]{:S(2)}) %all-to-all-start.2) | async-done | bytes 1572896 | tf_op jit(solution)/shard_map/all_to_all | solution.py:42
  81.4 8.1 %all-to-all-start = ((bf16[16,24,16,256]{3,2,1,0:T(8,128)(2,1)}), bf16[16,24,16,256]{3,2,1,0:T(8,128)(2,1)}, u32[]{:S(2)}, u32[]{:S(2)}) async-start(bf16[16,24,16,256]{3,2,1,0:T(8,128)(2,1)} %copy_bitcast_fusion.1), calls=%async_computation | async-start | bytes 6291456 | tf_op jit(solution)/shard_map/all_to_all | solution.py:207
  89.5 6.3 %copy.61 = bf16[8,24,32,128]{2,3,1,0:T(8,128)(2,1)} copy(bf16[8,24,32,128]{3,2,1,0:T(8,128)(2,1)} %all-to-all-done.2) | data formatting | bytes 3145728 | tf_op jit(solution)/shard_map/all_to_all | solution.py:42
  95.8 12.7 %copy.62 = bf16[16,12,2,8,8,32]{5,4,3,2,1,0:T(8,128)(2,1)} copy(bf16[16,12,2,8,8,32]{5,3,0,2,1,4:T(8,128)(2,1)} %bitcast.95) | data formatting | bytes 3145728 | tf_op jit(solution)/shard_map/transpose | solution.py:206
  108.5 8.4 %reshape.73 = bf16[16,12,16,256]{3,2,1,0:T(8,128)(2,1)} reshape(bf16[16,12,2,8,8,32]{5,4,3,2,1,0:T(8,128)(2,1)} %copy.62) | data formatting | bytes 3145728 | tf_op jit(solution)/shard_map/reshape | solution.py:206
  116.9 19.6 %all-to-all-done.spec_in = bf16[16,24,16,256]{3,2,1,0:T(8,128)(2,1)} async-done(((bf16[16,24,16,256]{3,2,1,0:T(8,128)(2,1)}), bf16[16,24,16,256]{3,2,1,0:T(8,128)(2,1)}, u32[]{:S(2)}, u32[]{:S(2)}) %all-to-all-start) | async-done | bytes 3145760 | tf_op jit(solution)/shard_map/all_to_all | solution.py:207
  136.5 4.6 %all-to-all-start.3 = ((bf16[16,12,16,256]{3,2,1,0:T(8,128)(2,1)}), bf16[16,12,16,256]{3,2,1,0:T(8,128)(2,1)}, u32[]{:S(2)}, u32[]{:S(2)}) async-start(bf16[16,12,16,256]{3,2,1,0:T(8,128)(2,1)} %reshape.73), calls=%async_computation.3 | async-start | bytes 3145728 | tf_op jit(solution)/shard_map/all_to_all | solution.py:208
  141.2 3.0 copy.70
  144.2 2.6 copy.72
  146.8 16.7 %all-to-all-done.3.var_in = bf16[16,12,16,256]{3,2,1,0:T(8,128)(2,1)} async-done(((bf16[16,12,16,256]{3,2,1,0:T(8,128)(2,1)}), bf16[16,12,16,256]{3,2,1,0:T(8,128)(2,1)}, u32[]{:S(2)}, u32[]{:S(2)}) %all-to-all-start.3) | async-done | bytes 1572896 | tf_op jit(solution)/shard_map/all_to_all | solution.py:208
  163.4 107.1 %shard_map.95 = (f32[24,8,128]{2,1,0:T(8,128)}, f32[24,8,128]{2,1,0:T(8,128)}) custom-call(bf16[16,24,16,256]{3,2,1,0:T(8,128)(2,1)} %all-to-all-done.spec_in, bf16[16,12,16,256]{3,2,1,0:T(8,128)(2,1)} %all-to-all-done.3.var_in), custom_call_target="tpu_custom_call" | custom-call | tf_op jit(solution)/shard_map/pallas_call | solution.py:127
  272.3 11.9 %shard_map.96 = f32[16,72,128]{2,1,0:T(8,128)} custom-call(f32[72,128]{1,0:T(8,128)} %reshape.74.x_ref), custom_call_target="tpu_custom_call" | custom-call | tf_op jit(solution)/shard_map/pallas_call | solution.py:180
  284.2 4.1 %reshape.75 = f32[16,2,24,8,24]{4,3,2,1,0:T(8,128)} reshape(f32[16,72,128]{2,1,0:T(8,128)} %shard_map.96) | data formatting | bytes 1179648 | tf_op jit(solution)/shard_map/reshape | solution.py:214
  288.3 2.3 copy.88
  290.6 1.9 slice_bitcast_fusion
  293.7 1.8 copy.64
  295.6 2.6 copy.66
  298.2 2.6 copy.65
  300.7 2.2 maximum_maximum_fusion
  302.9 3.2 %copy.68 = f32[48,128,48]{2,0,1:T(8,128)} copy(f32[48,128,48]{1,2,0:T(8,128)} %maximum_maximum_fusion) | data formatting | bytes 2359296 | tf_op jit(solution)/shard_map/concatenate | solution.py:219
  306.1 6.5 %fusion.9 = f32[128,48,256]{2,1,0:T(8,128)S(1)} fusion(f32[48,128,48]{2,0,1:T(8,128)} %copy.68, bf16[48,128,256]{2,1,0:T(8,128)(2,1)S(1)} %bitcast.93), kind=kOutput, calls=%fused_computation.13 | convolution fusion | flops 905969664 | bytes 10616832 | tf_op jit(solution)/shard_map/jfa,aft->jft/dot_general | solution.py:221
  312.6 6.3 %copy.71 = f32[2,24,128,256]{3,2,1,0:T(8,128)} copy(f32[2,24,128,256]{3,1,0,2:T(8,128)S(1)} %bitcast.94) | data formatting | bytes 12582912
  (25 shorter events, 5.1 us)
Async XLA Ops:
  0.6 40.1 %copy-start = (bf16[1024,1024]{1,0:T(8,128)(2,1)S(1)}, bf16[1024,1024]{1,0:T(8,128)(2,1)}, u32[]{:S(2)}) copy-start(bf16[1024,1024]{1,0:T(8,128)(2,1)} %param.12) | copy-start | bytes 6291460
  13.0 27.8 %copy-start.4 = (f32[1024]{0:T(1024)S(1)}, f32[1024]{0:T(1024)}, u32[]{:S(2)}) copy-start(f32[1024]{0:T(1024)} %param.11) | copy-start | bytes 12292
  13.0 27.8 %copy-start.5 = (f32[1024]{0:T(1024)S(1)}, f32[1024]{0:T(1024)}, u32[]{:S(2)}) copy-start(f32[1024]{0:T(1024)} %param.9) | copy-start | bytes 12292
  39.0 1.1 copy-start.3
  40.7 7.3 %copy-start.6 = (f32[1024]{0:T(1024)S(1)}, f32[1024]{0:T(1024)}, u32[]{:S(2)}) copy-start(f32[1024]{0:T(1024)} %param.15) | copy-start | bytes 12292
  40.7 7.2 %copy-start.7 = (f32[1024]{0:T(1024)S(1)}, f32[1024]{0:T(1024)}, u32[]{:S(2)}) copy-start(f32[1024]{0:T(1024)} %param.13) | copy-start | bytes 12292
  53.9 5.9 %copy-start.2 = (bf16[2,24,128,256]{3,2,1,0:T(8,128)(2,1)S(1)}, bf16[2,24,128,256]{3,2,1,0:T(8,128)(2,1)}, u32[]{:S(2)}) copy-start(bf16[2,24,128,256]{3,2,1,0:T(8,128)(2,1)} %param.8) | copy-start | bytes 9437188
  55.4 26.0 %all-to-all-start.2 = ((bf16[8,24,32,128]{3,2,1,0:T(8,128)(2,1)}), bf16[8,24,32,128]{3,2,1,0:T(8,128)(2,1)}, u32[]{:S(2)}, u32[]{:S(2)}) async-start(bf16[8,24,32,128]{3,2,1,0:T(8,128)(2,1)} %bitcast.98), calls=%async_computation.2 | async-start | bytes 3145728 | tf_op jit(solution)/shard_map/all_to_all | solution.py:42
  81.4 55.1 %all-to-all-start = ((bf16[16,24,16,256]{3,2,1,0:T(8,128)(2,1)}), bf16[16,24,16,256]{3,2,1,0:T(8,128)(2,1)}, u32[]{:S(2)}, u32[]{:S(2)}) async-start(bf16[16,24,16,256]{3,2,1,0:T(8,128)(2,1)} %copy_bitcast_fusion.1), calls=%async_computation | async-start | bytes 6291456 | tf_op jit(solution)/shard_map/all_to_all | solution.py:207
  136.5 26.9 %all-to-all-start.3 = ((bf16[16,12,16,256]{3,2,1,0:T(8,128)(2,1)}), bf16[16,12,16,256]{3,2,1,0:T(8,128)(2,1)}, u32[]{:S(2)}, u32[]{:S(2)}) async-start(bf16[16,12,16,256]{3,2,1,0:T(8,128)(2,1)} %reshape.73), calls=%async_computation.3 | async-start | bytes 3145728 | tf_op jit(solution)/shard_map/all_to_all | solution.py:208
  312.6 6.4 %copy-start.1 = (bf16[1024,1024]{1,0:T(8,128)(2,1)S(1)}, bf16[1024,1024]{1,0:T(8,128)(2,1)}, u32[]{:S(2)}) copy-start(bf16[1024,1024]{1,0:T(8,128)(2,1)} %param.12) | copy-start | bytes 6291460

commit v10 on v8

--- a/solution.py
+++ b/solution.py
@@ -218,7 +218,7 @@
     mix = jnp.concatenate([top, bottom], axis=0)
     stacked = spectra.reshape(2 * count, spectra.shape[2], spectra.shape[3]).astype(jnp.float32)
     demixed = jnp.einsum(
-        "jfa,aft->jft", mix, stacked, precision=lax.Precision.HIGHEST,
+        "jfa,aft->jft", mix, stacked, precision=lax.Precision.HIGH,
         preferred_element_type=jnp.float32,
     )
     return (demixed.reshape(spectra.shape), variances)

time: 321 us -> 320 us (level)
  no operation moved by 1% of the time
where the time goes in v10:
time: 320 us; the launch traced here: 318 us
  Pallas kernels  119 us (37%)
  waiting for transfers between devices  65.6 us (20%)
  local copies, waits for them, and re-layouts  63.6 us (20%)
  blocking collectives  26 us (8%)
  matrix products  18.4 us (6%)
  starting transfers between devices  17.1 us (5%)
  other arithmetic  7.21 us (2%)
    pallas_call x1, Pallas kernels, sweep(): pl.pallas_call(functools.partial(sweep_kernel, frames), out_shape=(jax.Sh...  107 us
    all_to_all x1, waiting for transfers between devices, on_device(): lax.all_to_all(spec_send, 'frame', split_axis=0, concat_axis=0, tiled=True)  29.3 us
    all_to_all x1, blocking collectives, source_model(): lax.all_to_all(send, 'freq', split_axis=0, concat_axis=0, tiled=True)  26 us
    all_to_all x1, waiting for transfers between devices, source_model(): lax.all_to_all(send, 'freq', split_axis=0, concat_axis=0, tiled=True)  19.6 us
    all_to_all x1, waiting for transfers between devices, on_device(): lax.all_to_all(var_send, 'frame', split_axis=0, concat_axis=0, tiled=True)  16.7 us
    unnamed x20, local copies, waits for them, and re-layouts  15 us
    pallas_call x1, Pallas kernels, frame_gather(): pl.pallas_call(gather_kernel, out_shape=jax.ShapeDtypeStruct((n,) + x.sha...  11.9 us
    another operation x1, local copies, waits for them, and re-layouts, on_device(): variances.reshape(count // 2, 2, peers, bins, span).transpose(2, 0, 1, 3, 4)  8.41 us
  transfers between devices with their start and end apart: 3, of which 3 were waited for; matrix products, arithmetic and copies ran while one was open for 8% of the time, Pallas kernels for 0%

profile of v10, /device:TPU:0, one launch (start us, length us, event | category | flops | bytes accessed | tf_op | source)
XLA Modules:
  0.0 317.8 jit_solution(9630666327041405978)
XLA Ops:
  0.6 4.0 %fusion.37 = (bf16[1,24,128,256]{3,2,1,0:T(8,128)(2,1)}, bf16[1,24,128,256]{3,2,1,0:T(8,128)(2,1)}) fusion(bf16[2,24,128,256]{3,2,1,0:T(8,128)(2,1)} %param.8), kind=kLoop, calls=%fused_computation.45 | loop fusion | bytes 6291456 | tf_op jit(solution)/shard_map/slice | solution.py:16
  4.7 2.6 copy.74
  7.3 2.6 copy.75
  9.9 2.8 log_convert_fusion
  13.0 26.0 %all_to_all.20 = bf16[8,24,32,128]{3,2,1,0:T(8,128)(2,1)S(1)} all-to-all(bf16[8,24,32,128]{3,2,1,0:T(8,128)(2,1)S(1)} %copy.58), channel_id=1, replica_groups=mesh['freq'=8,'frame'=16] {'freq'}, dimensions={0} | all-to-all | bytes 3145728 | tf_op jit(solution)/shard_map/all_to_all | solution.py:25
  40.8 7.2 %fusion.13 = f32[24,32,1024]{2,1,0:T(8,128)} fusion(bf16[1024,1024]{1,0:T(8,128)(2,1)S(1)} %copy-done, f32[1024]{0:T(1024)S(1)} %copy-done.4, bf16[1024,1024]{1,0:T(8,128)(2,1)} %param.10, f32[1024]{0:T(1024)S(1)} %copy-done.5, f32[24,32]{1,0:T(8,128)S(1)} %add_rsqrt_fusion, f32[24,32]{1,0:T(8,128)S(1)} %broadcast_multiply_fusion, ...), kind=kOutput, calls=%fused_computation.22 | convolution fusion | flops 3229876224 | bytes 8927232 | tf_op jit(solution)/shard_map/nth,hg->ntg/dot_general | solution.py:35
  48.0 5.9 %fusion.23 = bf16[24,4,8,8,128]{4,3,2,1,0:T(8,128)(2,1)S(1)} fusion(f32[1024]{0:T(1024)S(1)} %copy-done.6, bf16[1024,1024]{1,0:T(8,128)(2,1)} %param.14, f32[24,32,1024]{2,1,0:T(8,128)} %fusion.13, f32[1024]{0:T(1024)S(1)} %copy-done.7), kind=kOutput, calls=%fused_computation.35 | convolution fusion | flops 1622409216 | bytes 6823936 | tf_op jit(solution)/shard_map/nth,hf->ntf/dot_general | solution.py:38
  53.9 1.4 copy.91
  55.4 4.4 %all-to-all-start.2 = ((bf16[8,24,32,128]{3,2,1,0:T(8,128)(2,1)}), bf16[8,24,32,128]{3,2,1,0:T(8,128)(2,1)}, u32[]{:S(2)}, u32[]{:S(2)}) async-start(bf16[8,24,32,128]{3,2,1,0:T(8,128)(2,1)} %bitcast.100), calls=%async_computation.2 | async-start | bytes 3145728 | tf_op jit(solution)/shard_map/all_to_all | solution.py:42
  59.8 2.0 copy_bitcast_fusion.1
  61.8 19.6 %all-to-all-done.2 = bf16[8,24,32,128]{3,2,1,0:T(8,128)(2,1)} async-done(((bf16[8,24,32,128]{3,2,1,0:T(8,128)(2,1)}), bf16[8,24,32,128]{3,2,1,0:T(8,128)(2,1)}, u32[]{:S(2)}, u32[]{:S(2)}) %all-to-all-start.2) | async-done | bytes 1572896 | tf_op jit(solution)/shard_map/all_to_all | solution.py:42
  81.4 8.1 %all-to-all-start = ((bf16[16,24,16,256]{3,2,1,0:T(8,128)(2,1)}), bf16[16,24,16,256]{3,2,1,0:T(8,128)(2,1)}, u32[]{:S(2)}, u32[]{:S(2)}) async-start(bf16[16,24,16,256]{3,2,1,0:T(8,128)(2,1)} %copy_bitcast_fusion.1), calls=%async_computation | async-start | bytes 6291456 | tf_op jit(solution)/shard_map/all_to_all | solution.py:206
  89.5 6.6 %copy.62 = bf16[24,128,8,32]{3,2,1,0:T(8,128)(2,1)} copy(bf16[24,128,8,32]{1,3,0,2:T(8,128)(2,1)} %bitcast.13) | data formatting | bytes 3145728 | tf_op jit(solution)/shard_map/transpose | solution.py:43
  96.1 8.4 %reshape_reshape.3 = bf16[12,2,16,8,256]{4,3,2,1,0:T(8,128)(2,1)} reshape(bf16[24,128,8,32]{3,2,1,0:T(8,128)(2,1)} %copy.62) | data formatting | bytes 3145728 | tf_op jit(solution)/shard_map/reshape;reshape | solution.py:204
  104.5 2.7 copy_bitcast_fusion.2
  107.2 29.3 %all-to-all-done.spec_in = bf16[16,24,16,256]{3,2,1,0:T(8,128)(2,1)} async-done(((bf16[16,24,16,256]{3,2,1,0:T(8,128)(2,1)}), bf16[16,24,16,256]{3,2,1,0:T(8,128)(2,1)}, u32[]{:S(2)}, u32[]{:S(2)}) %all-to-all-start) | async-done | bytes 3145760 | tf_op jit(solution)/shard_map/all_to_all | solution.py:206
  136.5 4.6 %all-to-all-start.3 = ((bf16[16,12,16,256]{3,2,1,0:T(8,128)(2,1)}), bf16[16,12,16,256]{3,2,1,0:T(8,128)(2,1)}, u32[]{:S(2)}, u32[]{:S(2)}) async-start(bf16[16,12,16,256]{3,2,1,0:T(8,128)(2,1)} %copy_bitcast_fusion.2), calls=%async_computation.3 | async-start | bytes 3145728 | tf_op jit(solution)/shard_map/all_to_all | solution.py:207
  141.1 3.0 copy.61
  144.2 2.6 copy.72
  146.7 16.7 %all-to-all-done.3.var_in = bf16[16,12,16,256]{3,2,1,0:T(8,128)(2,1)} async-done(((bf16[16,12,16,256]{3,2,1,0:T(8,128)(2,1)}), bf16[16,12,16,256]{3,2,1,0:T(8,128)(2,1)}, u32[]{:S(2)}, u32[]{:S(2)}) %all-to-all-start.3) | async-done | bytes 1572896 | tf_op jit(solution)/shard_map/all_to_all | solution.py:207
  163.4 107.1 %shard_map.95 = (f32[24,8,128]{2,1,0:T(8,128)}, f32[24,8,128]{2,1,0:T(8,128)}) custom-call(bf16[16,24,16,256]{3,2,1,0:T(8,128)(2,1)} %all-to-all-done.spec_in, bf16[16,12,16,256]{3,2,1,0:T(8,128)(2,1)} %all-to-all-done.3.var_in), custom_call_target="tpu_custom_call" | custom-call | tf_op jit(solution)/shard_map/pallas_call | solution.py:127
  272.3 11.9 %shard_map.96 = f32[16,72,128]{2,1,0:T(8,128)} custom-call(f32[72,128]{1,0:T(8,128)} %reshape.70.x_ref), custom_call_target="tpu_custom_call" | custom-call | tf_op jit(solution)/shard_map/pallas_call | solution.py:180
  284.2 4.1 %reshape.71 = f32[16,2,24,8,24]{4,3,2,1,0:T(8,128)} reshape(f32[16,72,128]{2,1,0:T(8,128)} %shard_map.96) | data formatting | bytes 1179648 | tf_op jit(solution)/shard_map/reshape | solution.py:213
  288.3 2.3 copy.90
  291.8 1.9 slice_bitcast_fusion
  293.7 1.8 copy.66
  295.6 2.6 copy.67
  298.1 2.6 copy.65
  300.7 2.3 maximum_maximum_fusion
  303.0 3.2 %copy.69 = f32[48,128,48]{2,0,1:T(8,128)} copy(f32[48,128,48]{1,2,0:T(8,128)} %maximum_maximum_fusion) | data formatting | bytes 2359296 | tf_op jit(solution)/shard_map/concatenate | solution.py:218
  306.2 5.3 %fusion.9 = f32[128,48,256]{2,1,0:T(8,128)S(1)} fusion(f32[48,128,48]{2,0,1:T(8,128)} %copy.69, bf16[48,128,256]{2,1,0:T(8,128)(2,1)S(1)} %bitcast.96), kind=kOutput, calls=%fused_computation.13 | convolution fusion | flops 452984832 | bytes 10616832 | tf_op jit(solution)/shard_map/jfa,aft->jft/dot_general | solution.py:220
  311.4 6.3 %copy.71 = f32[2,24,128,256]{3,2,1,0:T(8,128)} copy(f32[2,24,128,256]{3,1,0,2:T(8,128)S(1)} %bitcast.97) | data formatting | bytes 12582912
  (25 shorter events, 5.0 us)
Async XLA Ops:
  0.6 40.1 %copy-start = (bf16[1024,1024]{1,0:T(8,128)(2,1)S(1)}, bf16[1024,1024]{1,0:T(8,128)(2,1)}, u32[]{:S(2)}) copy-start(bf16[1024,1024]{1,0:T(8,128)(2,1)} %param.12) | copy-start | bytes 6291460
  13.0 27.8 %copy-start.4 = (f32[1024]{0:T(1024)S(1)}, f32[1024]{0:T(1024)}, u32[]{:S(2)}) copy-start(f32[1024]{0:T(1024)} %param.11) | copy-start | bytes 12292
  13.0 27.8 %copy-start.5 = (f32[1024]{0:T(1024)S(1)}, f32[1024]{0:T(1024)}, u32[]{:S(2)}) copy-start(f32[1024]{0:T(1024)} %param.9) | copy-start | bytes 12292
  39.0 1.1 copy-start.3
  40.7 7.3 %copy-start.6 = (f32[1024]{0:T(1024)S(1)}, f32[1024]{0:T(1024)}, u32[]{:S(2)}) copy-start(f32[1024]{0:T(1024)} %param.15) | copy-start | bytes 12292
  40.7 7.2 %copy-start.7 = (f32[1024]{0:T(1024)S(1)}, f32[1024]{0:T(1024)}, u32[]{:S(2)}) copy-start(f32[1024]{0:T(1024)} %param.13) | copy-start | bytes 12292
  53.9 5.9 %copy-start.2 = (bf16[2,24,128,256]{3,2,1,0:T(8,128)(2,1)S(1)}, bf16[2,24,128,256]{3,2,1,0:T(8,128)(2,1)}, u32[]{:S(2)}) copy-start(bf16[2,24,128,256]{3,2,1,0:T(8,128)(2,1)} %param.8) | copy-start | bytes 9437188
  55.4 26.0 %all-to-all-start.2 = ((bf16[8,24,32,128]{3,2,1,0:T(8,128)(2,1)}), bf16[8,24,32,128]{3,2,1,0:T(8,128)(2,1)}, u32[]{:S(2)}, u32[]{:S(2)}) async-start(bf16[8,24,32,128]{3,2,1,0:T(8,128)(2,1)} %bitcast.100), calls=%async_computation.2 | async-start | bytes 3145728 | tf_op jit(solution)/shard_map/all_to_all | solution.py:42
  81.4 55.1 %all-to-all-start = ((bf16[16,24,16,256]{3,2,1,0:T(8,128)(2,1)}), bf16[16,24,16,256]{3,2,1,0:T(8,128)(2,1)}, u32[]{:S(2)}, u32[]{:S(2)}) async-start(bf16[16,24,16,256]{3,2,1,0:T(8,128)(2,1)} %copy_bitcast_fusion.1), calls=%async_computation | async-start | bytes 6291456 | tf_op jit(solution)/shard_map/all_to_all | solution.py:206
  136.5 26.9 %all-to-all-start.3 = ((bf16[16,12,16,256]{3,2,1,0:T(8,128)(2,1)}), bf16[16,12,16,256]{3,2,1,0:T(8,128)(2,1)}, u32[]{:S(2)}, u32[]{:S(2)}) async-start(bf16[16,12,16,256]{3,2,1,0:T(8,128)(2,1)} %copy_bitcast_fusion.2), calls=%async_computation.3 | async-start | bytes 3145728 | tf_op jit(solution)/shard_map/all_to_all | solution.py:207
  311.4 6.4 %copy-start.1 = (bf16[1024,1024]{1,0:T(8,128)(2,1)S(1)}, bf16[1024,1024]{1,0:T(8,128)(2,1)}, u32[]{:S(2)}) copy-start(bf16[1024,1024]{1,0:T(8,128)(2,1)} %param.12) | copy-start | bytes 6291460

commit v11 on v10

--- a/solution.py
+++ b/solution.py
@@ -46,7 +46,7 @@
 def sweep_kernel(frames, spec_in, var_in, mr_ref, mi_ref, yr, yi, w, pr, pi, pp):
     count, bins, length = yr.shape
     peers, _, _, span = spec_in.shape
-    chunk = 512
+    chunk = 256
     chunks = length // chunk
 
     def init(s, carry):
@@ -83,37 +83,43 @@
         mkr = mr_ref[k]
         mki = mi_ref[k]
 
-        def per_source(j, carry):
-            acc_r = jnp.zeros((bins, chunk), jnp.float32)
-            acc_i = jnp.zeros((bins, chunk), jnp.float32)
-            acc_d = jnp.zeros((bins, chunk), jnp.float32)
-            for c in range(chunks):
-                sl = pl.ds(c * chunk, chunk)
-                a_r = yr[j, :, sl]
-                a_i = yi[j, :, sl]
-                ww = w[j, :, sl]
-                b_r = pr[:, sl]
-                b_i = pi[:, sl]
-                acc_r = acc_r + ww * (a_r * b_r + a_i * b_i)
-                acc_i = acc_i + ww * (a_i * b_r - a_r * b_i)
-                acc_d = acc_d + ww * pp[:, sl]
-            numer_real = jnp.sum(acc_r, axis=1, keepdims=True) / frames
-            numer_imag = jnp.sum(acc_i, axis=1, keepdims=True) / frames
-            denom = jnp.sum(acc_d, axis=1, keepdims=True) / frames
-            is_self = j == k
-            coef_real = jnp.where(is_self, 1.0 - lax.rsqrt(denom), numer_real / denom)
-            coef_imag = jnp.where(is_self, 0.0, numer_imag / denom)
+        def per_pair(p, carry):
+            sources = tuple(4 * p + h for h in range(4))
+            acc = [[jnp.zeros((bins, chunk), jnp.float32) for _ in range(3)] for _ in sources]
             for c in range(chunks):
                 sl = pl.ds(c * chunk, chunk)
                 b_r = pr[:, sl]
                 b_i = pi[:, sl]
-                yr[j, :, sl] = yr[j, :, sl] - (coef_real * b_r - coef_imag * b_i)
-                yi[j, :, sl] = yi[j, :, sl] - (coef_real * b_i + coef_imag * b_r)
-            mr_ref[j] = mr_ref[j] - (coef_real * mkr - coef_imag * mki)
-            mi_ref[j] = mi_ref[j] - (coef_real * mki + coef_imag * mkr)
+                b_p = pp[:, sl]
+                for h, j in enumerate(sources):
+                    a_r = yr[j, :, sl]
+                    a_i = yi[j, :, sl]
+                    ww = w[j, :, sl]
+                    acc[h][0] = acc[h][0] + ww * (a_r * b_r + a_i * b_i)
+                    acc[h][1] = acc[h][1] + ww * (a_i * b_r - a_r * b_i)
+                    acc[h][2] = acc[h][2] + ww * b_p
+            coefs = []
+            for h, j in enumerate(sources):
+                numer_real = jnp.sum(acc[h][0], axis=1, keepdims=True) / frames
+                numer_imag = jnp.sum(acc[h][1], axis=1, keepdims=True) / frames
+                denom = jnp.sum(acc[h][2], axis=1, keepdims=True) / frames
+                is_self = j == k
+                coef_real = jnp.where(is_self, 1.0 - lax.rsqrt(denom), numer_real / denom)
+                coef_imag = jnp.where(is_self, 0.0, numer_imag / denom)
+                coefs.append((coef_real, coef_imag))
+            for c in range(chunks):
+                sl = pl.ds(c * chunk, chunk)
+                b_r = pr[:, sl]
+                b_i = pi[:, sl]
+                for j, (coef_real, coef_imag) in zip(sources, coefs):
+                    yr[j, :, sl] = yr[j, :, sl] - (coef_real * b_r - coef_imag * b_i)
+                    yi[j, :, sl] = yi[j, :, sl] - (coef_real * b_i + coef_imag * b_r)
+            for j, (coef_real, coef_imag) in zip(sources, coefs):
+                mr_ref[j] = mr_ref[j] - (coef_real * mkr - coef_imag * mki)
+                mi_ref[j] = mi_ref[j] - (coef_real * mki + coef_imag * mkr)
             return carry
 
-        lax.fori_loop(0, count, per_source, 0)
+        lax.fori_loop(0, count // 4, per_pair, 0)
         return carry
 
     lax.fori_loop(0, count, step, 0)

time: 320 us -> 276 us (0.86)
  Pallas kernels: 119 us -> 75.4 us
    pallas_call x1, Pallas kernels: 107 us -> 63.5 us  [sweep(): pl.pallas_call(functools.partial(sweep_kernel, frames), out_shape=(jax.Sh...]
  transfers between devices with their start and end apart: 3 -> 3, of which waited for: 3 -> 3; matrix products, arithmetic and copies ran while one was open for 8% -> 9% of each run, Pallas kernels for 0% -> 0%
where the time goes in v11:
time: 276 us; the launch traced here: 274 us
  Pallas kernels  75.4 us (27%)
  waiting for transfers between devices  65.6 us (24%)
  local copies, waits for them, and re-layouts  63.6 us (23%)
  blocking collectives  26 us (9%)
  matrix products  18.4 us (7%)
  starting transfers between devices  17.1 us (6%)
  other arithmetic  7.21 us (3%)
    pallas_call x1, Pallas kernels, sweep(): pl.pallas_call(functools.partial(sweep_kernel, frames), out_shape=(jax.Sh...  63.5 us
    all_to_all x1, waiting for transfers between devices, on_device(): lax.all_to_all(spec_send, 'frame', split_axis=0, concat_axis=0, tiled=True)  29.3 us
    all_to_all x1, blocking collectives, source_model(): lax.all_to_all(send, 'freq', split_axis=0, concat_axis=0, tiled=True)  26 us
    all_to_all x1, waiting for transfers between devices, source_model(): lax.all_to_all(send, 'freq', split_axis=0, concat_axis=0, tiled=True)  19.6 us
    all_to_all x1, waiting for transfers between devices, on_device(): lax.all_to_all(var_send, 'frame', split_axis=0, concat_axis=0, tiled=True)  16.7 us
    unnamed x20, local copies, waits for them, and re-layouts  15 us
    pallas_call x1, Pallas kernels, frame_gather(): pl.pallas_call(gather_kernel, out_shape=jax.ShapeDtypeStruct((n,) + x.sha...  11.9 us
    another operation x1, local copies, waits for them, and re-layouts, on_device(): variances.reshape(count // 2, 2, peers, bins, span).transpose(2, 0, 1, 3, 4)  8.41 us
  transfers between devices with their start and end apart: 3, of which 3 were waited for; matrix products, arithmetic and copies ran while one was open for 9% of the time, Pallas kernels for 0%

profile of v11, /device:TPU:0, one launch (start us, length us, event | category | flops | bytes accessed | tf_op | source)
XLA Modules:
  0.0 274.2 jit_solution(14336349443475090156)
XLA Ops:
  0.6 4.0 %fusion.37 = (bf16[1,24,128,256]{3,2,1,0:T(8,128)(2,1)}, bf16[1,24,128,256]{3,2,1,0:T(8,128)(2,1)}) fusion(bf16[2,24,128,256]{3,2,1,0:T(8,128)(2,1)} %param.8), kind=kLoop, calls=%fused_computation.45 | loop fusion | bytes 6291456 | tf_op jit(solution)/shard_map/slice | solution.py:16
  4.7 2.6 copy.74
  7.3 2.6 copy.75
  9.9 2.8 %log_convert_fusion = bf16[1,24,128,256]{2,3,1,0:T(8,128)(2,1)S(1)} fusion(bf16[1,24,128,256]{2,3,1,0:T(8,128)(2,1)} %copy.75, bf16[1,24,128,256]{2,3,1,0:T(8,128)(2,1)} %copy.74), kind=kLoop, calls=%fused_computation.17 | loop fusion | flops 5505024 | bytes 4718592 | tf_op jit(solution)/shard_map/convert_element_type | solution.py:18
  13.0 26.0 %all_to_all.20 = bf16[8,24,32,128]{3,2,1,0:T(8,128)(2,1)S(1)} all-to-all(bf16[8,24,32,128]{3,2,1,0:T(8,128)(2,1)S(1)} %copy.58), channel_id=1, replica_groups=mesh['freq'=8,'frame'=16] {'freq'}, dimensions={0} | all-to-all | bytes 3145728 | tf_op jit(solution)/shard_map/all_to_all | solution.py:25
  40.8 7.2 %fusion.13 = f32[24,32,1024]{2,1,0:T(8,128)} fusion(bf16[1024,1024]{1,0:T(8,128)(2,1)S(1)} %copy-done, f32[1024]{0:T(1024)S(1)} %copy-done.4, bf16[1024,1024]{1,0:T(8,128)(2,1)} %param.10, f32[1024]{0:T(1024)S(1)} %copy-done.5, f32[24,32]{1,0:T(8,128)S(1)} %add_rsqrt_fusion, f32[24,32]{1,0:T(8,128)S(1)} %broadcast_multiply_fusion, ...), kind=kOutput, calls=%fused_computation.22 | convolution fusion | flops 3229876224 | bytes 8927232 | tf_op jit(solution)/shard_map/nth,hg->ntg/dot_general | solution.py:35
  48.0 5.9 %fusion.23 = bf16[24,4,8,8,128]{4,3,2,1,0:T(8,128)(2,1)S(1)} fusion(f32[1024]{0:T(1024)S(1)} %copy-done.6, bf16[1024,1024]{1,0:T(8,128)(2,1)} %param.14, f32[24,32,1024]{2,1,0:T(8,128)} %fusion.13, f32[1024]{0:T(1024)S(1)} %copy-done.7), kind=kOutput, calls=%fused_computation.35 | convolution fusion | flops 1622409216 | bytes 6823936 | tf_op jit(solution)/shard_map/nth,hf->ntf/dot_general | solution.py:38
  53.9 1.4 copy.91
  55.4 4.4 %all-to-all-start.2 = ((bf16[8,24,32,128]{3,2,1,0:T(8,128)(2,1)}), bf16[8,24,32,128]{3,2,1,0:T(8,128)(2,1)}, u32[]{:S(2)}, u32[]{:S(2)}) async-start(bf16[8,24,32,128]{3,2,1,0:T(8,128)(2,1)} %bitcast.100), calls=%async_computation.2 | async-start | bytes 3145728 | tf_op jit(solution)/shard_map/all_to_all | solution.py:42
  59.8 2.0 copy_bitcast_fusion.1
  61.8 19.6 %all-to-all-done.2 = bf16[8,24,32,128]{3,2,1,0:T(8,128)(2,1)} async-done(((bf16[8,24,32,128]{3,2,1,0:T(8,128)(2,1)}), bf16[8,24,32,128]{3,2,1,0:T(8,128)(2,1)}, u32[]{:S(2)}, u32[]{:S(2)}) %all-to-all-start.2) | async-done | bytes 1572896 | tf_op jit(solution)/shard_map/all_to_all | solution.py:42
  81.4 8.1 %all-to-all-start = ((bf16[16,24,16,256]{3,2,1,0:T(8,128)(2,1)}), bf16[16,24,16,256]{3,2,1,0:T(8,128)(2,1)}, u32[]{:S(2)}, u32[]{:S(2)}) async-start(bf16[16,24,16,256]{3,2,1,0:T(8,128)(2,1)} %copy_bitcast_fusion.1), calls=%async_computation | async-start | bytes 6291456 | tf_op jit(solution)/shard_map/all_to_all | solution.py:212
  89.5 6.6 %copy.62 = bf16[24,128,8,32]{3,2,1,0:T(8,128)(2,1)} copy(bf16[24,128,8,32]{1,3,0,2:T(8,128)(2,1)} %bitcast.13) | data formatting | bytes 3145728 | tf_op jit(solution)/shard_map/transpose | solution.py:43
  96.1 8.4 %reshape_reshape.3 = bf16[12,2,16,8,256]{4,3,2,1,0:T(8,128)(2,1)} reshape(bf16[24,128,8,32]{3,2,1,0:T(8,128)(2,1)} %copy.62) | data formatting | bytes 3145728 | tf_op jit(solution)/shard_map/reshape;reshape | solution.py:210
  104.5 2.7 copy_bitcast_fusion.2
  107.2 29.3 %all-to-all-done.spec_in = bf16[16,24,16,256]{3,2,1,0:T(8,128)(2,1)} async-done(((bf16[16,24,16,256]{3,2,1,0:T(8,128)(2,1)}), bf16[16,24,16,256]{3,2,1,0:T(8,128)(2,1)}, u32[]{:S(2)}, u32[]{:S(2)}) %all-to-all-start) | async-done | bytes 3145760 | tf_op jit(solution)/shard_map/all_to_all | solution.py:212
  136.5 4.6 %all-to-all-start.3 = ((bf16[16,12,16,256]{3,2,1,0:T(8,128)(2,1)}), bf16[16,12,16,256]{3,2,1,0:T(8,128)(2,1)}, u32[]{:S(2)}, u32[]{:S(2)}) async-start(bf16[16,12,16,256]{3,2,1,0:T(8,128)(2,1)} %copy_bitcast_fusion.2), calls=%async_computation.3 | async-start | bytes 3145728 | tf_op jit(solution)/shard_map/all_to_all | solution.py:213
  141.1 3.0 %copy.61 = bf16[8,24,32,128]{3,2,0,1:T(8,128)(2,1)} copy(bf16[8,24,32,128]{3,2,1,0:T(8,128)(2,1)} %all-to-all-done.2) | data formatting | bytes 3145728 | tf_op jit(solution)/shard_map/all_to_all | solution.py:42
  144.2 2.6 copy.72
  146.7 16.7 %all-to-all-done.3.var_in = bf16[16,12,16,256]{3,2,1,0:T(8,128)(2,1)} async-done(((bf16[16,12,16,256]{3,2,1,0:T(8,128)(2,1)}), bf16[16,12,16,256]{3,2,1,0:T(8,128)(2,1)}, u32[]{:S(2)}, u32[]{:S(2)}) %all-to-all-start.3) | async-done | bytes 1572896 | tf_op jit(solution)/shard_map/all_to_all | solution.py:213
  163.4 63.5 %shard_map.95 = (f32[24,8,128]{2,1,0:T(8,128)}, f32[24,8,128]{2,1,0:T(8,128)}) custom-call(bf16[16,24,16,256]{3,2,1,0:T(8,128)(2,1)} %all-to-all-done.spec_in, bf16[16,12,16,256]{3,2,1,0:T(8,128)(2,1)} %all-to-all-done.3.var_in), custom_call_target="tpu_custom_call" | custom-call | tf_op jit(solution)/shard_map/pallas_call | solution.py:133
  228.6 11.9 %shard_map.96 = f32[16,72,128]{2,1,0:T(8,128)} custom-call(f32[72,128]{1,0:T(8,128)} %reshape.70.x_ref), custom_call_target="tpu_custom_call" | custom-call | tf_op jit(solution)/shard_map/pallas_call | solution.py:186
  240.5 4.1 %reshape.71 = f32[16,2,24,8,24]{4,3,2,1,0:T(8,128)} reshape(f32[16,72,128]{2,1,0:T(8,128)} %shard_map.96) | data formatting | bytes 1179648 | tf_op jit(solution)/shard_map/reshape | solution.py:219
  244.6 2.3 copy.90
  248.2 1.9 slice_bitcast_fusion
  250.1 1.8 copy.66
  251.9 2.6 copy.67
  254.5 2.6 copy.65
  257.1 2.3 maximum_maximum_fusion
  259.3 3.2 %copy.69 = f32[48,128,48]{2,0,1:T(8,128)} copy(f32[48,128,48]{1,2,0:T(8,128)} %maximum_maximum_fusion) | data formatting | bytes 2359296 | tf_op jit(solution)/shard_map/concatenate | solution.py:224
  262.5 5.3 %fusion.9 = f32[128,48,256]{2,1,0:T(8,128)S(1)} fusion(f32[48,128,48]{2,0,1:T(8,128)} %copy.69, bf16[48,128,256]{2,1,0:T(8,128)(2,1)S(1)} %bitcast.96), kind=kOutput, calls=%fused_computation.13 | convolution fusion | flops 452984832 | bytes 10616832 | tf_op jit(solution)/shard_map/jfa,aft->jft/dot_general | solution.py:226
  267.8 6.3 %copy.71 = f32[2,24,128,256]{3,2,1,0:T(8,128)} copy(f32[2,24,128,256]{3,1,0,2:T(8,128)S(1)} %bitcast.97) | data formatting | bytes 12582912
  (25 shorter events, 5.0 us)
Async XLA Ops:
  0.6 40.1 %copy-start = (bf16[1024,1024]{1,0:T(8,128)(2,1)S(1)}, bf16[1024,1024]{1,0:T(8,128)(2,1)}, u32[]{:S(2)}) copy-start(bf16[1024,1024]{1,0:T(8,128)(2,1)} %param.12) | copy-start | bytes 6291460
  13.0 27.8 %copy-start.4 = (f32[1024]{0:T(1024)S(1)}, f32[1024]{0:T(1024)}, u32[]{:S(2)}) copy-start(f32[1024]{0:T(1024)} %param.11) | copy-start | bytes 12292
  13.0 27.8 %copy-start.5 = (f32[1024]{0:T(1024)S(1)}, f32[1024]{0:T(1024)}, u32[]{:S(2)}) copy-start(f32[1024]{0:T(1024)} %param.9) | copy-start | bytes 12292
  39.0 1.1 copy-start.3
  40.7 7.3 %copy-start.6 = (f32[1024]{0:T(1024)S(1)}, f32[1024]{0:T(1024)}, u32[]{:S(2)}) copy-start(f32[1024]{0:T(1024)} %param.15) | copy-start | bytes 12292
  40.7 7.2 %copy-start.7 = (f32[1024]{0:T(1024)S(1)}, f32[1024]{0:T(1024)}, u32[]{:S(2)}) copy-start(f32[1024]{0:T(1024)} %param.13) | copy-start | bytes 12292
  53.9 5.9 %copy-start.2 = (bf16[2,24,128,256]{3,2,1,0:T(8,128)(2,1)S(1)}, bf16[2,24,128,256]{3,2,1,0:T(8,128)(2,1)}, u32[]{:S(2)}) copy-start(bf16[2,24,128,256]{3,2,1,0:T(8,128)(2,1)} %param.8) | copy-start | bytes 9437188
  55.4 26.0 %all-to-all-start.2 = ((bf16[8,24,32,128]{3,2,1,0:T(8,128)(2,1)}), bf16[8,24,32,128]{3,2,1,0:T(8,128)(2,1)}, u32[]{:S(2)}, u32[]{:S(2)}) async-start(bf16[8,24,32,128]{3,2,1,0:T(8,128)(2,1)} %bitcast.100), calls=%async_computation.2 | async-start | bytes 3145728 | tf_op jit(solution)/shard_map/all_to_all | solution.py:42
  81.4 55.1 %all-to-all-start = ((bf16[16,24,16,256]{3,2,1,0:T(8,128)(2,1)}), bf16[16,24,16,256]{3,2,1,0:T(8,128)(2,1)}, u32[]{:S(2)}, u32[]{:S(2)}) async-start(bf16[16,24,16,256]{3,2,1,0:T(8,128)(2,1)} %copy_bitcast_fusion.1), calls=%async_computation | async-start | bytes 6291456 | tf_op jit(solution)/shard_map/all_to_all | solution.py:212
  136.5 26.9 %all-to-all-start.3 = ((bf16[16,12,16,256]{3,2,1,0:T(8,128)(2,1)}), bf16[16,12,16,256]{3,2,1,0:T(8,128)(2,1)}, u32[]{:S(2)}, u32[]{:S(2)}) async-start(bf16[16,12,16,256]{3,2,1,0:T(8,128)(2,1)} %copy_bitcast_fusion.2), calls=%async_computation.3 | async-start | bytes 3145728 | tf_op jit(solution)/shard_map/all_to_all | solution.py:213
  267.8 6.4 %copy-start.1 = (bf16[1024,1024]{1,0:T(8,128)(2,1)S(1)}, bf16[1024,1024]{1,0:T(8,128)(2,1)}, u32[]{:S(2)}) copy-start(bf16[1024,1024]{1,0:T(8,128)(2,1)} %param.12) | copy-start | bytes 6291460

commit v12 on v11

--- a/solution.py
+++ b/solution.py
@@ -84,7 +84,7 @@
         mki = mi_ref[k]
 
         def per_pair(p, carry):
-            sources = tuple(4 * p + h for h in range(4))
+            sources = tuple(6 * p + h for h in range(6))
             acc = [[jnp.zeros((bins, chunk), jnp.float32) for _ in range(3)] for _ in sources]
             for c in range(chunks):
                 sl = pl.ds(c * chunk, chunk)
@@ -119,7 +119,7 @@
                 mi_ref[j] = mi_ref[j] - (coef_real * mki + coef_imag * mkr)
             return carry
 
-        lax.fori_loop(0, count // 4, per_pair, 0)
+        lax.fori_loop(0, count // 6, per_pair, 0)
         return carry
 
     lax.fori_loop(0, count, step, 0)

time: 276 us -> 274 us (level)
  no operation moved by 1% of the time
where the time goes in v12:
time: 274 us; the launch traced here: 272 us
  Pallas kernels  73.4 us (27%)
  waiting for transfers between devices  65.6 us (24%)
  local copies, waits for them, and re-layouts  63.6 us (23%)
  blocking collectives  26 us (9%)
  matrix products  18.4 us (7%)
  starting transfers between devices  17.1 us (6%)
  other arithmetic  7.21 us (3%)
    pallas_call x1, Pallas kernels, sweep(): pl.pallas_call(functools.partial(sweep_kernel, frames), out_shape=(jax.Sh...  61.5 us
    all_to_all x1, waiting for transfers between devices, on_device(): lax.all_to_all(spec_send, 'frame', split_axis=0, concat_axis=0, tiled=True)  29.3 us
    all_to_all x1, blocking collectives, source_model(): lax.all_to_all(send, 'freq', split_axis=0, concat_axis=0, tiled=True)  26 us
    all_to_all x1, waiting for transfers between devices, source_model(): lax.all_to_all(send, 'freq', split_axis=0, concat_axis=0, tiled=True)  19.6 us
    all_to_all x1, waiting for transfers between devices, on_device(): lax.all_to_all(var_send, 'frame', split_axis=0, concat_axis=0, tiled=True)  16.7 us
    unnamed x20, local copies, waits for them, and re-layouts  15 us
    pallas_call x1, Pallas kernels, frame_gather(): pl.pallas_call(gather_kernel, out_shape=jax.ShapeDtypeStruct((n,) + x.sha...  11.9 us
    another operation x1, local copies, waits for them, and re-layouts, on_device(): variances.reshape(count // 2, 2, peers, bins, span).transpose(2, 0, 1, 3, 4)  8.41 us
  transfers between devices with their start and end apart: 3, of which 3 were waited for; matrix products, arithmetic and copies ran while one was open for 9% of the time, Pallas kernels for 0%

profile of v12, /device:TPU:0, one launch (start us, length us, event | category | flops | bytes accessed | tf_op | source)
XLA Modules:
  0.0 272.2 jit_solution(18424160157138937851)
XLA Ops:
  0.6 4.0 %fusion.37 = (bf16[1,24,128,256]{3,2,1,0:T(8,128)(2,1)}, bf16[1,24,128,256]{3,2,1,0:T(8,128)(2,1)}) fusion(bf16[2,24,128,256]{3,2,1,0:T(8,128)(2,1)} %param.8), kind=kLoop, calls=%fused_computation.45 | loop fusion | bytes 6291456 | tf_op jit(solution)/shard_map/slice | solution.py:16
  4.7 2.6 copy.74
  7.3 2.6 copy.75
  9.9 2.8 %log_convert_fusion = bf16[1,24,128,256]{2,3,1,0:T(8,128)(2,1)S(1)} fusion(bf16[1,24,128,256]{2,3,1,0:T(8,128)(2,1)} %copy.75, bf16[1,24,128,256]{2,3,1,0:T(8,128)(2,1)} %copy.74), kind=kLoop, calls=%fused_computation.17 | loop fusion | flops 5505024 | bytes 4718592 | tf_op jit(solution)/shard_map/convert_element_type | solution.py:18
  13.0 26.0 %all_to_all.20 = bf16[8,24,32,128]{3,2,1,0:T(8,128)(2,1)S(1)} all-to-all(bf16[8,24,32,128]{3,2,1,0:T(8,128)(2,1)S(1)} %copy.58), channel_id=1, replica_groups=mesh['freq'=8,'frame'=16] {'freq'}, dimensions={0} | all-to-all | bytes 3145728 | tf_op jit(solution)/shard_map/all_to_all | solution.py:25
  40.8 7.2 %fusion.13 = f32[24,32,1024]{2,1,0:T(8,128)} fusion(bf16[1024,1024]{1,0:T(8,128)(2,1)S(1)} %copy-done, f32[1024]{0:T(1024)S(1)} %copy-done.4, bf16[1024,1024]{1,0:T(8,128)(2,1)} %param.10, f32[1024]{0:T(1024)S(1)} %copy-done.5, f32[24,32]{1,0:T(8,128)S(1)} %add_rsqrt_fusion, f32[24,32]{1,0:T(8,128)S(1)} %broadcast_multiply_fusion, ...), kind=kOutput, calls=%fused_computation.22 | convolution fusion | flops 3229876224 | bytes 8927232 | tf_op jit(solution)/shard_map/nth,hg->ntg/dot_general | solution.py:35
  48.0 5.9 %fusion.23 = bf16[24,4,8,8,128]{4,3,2,1,0:T(8,128)(2,1)S(1)} fusion(f32[1024]{0:T(1024)S(1)} %copy-done.6, bf16[1024,1024]{1,0:T(8,128)(2,1)} %param.14, f32[24,32,1024]{2,1,0:T(8,128)} %fusion.13, f32[1024]{0:T(1024)S(1)} %copy-done.7), kind=kOutput, calls=%fused_computation.35 | convolution fusion | flops 1622409216 | bytes 6823936 | tf_op jit(solution)/shard_map/nth,hf->ntf/dot_general | solution.py:38
  53.9 1.4 copy.91
  55.4 4.4 %all-to-all-start.2 = ((bf16[8,24,32,128]{3,2,1,0:T(8,128)(2,1)}), bf16[8,24,32,128]{3,2,1,0:T(8,128)(2,1)}, u32[]{:S(2)}, u32[]{:S(2)}) async-start(bf16[8,24,32,128]{3,2,1,0:T(8,128)(2,1)} %bitcast.100), calls=%async_computation.2 | async-start | bytes 3145728 | tf_op jit(solution)/shard_map/all_to_all | solution.py:42
  59.8 2.0 copy_bitcast_fusion.1
  61.8 19.6 %all-to-all-done.2 = bf16[8,24,32,128]{3,2,1,0:T(8,128)(2,1)} async-done(((bf16[8,24,32,128]{3,2,1,0:T(8,128)(2,1)}), bf16[8,24,32,128]{3,2,1,0:T(8,128)(2,1)}, u32[]{:S(2)}, u32[]{:S(2)}) %all-to-all-start.2) | async-done | bytes 1572896 | tf_op jit(solution)/shard_map/all_to_all | solution.py:42
  81.4 8.1 %all-to-all-start = ((bf16[16,24,16,256]{3,2,1,0:T(8,128)(2,1)}), bf16[16,24,16,256]{3,2,1,0:T(8,128)(2,1)}, u32[]{:S(2)}, u32[]{:S(2)}) async-start(bf16[16,24,16,256]{3,2,1,0:T(8,128)(2,1)} %copy_bitcast_fusion.1), calls=%async_computation | async-start | bytes 6291456 | tf_op jit(solution)/shard_map/all_to_all | solution.py:212
  89.5 6.6 %copy.62 = bf16[24,128,8,32]{3,2,1,0:T(8,128)(2,1)} copy(bf16[24,128,8,32]{1,3,0,2:T(8,128)(2,1)} %bitcast.13) | data formatting | bytes 3145728 | tf_op jit(solution)/shard_map/transpose | solution.py:43
  96.1 8.4 %reshape_reshape.3 = bf16[12,2,16,8,256]{4,3,2,1,0:T(8,128)(2,1)} reshape(bf16[24,128,8,32]{3,2,1,0:T(8,128)(2,1)} %copy.62) | data formatting | bytes 3145728 | tf_op jit(solution)/shard_map/reshape;reshape | solution.py:210
  104.5 2.7 copy_bitcast_fusion.2
  107.2 29.3 %all-to-all-done.spec_in = bf16[16,24,16,256]{3,2,1,0:T(8,128)(2,1)} async-done(((bf16[16,24,16,256]{3,2,1,0:T(8,128)(2,1)}), bf16[16,24,16,256]{3,2,1,0:T(8,128)(2,1)}, u32[]{:S(2)}, u32[]{:S(2)}) %all-to-all-start) | async-done | bytes 3145760 | tf_op jit(solution)/shard_map/all_to_all | solution.py:212
  136.5 4.6 %all-to-all-start.3 = ((bf16[16,12,16,256]{3,2,1,0:T(8,128)(2,1)}), bf16[16,12,16,256]{3,2,1,0:T(8,128)(2,1)}, u32[]{:S(2)}, u32[]{:S(2)}) async-start(bf16[16,12,16,256]{3,2,1,0:T(8,128)(2,1)} %copy_bitcast_fusion.2), calls=%async_computation.3 | async-start | bytes 3145728 | tf_op jit(solution)/shard_map/all_to_all | solution.py:213
  141.1 3.0 %copy.61 = bf16[8,24,32,128]{3,2,0,1:T(8,128)(2,1)} copy(bf16[8,24,32,128]{3,2,1,0:T(8,128)(2,1)} %all-to-all-done.2) | data formatting | bytes 3145728 | tf_op jit(solution)/shard_map/all_to_all | solution.py:42
  144.2 2.6 copy.72
  146.7 16.7 %all-to-all-done.3.var_in = bf16[16,12,16,256]{3,2,1,0:T(8,128)(2,1)} async-done(((bf16[16,12,16,256]{3,2,1,0:T(8,128)(2,1)}), bf16[16,12,16,256]{3,2,1,0:T(8,128)(2,1)}, u32[]{:S(2)}, u32[]{:S(2)}) %all-to-all-start.3) | async-done | bytes 1572896 | tf_op jit(solution)/shard_map/all_to_all | solution.py:213
  163.4 61.5 %shard_map.95 = (f32[24,8,128]{2,1,0:T(8,128)}, f32[24,8,128]{2,1,0:T(8,128)}) custom-call(bf16[16,24,16,256]{3,2,1,0:T(8,128)(2,1)} %all-to-all-done.spec_in, bf16[16,12,16,256]{3,2,1,0:T(8,128)(2,1)} %all-to-all-done.3.var_in), custom_call_target="tpu_custom_call" | custom-call | tf_op jit(solution)/shard_map/pallas_call | solution.py:133
  226.7 11.9 %shard_map.96 = f32[16,72,128]{2,1,0:T(8,128)} custom-call(f32[72,128]{1,0:T(8,128)} %reshape.70.x_ref), custom_call_target="tpu_custom_call" | custom-call | tf_op jit(solution)/shard_map/pallas_call | solution.py:186
  238.6 4.1 %reshape.71 = f32[16,2,24,8,24]{4,3,2,1,0:T(8,128)} reshape(f32[16,72,128]{2,1,0:T(8,128)} %shard_map.96) | data formatting | bytes 1179648 | tf_op jit(solution)/shard_map/reshape | solution.py:219
  242.7 2.3 copy.90
  246.2 1.9 slice_bitcast_fusion
  248.1 1.8 copy.66
  250.0 2.6 copy.67
  252.6 2.6 copy.65
  255.1 2.3 maximum_maximum_fusion
  257.4 3.2 %copy.69 = f32[48,128,48]{2,0,1:T(8,128)} copy(f32[48,128,48]{1,2,0:T(8,128)} %maximum_maximum_fusion) | data formatting | bytes 2359296 | tf_op jit(solution)/shard_map/concatenate | solution.py:224
  260.6 5.3 %fusion.9 = f32[128,48,256]{2,1,0:T(8,128)S(1)} fusion(f32[48,128,48]{2,0,1:T(8,128)} %copy.69, bf16[48,128,256]{2,1,0:T(8,128)(2,1)S(1)} %bitcast.96), kind=kOutput, calls=%fused_computation.13 | convolution fusion | flops 452984832 | bytes 10616832 | tf_op jit(solution)/shard_map/jfa,aft->jft/dot_general | solution.py:226
  265.9 6.3 %copy.71 = f32[2,24,128,256]{3,2,1,0:T(8,128)} copy(f32[2,24,128,256]{3,1,0,2:T(8,128)S(1)} %bitcast.97) | data formatting | bytes 12582912
  (25 shorter events, 5.0 us)
Async XLA Ops:
  0.6 40.1 %copy-start = (bf16[1024,1024]{1,0:T(8,128)(2,1)S(1)}, bf16[1024,1024]{1,0:T(8,128)(2,1)}, u32[]{:S(2)}) copy-start(bf16[1024,1024]{1,0:T(8,128)(2,1)} %param.12) | copy-start | bytes 6291460
  13.0 27.8 %copy-start.4 = (f32[1024]{0:T(1024)S(1)}, f32[1024]{0:T(1024)}, u32[]{:S(2)}) copy-start(f32[1024]{0:T(1024)} %param.11) | copy-start | bytes 12292
  13.0 27.8 %copy-start.5 = (f32[1024]{0:T(1024)S(1)}, f32[1024]{0:T(1024)}, u32[]{:S(2)}) copy-start(f32[1024]{0:T(1024)} %param.9) | copy-start | bytes 12292
  39.0 1.1 copy-start.3
  40.7 7.3 %copy-start.6 = (f32[1024]{0:T(1024)S(1)}, f32[1024]{0:T(1024)}, u32[]{:S(2)}) copy-start(f32[1024]{0:T(1024)} %param.15) | copy-start | bytes 12292
  40.7 7.2 %copy-start.7 = (f32[1024]{0:T(1024)S(1)}, f32[1024]{0:T(1024)}, u32[]{:S(2)}) copy-start(f32[1024]{0:T(1024)} %param.13) | copy-start | bytes 12292
  53.9 5.9 %copy-start.2 = (bf16[2,24,128,256]{3,2,1,0:T(8,128)(2,1)S(1)}, bf16[2,24,128,256]{3,2,1,0:T(8,128)(2,1)}, u32[]{:S(2)}) copy-start(bf16[2,24,128,256]{3,2,1,0:T(8,128)(2,1)} %param.8) | copy-start | bytes 9437188
  55.4 26.0 %all-to-all-start.2 = ((bf16[8,24,32,128]{3,2,1,0:T(8,128)(2,1)}), bf16[8,24,32,128]{3,2,1,0:T(8,128)(2,1)}, u32[]{:S(2)}, u32[]{:S(2)}) async-start(bf16[8,24,32,128]{3,2,1,0:T(8,128)(2,1)} %bitcast.100), calls=%async_computation.2 | async-start | bytes 3145728 | tf_op jit(solution)/shard_map/all_to_all | solution.py:42
  81.4 55.1 %all-to-all-start = ((bf16[16,24,16,256]{3,2,1,0:T(8,128)(2,1)}), bf16[16,24,16,256]{3,2,1,0:T(8,128)(2,1)}, u32[]{:S(2)}, u32[]{:S(2)}) async-start(bf16[16,24,16,256]{3,2,1,0:T(8,128)(2,1)} %copy_bitcast_fusion.1), calls=%async_computation | async-start | bytes 6291456 | tf_op jit(solution)/shard_map/all_to_all | solution.py:212
  136.5 26.9 %all-to-all-start.3 = ((bf16[16,12,16,256]{3,2,1,0:T(8,128)(2,1)}), bf16[16,12,16,256]{3,2,1,0:T(8,128)(2,1)}, u32[]{:S(2)}, u32[]{:S(2)}) async-start(bf16[16,12,16,256]{3,2,1,0:T(8,128)(2,1)} %copy_bitcast_fusion.2), calls=%async_computation.3 | async-start | bytes 3145728 | tf_op jit(solution)/shard_map/all_to_all | solution.py:213
  265.8 6.4 %copy-start.1 = (bf16[1024,1024]{1,0:T(8,128)(2,1)S(1)}, bf16[1024,1024]{1,0:T(8,128)(2,1)}, u32[]{:S(2)}) copy-start(bf16[1024,1024]{1,0:T(8,128)(2,1)} %param.12) | copy-start | bytes 6291460

commit v13 on v12

--- a/solution.py
+++ b/solution.py
@@ -43,11 +43,12 @@
     return received.transpose(1, 3, 0, 2).reshape(count, freq, span)
 
 
-def sweep_kernel(frames, spec_in, var_in, mr_ref, mi_ref, yr, yi, w, pr, pi, pp):
+def sweep_kernel(frames, spec_in, var_in, mr_ref, mi_ref, yr, yi, w, pr, pi, qr, qi, qp, cr, ci):
     count, bins, length = yr.shape
     peers, _, _, span = spec_in.shape
     chunk = 256
     chunks = length // chunk
+    group = 6
 
     def init(s, carry):
         cols = pl.ds(pl.multiple_of(s * span, span), span)
@@ -76,50 +77,80 @@
 
     lax.fori_loop(0, count, init_mix, 0)
 
+    def coefficients(acc, j, source):
+        numer_real = jnp.sum(acc[0], axis=1, keepdims=True) / frames
+        numer_imag = jnp.sum(acc[1], axis=1, keepdims=True) / frames
+        denom = jnp.sum(acc[2], axis=1, keepdims=True) / frames
+        is_self = j == source
+        coef_real = jnp.where(is_self, 1.0 - lax.rsqrt(denom), numer_real / denom)
+        coef_imag = jnp.where(is_self, 0.0, numer_imag / denom)
+        cr[j] = jnp.broadcast_to(coef_real, (bins, 128))
+        ci[j] = jnp.broadcast_to(coef_imag, (bins, 128))
+
+    def accumulate(acc, ww, a_r, a_i, b_r, b_i, b_p):
+        acc[0] = acc[0] + ww * (a_r * b_r + a_i * b_i)
+        acc[1] = acc[1] + ww * (a_i * b_r - a_r * b_i)
+        acc[2] = acc[2] + ww * b_p
+
+    qr[...] = yr[0]
+    qi[...] = yi[0]
+    qp[...] = qr[...] * qr[...] + qi[...] * qi[...]
+
+    def first(g, carry):
+        sources = tuple(group * g + h for h in range(group))
+        acc = [[jnp.zeros((bins, chunk), jnp.float32) for _ in range(3)] for _ in sources]
+        for c in range(chunks):
+            sl = pl.ds(c * chunk, chunk)
+            b_r, b_i, b_p = qr[:, sl], qi[:, sl], qp[:, sl]
+            for h, j in enumerate(sources):
+                accumulate(acc[h], w[j, :, sl], yr[j, :, sl], yi[j, :, sl], b_r, b_i, b_p)
+        for h, j in enumerate(sources):
+            coefficients(acc[h], j, 0)
+        return carry
+
+    lax.fori_loop(0, count // group, first, 0)
+
     def step(k, carry):
-        pr[...] = yr[k]
-        pi[...] = yi[k]
-        pp[...] = pr[...] * pr[...] + pi[...] * pi[...]
+        pr[...] = qr[...]
+        pi[...] = qi[...]
         mkr = mr_ref[k]
         mki = mi_ref[k]
 
-        def per_pair(p, carry):
-            sources = tuple(6 * p + h for h in range(6))
+        def mix(j, carry):
+            c_r = cr[j][:, :1]
+            c_i = ci[j][:, :1]
+            mr_ref[j] = mr_ref[j] - (c_r * mkr - c_i * mki)
+            mi_ref[j] = mi_ref[j] - (c_r * mki + c_i * mkr)
+            return carry
+
+        lax.fori_loop(0, count, mix, 0)
+        after = lax.min(k + 1, count - 1)
+        c_r = cr[after][:, :1]
+        c_i = ci[after][:, :1]
+        qr[...] = yr[after] - (c_r * pr[...] - c_i * pi[...])
+        qi[...] = yi[after] - (c_r * pi[...] + c_i * pr[...])
+        qp[...] = qr[...] * qr[...] + qi[...] * qi[...]
+
+        def fused(g, carry):
+            sources = tuple(group * g + h for h in range(group))
+            coefs = [(cr[j][:, :1], ci[j][:, :1]) for j in sources]
             acc = [[jnp.zeros((bins, chunk), jnp.float32) for _ in range(3)] for _ in sources]
             for c in range(chunks):
                 sl = pl.ds(c * chunk, chunk)
-                b_r = pr[:, sl]
-                b_i = pi[:, sl]
-                b_p = pp[:, sl]
+                b_r, b_i = pr[:, sl], pi[:, sl]
+                n_r, n_i, n_p = qr[:, sl], qi[:, sl], qp[:, sl]
                 for h, j in enumerate(sources):
-                    a_r = yr[j, :, sl]
-                    a_i = yi[j, :, sl]
-                    ww = w[j, :, sl]
-                    acc[h][0] = acc[h][0] + ww * (a_r * b_r + a_i * b_i)
-                    acc[h][1] = acc[h][1] + ww * (a_i * b_r - a_r * b_i)
-                    acc[h][2] = acc[h][2] + ww * b_p
-            coefs = []
+                    coef_real, coef_imag = coefs[h]
+                    a_r = yr[j, :, sl] - (coef_real * b_r - coef_imag * b_i)
+                    a_i = yi[j, :, sl] - (coef_real * b_i + coef_imag * b_r)
+                    yr[j, :, sl] = a_r
+                    yi[j, :, sl] = a_i
+                    accumulate(acc[h], w[j, :, sl], a_r, a_i, n_r, n_i, n_p)
             for h, j in enumerate(sources):
-                numer_real = jnp.sum(acc[h][0], axis=1, keepdims=True) / frames
-                numer_imag = jnp.sum(acc[h][1], axis=1, keepdims=True) / frames
-                denom = jnp.sum(acc[h][2], axis=1, keepdims=True) / frames
-                is_self = j == k
-                coef_real = jnp.where(is_self, 1.0 - lax.rsqrt(denom), numer_real / denom)
-                coef_imag = jnp.where(is_self, 0.0, numer_imag / denom)
-                coefs.append((coef_real, coef_imag))
-            for c in range(chunks):
-                sl = pl.ds(c * chunk, chunk)
-                b_r = pr[:, sl]
-                b_i = pi[:, sl]
-                for j, (coef_real, coef_imag) in zip(sources, coefs):
-                    yr[j, :, sl] = yr[j, :, sl] - (coef_real * b_r - coef_imag * b_i)
-                    yi[j, :, sl] = yi[j, :, sl] - (coef_real * b_i + coef_imag * b_r)
-            for j, (coef_real, coef_imag) in zip(sources, coefs):
-                mr_ref[j] = mr_ref[j] - (coef_real * mkr - coef_imag * mki)
-                mi_ref[j] = mi_ref[j] - (coef_real * mki + coef_imag * mkr)
+                coefficients(acc[h], j, k + 1)
             return carry
 
-        lax.fori_loop(0, count // 6, per_pair, 0)
+        lax.fori_loop(0, count // group, fused, 0)
         return carry
 
     lax.fori_loop(0, count, step, 0)
@@ -145,6 +176,10 @@
             pltpu.VMEM((bins, length), jnp.float32),
             pltpu.VMEM((bins, length), jnp.float32),
             pltpu.VMEM((bins, length), jnp.float32),
+            pltpu.VMEM((bins, length), jnp.float32),
+            pltpu.VMEM((bins, length), jnp.float32),
+            pltpu.VMEM((count, bins, lanes), jnp.float32),
+            pltpu.VMEM((count, bins, lanes), jnp.float32),
         ],
         compiler_params=pltpu.CompilerParams(vmem_limit_bytes=60 * 1024 * 1024),
     )(spec_in, var_in)

time: 274 us -> 327 us (1.19)
  Pallas kernels: 73.4 us -> 126 us
    pallas_call x1, Pallas kernels: 61.5 us -> 114 us  [sweep(): pl.pallas_call(functools.partial(sweep_kernel, frames), out_shape=(jax.Sh...]
  transfers between devices with their start and end apart: 3 -> 3, of which waited for: 3 -> 3; matrix products, arithmetic and copies ran while one was open for 9% -> 8% of each run, Pallas kernels for 0% -> 0%
where the time goes in v13:
time: 327 us; the launch traced here: 325 us
  Pallas kernels  126 us (39%)
  waiting for transfers between devices  65.6 us (20%)
  local copies, waits for them, and re-layouts  63.6 us (19%)
  blocking collectives  26 us (8%)
  matrix products  18.4 us (6%)
  starting transfers between devices  17.1 us (5%)
  other arithmetic  7.21 us (2%)
    pallas_call x1, Pallas kernels, sweep(): pl.pallas_call(functools.partial(sweep_kernel, frames), out_shape=(jax.Sh...  114 us
    all_to_all x1, waiting for transfers between devices, on_device(): lax.all_to_all(spec_send, 'frame', split_axis=0, concat_axis=0, tiled=True)  29.3 us
    all_to_all x1, blocking collectives, source_model(): lax.all_to_all(send, 'freq', split_axis=0, concat_axis=0, tiled=True)  26 us
    all_to_all x1, waiting for transfers between devices, source_model(): lax.all_to_all(send, 'freq', split_axis=0, concat_axis=0, tiled=True)  19.6 us
    all_to_all x1, waiting for transfers between devices, on_device(): lax.all_to_all(var_send, 'frame', split_axis=0, concat_axis=0, tiled=True)  16.7 us
    unnamed x20, local copies, waits for them, and re-layouts  15 us
    pallas_call x1, Pallas kernels, frame_gather(): pl.pallas_call(gather_kernel, out_shape=jax.ShapeDtypeStruct((n,) + x.sha...  11.9 us
    another operation x1, local copies, waits for them, and re-layouts, on_device(): variances.reshape(count // 2, 2, peers, bins, span).transpose(2, 0, 1, 3, 4)  8.41 us
  transfers between devices with their start and end apart: 3, of which 3 were waited for; matrix products, arithmetic and copies ran while one was open for 8% of the time, Pallas kernels for 0%

profile of v13, /device:TPU:0, one launch (start us, length us, event | category | flops | bytes accessed | tf_op | source)
XLA Modules:
  0.0 325.2 jit_solution(15066476256803990909)
XLA Ops:
  0.6 4.0 %fusion.37 = (bf16[1,24,128,256]{3,2,1,0:T(8,128)(2,1)}, bf16[1,24,128,256]{3,2,1,0:T(8,128)(2,1)}) fusion(bf16[2,24,128,256]{3,2,1,0:T(8,128)(2,1)} %param.8), kind=kLoop, calls=%fused_computation.45 | loop fusion | bytes 6291456 | tf_op jit(solution)/shard_map/slice | solution.py:16
  4.7 2.6 copy.74
  7.3 2.6 copy.75
  9.9 2.8 log_convert_fusion
  13.0 26.0 %all_to_all.20 = bf16[8,24,32,128]{3,2,1,0:T(8,128)(2,1)S(1)} all-to-all(bf16[8,24,32,128]{3,2,1,0:T(8,128)(2,1)S(1)} %copy.58), channel_id=1, replica_groups=mesh['freq'=8,'frame'=16] {'freq'}, dimensions={0} | all-to-all | bytes 3145728 | tf_op jit(solution)/shard_map/all_to_all | solution.py:25
  40.8 7.2 %fusion.13 = f32[24,32,1024]{2,1,0:T(8,128)} fusion(bf16[1024,1024]{1,0:T(8,128)(2,1)S(1)} %copy-done, f32[1024]{0:T(1024)S(1)} %copy-done.4, bf16[1024,1024]{1,0:T(8,128)(2,1)} %param.10, f32[1024]{0:T(1024)S(1)} %copy-done.5, f32[24,32]{1,0:T(8,128)S(1)} %add_rsqrt_fusion, f32[24,32]{1,0:T(8,128)S(1)} %broadcast_multiply_fusion, ...), kind=kOutput, calls=%fused_computation.22 | convolution fusion | flops 3229876224 | bytes 8927232 | tf_op jit(solution)/shard_map/nth,hg->ntg/dot_general | solution.py:35
  48.0 5.9 %fusion.23 = bf16[24,4,8,8,128]{4,3,2,1,0:T(8,128)(2,1)S(1)} fusion(f32[1024]{0:T(1024)S(1)} %copy-done.6, bf16[1024,1024]{1,0:T(8,128)(2,1)} %param.14, f32[24,32,1024]{2,1,0:T(8,128)} %fusion.13, f32[1024]{0:T(1024)S(1)} %copy-done.7), kind=kOutput, calls=%fused_computation.35 | convolution fusion | flops 1622409216 | bytes 6823936 | tf_op jit(solution)/shard_map/nth,hf->ntf/dot_general | solution.py:38
  53.9 1.4 copy.91
  55.4 4.4 %all-to-all-start.2 = ((bf16[8,24,32,128]{3,2,1,0:T(8,128)(2,1)}), bf16[8,24,32,128]{3,2,1,0:T(8,128)(2,1)}, u32[]{:S(2)}, u32[]{:S(2)}) async-start(bf16[8,24,32,128]{3,2,1,0:T(8,128)(2,1)} %bitcast.100), calls=%async_computation.2 | async-start | bytes 3145728 | tf_op jit(solution)/shard_map/all_to_all | solution.py:42
  59.8 2.0 copy_bitcast_fusion.1
  61.8 19.6 %all-to-all-done.2 = bf16[8,24,32,128]{3,2,1,0:T(8,128)(2,1)} async-done(((bf16[8,24,32,128]{3,2,1,0:T(8,128)(2,1)}), bf16[8,24,32,128]{3,2,1,0:T(8,128)(2,1)}, u32[]{:S(2)}, u32[]{:S(2)}) %all-to-all-start.2) | async-done | bytes 1572896 | tf_op jit(solution)/shard_map/all_to_all | solution.py:42
  81.4 8.1 %all-to-all-start = ((bf16[16,24,16,256]{3,2,1,0:T(8,128)(2,1)}), bf16[16,24,16,256]{3,2,1,0:T(8,128)(2,1)}, u32[]{:S(2)}, u32[]{:S(2)}) async-start(bf16[16,24,16,256]{3,2,1,0:T(8,128)(2,1)} %copy_bitcast_fusion.1), calls=%async_computation | async-start | bytes 6291456 | tf_op jit(solution)/shard_map/all_to_all | solution.py:247
  89.5 6.6 %copy.62 = bf16[24,128,8,32]{3,2,1,0:T(8,128)(2,1)} copy(bf16[24,128,8,32]{1,3,0,2:T(8,128)(2,1)} %bitcast.13) | data formatting | bytes 3145728 | tf_op jit(solution)/shard_map/transpose | solution.py:43
  96.1 8.4 %reshape_reshape.3 = bf16[12,2,16,8,256]{4,3,2,1,0:T(8,128)(2,1)} reshape(bf16[24,128,8,32]{3,2,1,0:T(8,128)(2,1)} %copy.62) | data formatting | bytes 3145728 | tf_op jit(solution)/shard_map/reshape;reshape | solution.py:245
  104.5 2.7 copy_bitcast_fusion.2
  107.2 29.3 %all-to-all-done.spec_in = bf16[16,24,16,256]{3,2,1,0:T(8,128)(2,1)} async-done(((bf16[16,24,16,256]{3,2,1,0:T(8,128)(2,1)}), bf16[16,24,16,256]{3,2,1,0:T(8,128)(2,1)}, u32[]{:S(2)}, u32[]{:S(2)}) %all-to-all-start) | async-done | bytes 3145760 | tf_op jit(solution)/shard_map/all_to_all | solution.py:247
  136.5 4.6 %all-to-all-start.3 = ((bf16[16,12,16,256]{3,2,1,0:T(8,128)(2,1)}), bf16[16,12,16,256]{3,2,1,0:T(8,128)(2,1)}, u32[]{:S(2)}, u32[]{:S(2)}) async-start(bf16[16,12,16,256]{3,2,1,0:T(8,128)(2,1)} %copy_bitcast_fusion.2), calls=%async_computation.3 | async-start | bytes 3145728 | tf_op jit(solution)/shard_map/all_to_all | solution.py:248
  141.1 3.0 copy.61
  144.2 2.6 copy.72
  146.7 16.7 %all-to-all-done.3.var_in = bf16[16,12,16,256]{3,2,1,0:T(8,128)(2,1)} async-done(((bf16[16,12,16,256]{3,2,1,0:T(8,128)(2,1)}), bf16[16,12,16,256]{3,2,1,0:T(8,128)(2,1)}, u32[]{:S(2)}, u32[]{:S(2)}) %all-to-all-start.3) | async-done | bytes 1572896 | tf_op jit(solution)/shard_map/all_to_all | solution.py:248
  163.4 114.5 %shard_map.95 = (f32[24,8,128]{2,1,0:T(8,128)}, f32[24,8,128]{2,1,0:T(8,128)}) custom-call(bf16[16,24,16,256]{3,2,1,0:T(8,128)(2,1)} %all-to-all-done.spec_in, bf16[16,12,16,256]{3,2,1,0:T(8,128)(2,1)} %all-to-all-done.3.var_in), custom_call_target="tpu_custom_call" | custom-call | tf_op jit(solution)/shard_map/pallas_call | solution.py:164
  279.6 11.9 %shard_map.96 = f32[16,72,128]{2,1,0:T(8,128)} custom-call(f32[72,128]{1,0:T(8,128)} %reshape.70.x_ref), custom_call_target="tpu_custom_call" | custom-call | tf_op jit(solution)/shard_map/pallas_call | solution.py:221
  291.5 4.1 %reshape.71 = f32[16,2,24,8,24]{4,3,2,1,0:T(8,128)} reshape(f32[16,72,128]{2,1,0:T(8,128)} %shard_map.96) | data formatting | bytes 1179648 | tf_op jit(solution)/shard_map/reshape | solution.py:254
  295.6 2.3 copy.90
  299.2 1.9 slice_bitcast_fusion
  301.1 1.8 copy.66
  302.9 2.6 copy.67
  305.5 2.6 copy.65
  308.1 2.3 maximum_maximum_fusion
  310.3 3.2 copy.69
  313.5 5.3 %fusion.9 = f32[128,48,256]{2,1,0:T(8,128)S(1)} fusion(f32[48,128,48]{2,0,1:T(8,128)} %copy.69, bf16[48,128,256]{2,1,0:T(8,128)(2,1)S(1)} %bitcast.96), kind=kOutput, calls=%fused_computation.13 | convolution fusion | flops 452984832 | bytes 10616832 | tf_op jit(solution)/shard_map/jfa,aft->jft/dot_general | solution.py:261
  318.8 6.3 %copy.71 = f32[2,24,128,256]{3,2,1,0:T(8,128)} copy(f32[2,24,128,256]{3,1,0,2:T(8,128)S(1)} %bitcast.97) | data formatting | bytes 12582912
  (25 shorter events, 5.0 us)
Async XLA Ops:
  0.6 40.1 %copy-start = (bf16[1024,1024]{1,0:T(8,128)(2,1)S(1)}, bf16[1024,1024]{1,0:T(8,128)(2,1)}, u32[]{:S(2)}) copy-start(bf16[1024,1024]{1,0:T(8,128)(2,1)} %param.12) | copy-start | bytes 6291460
  13.0 27.8 %copy-start.4 = (f32[1024]{0:T(1024)S(1)}, f32[1024]{0:T(1024)}, u32[]{:S(2)}) copy-start(f32[1024]{0:T(1024)} %param.11) | copy-start | bytes 12292
  13.0 27.8 %copy-start.5 = (f32[1024]{0:T(1024)S(1)}, f32[1024]{0:T(1024)}, u32[]{:S(2)}) copy-start(f32[1024]{0:T(1024)} %param.9) | copy-start | bytes 12292
  39.0 1.1 copy-start.3
  40.7 7.3 %copy-start.6 = (f32[1024]{0:T(1024)S(1)}, f32[1024]{0:T(1024)}, u32[]{:S(2)}) copy-start(f32[1024]{0:T(1024)} %param.15) | copy-start | bytes 12292
  40.7 7.2 %copy-start.7 = (f32[1024]{0:T(1024)S(1)}, f32[1024]{0:T(1024)}, u32[]{:S(2)}) copy-start(f32[1024]{0:T(1024)} %param.13) | copy-start | bytes 12292
  53.9 5.9 %copy-start.2 = (bf16[2,24,128,256]{3,2,1,0:T(8,128)(2,1)S(1)}, bf16[2,24,128,256]{3,2,1,0:T(8,128)(2,1)}, u32[]{:S(2)}) copy-start(bf16[2,24,128,256]{3,2,1,0:T(8,128)(2,1)} %param.8) | copy-start | bytes 9437188
  55.4 26.0 %all-to-all-start.2 = ((bf16[8,24,32,128]{3,2,1,0:T(8,128)(2,1)}), bf16[8,24,32,128]{3,2,1,0:T(8,128)(2,1)}, u32[]{:S(2)}, u32[]{:S(2)}) async-start(bf16[8,24,32,128]{3,2,1,0:T(8,128)(2,1)} %bitcast.100), calls=%async_computation.2 | async-start | bytes 3145728 | tf_op jit(solution)/shard_map/all_to_all | solution.py:42
  81.4 55.1 %all-to-all-start = ((bf16[16,24,16,256]{3,2,1,0:T(8,128)(2,1)}), bf16[16,24,16,256]{3,2,1,0:T(8,128)(2,1)}, u32[]{:S(2)}, u32[]{:S(2)}) async-start(bf16[16,24,16,256]{3,2,1,0:T(8,128)(2,1)} %copy_bitcast_fusion.1), calls=%async_computation | async-start | bytes 6291456 | tf_op jit(solution)/shard_map/all_to_all | solution.py:247
  136.5 26.9 %all-to-all-start.3 = ((bf16[16,12,16,256]{3,2,1,0:T(8,128)(2,1)}), bf16[16,12,16,256]{3,2,1,0:T(8,128)(2,1)}, u32[]{:S(2)}, u32[]{:S(2)}) async-start(bf16[16,12,16,256]{3,2,1,0:T(8,128)(2,1)} %copy_bitcast_fusion.2), calls=%async_computation.3 | async-start | bytes 3145728 | tf_op jit(solution)/shard_map/all_to_all | solution.py:248
  318.8 6.4 %copy-start.1 = (bf16[1024,1024]{1,0:T(8,128)(2,1)S(1)}, bf16[1024,1024]{1,0:T(8,128)(2,1)}, u32[]{:S(2)}) copy-start(bf16[1024,1024]{1,0:T(8,128)(2,1)} %param.12) | copy-start | bytes 6291460

commit v14 on v12

--- a/solution.py
+++ b/solution.py
@@ -46,7 +46,7 @@
 def sweep_kernel(frames, spec_in, var_in, mr_ref, mi_ref, yr, yi, w, pr, pi, pp):
     count, bins, length = yr.shape
     peers, _, _, span = spec_in.shape
-    chunk = 256
+    chunk = 128
     chunks = length // chunk
 
     def init(s, carry):
@@ -84,7 +84,7 @@
         mki = mi_ref[k]
 
         def per_pair(p, carry):
-            sources = tuple(6 * p + h for h in range(6))
+            sources = tuple(12 * p + h for h in range(12))
             acc = [[jnp.zeros((bins, chunk), jnp.float32) for _ in range(3)] for _ in sources]
             for c in range(chunks):
                 sl = pl.ds(c * chunk, chunk)
@@ -119,7 +119,7 @@
                 mi_ref[j] = mi_ref[j] - (coef_real * mki + coef_imag * mkr)
             return carry
 
-        lax.fori_loop(0, count // 6, per_pair, 0)
+        lax.fori_loop(0, count // 12, per_pair, 0)
         return carry
 
     lax.fori_loop(0, count, step, 0)

time: 274 us -> 279 us (1.018)
  Pallas kernels: 73.4 us -> 78.6 us
    pallas_call x1, Pallas kernels: 61.5 us -> 66.7 us  [sweep(): pl.pallas_call(functools.partial(sweep_kernel, frames), out_shape=(jax.Sh...]
where the time goes in v14:
time: 279 us; the launch traced here: 277 us
  Pallas kernels  78.6 us (28%)
  waiting for transfers between devices  65.6 us (24%)
  local copies, waits for them, and re-layouts  63.6 us (23%)
  blocking collectives  26 us (9%)
  matrix products  18.4 us (7%)
  starting transfers between devices  17.1 us (6%)
  other arithmetic  7.21 us (3%)
    pallas_call x1, Pallas kernels, sweep(): pl.pallas_call(functools.partial(sweep_kernel, frames), out_shape=(jax.Sh...  66.7 us
    all_to_all x1, waiting for transfers between devices, on_device(): lax.all_to_all(spec_send, 'frame', split_axis=0, concat_axis=0, tiled=True)  29.3 us
    all_to_all x1, blocking collectives, source_model(): lax.all_to_all(send, 'freq', split_axis=0, concat_axis=0, tiled=True)  26 us
    all_to_all x1, waiting for transfers between devices, source_model(): lax.all_to_all(send, 'freq', split_axis=0, concat_axis=0, tiled=True)  19.6 us
    all_to_all x1, waiting for transfers between devices, on_device(): lax.all_to_all(var_send, 'frame', split_axis=0, concat_axis=0, tiled=True)  16.7 us
    unnamed x20, local copies, waits for them, and re-layouts  15 us
    pallas_call x1, Pallas kernels, frame_gather(): pl.pallas_call(gather_kernel, out_shape=jax.ShapeDtypeStruct((n,) + x.sha...  11.9 us
    another operation x1, local copies, waits for them, and re-layouts, on_device(): variances.reshape(count // 2, 2, peers, bins, span).transpose(2, 0, 1, 3, 4)  8.41 us
  transfers between devices with their start and end apart: 3, of which 3 were waited for; matrix products, arithmetic and copies ran while one was open for 9% of the time, Pallas kernels for 0%

profile of v14, /device:TPU:0, one launch (start us, length us, event | category | flops | bytes accessed | tf_op | source)
XLA Modules:
  0.0 277.4 jit_solution(12860312349255252374)
XLA Ops:
  0.6 4.0 %fusion.37 = (bf16[1,24,128,256]{3,2,1,0:T(8,128)(2,1)}, bf16[1,24,128,256]{3,2,1,0:T(8,128)(2,1)}) fusion(bf16[2,24,128,256]{3,2,1,0:T(8,128)(2,1)} %param.8), kind=kLoop, calls=%fused_computation.45 | loop fusion | bytes 6291456 | tf_op jit(solution)/shard_map/slice | solution.py:16
  4.7 2.6 copy.74
  7.3 2.6 copy.75
  9.9 2.8 %log_convert_fusion = bf16[1,24,128,256]{2,3,1,0:T(8,128)(2,1)S(1)} fusion(bf16[1,24,128,256]{2,3,1,0:T(8,128)(2,1)} %copy.75, bf16[1,24,128,256]{2,3,1,0:T(8,128)(2,1)} %copy.74), kind=kLoop, calls=%fused_computation.17 | loop fusion | flops 5505024 | bytes 4718592 | tf_op jit(solution)/shard_map/convert_element_type | solution.py:18
  13.0 26.0 %all_to_all.20 = bf16[8,24,32,128]{3,2,1,0:T(8,128)(2,1)S(1)} all-to-all(bf16[8,24,32,128]{3,2,1,0:T(8,128)(2,1)S(1)} %copy.58), channel_id=1, replica_groups=mesh['freq'=8,'frame'=16] {'freq'}, dimensions={0} | all-to-all | bytes 3145728 | tf_op jit(solution)/shard_map/all_to_all | solution.py:25
  40.8 7.2 %fusion.13 = f32[24,32,1024]{2,1,0:T(8,128)} fusion(bf16[1024,1024]{1,0:T(8,128)(2,1)S(1)} %copy-done, f32[1024]{0:T(1024)S(1)} %copy-done.4, bf16[1024,1024]{1,0:T(8,128)(2,1)} %param.10, f32[1024]{0:T(1024)S(1)} %copy-done.5, f32[24,32]{1,0:T(8,128)S(1)} %add_rsqrt_fusion, f32[24,32]{1,0:T(8,128)S(1)} %broadcast_multiply_fusion, ...), kind=kOutput, calls=%fused_computation.22 | convolution fusion | flops 3229876224 | bytes 8927232 | tf_op jit(solution)/shard_map/nth,hg->ntg/dot_general | solution.py:35
  48.0 5.9 %fusion.23 = bf16[24,4,8,8,128]{4,3,2,1,0:T(8,128)(2,1)S(1)} fusion(f32[1024]{0:T(1024)S(1)} %copy-done.6, bf16[1024,1024]{1,0:T(8,128)(2,1)} %param.14, f32[24,32,1024]{2,1,0:T(8,128)} %fusion.13, f32[1024]{0:T(1024)S(1)} %copy-done.7), kind=kOutput, calls=%fused_computation.35 | convolution fusion | flops 1622409216 | bytes 6823936 | tf_op jit(solution)/shard_map/nth,hf->ntf/dot_general | solution.py:38
  53.9 1.4 copy.91
  55.4 4.4 %all-to-all-start.2 = ((bf16[8,24,32,128]{3,2,1,0:T(8,128)(2,1)}), bf16[8,24,32,128]{3,2,1,0:T(8,128)(2,1)}, u32[]{:S(2)}, u32[]{:S(2)}) async-start(bf16[8,24,32,128]{3,2,1,0:T(8,128)(2,1)} %bitcast.100), calls=%async_computation.2 | async-start | bytes 3145728 | tf_op jit(solution)/shard_map/all_to_all | solution.py:42
  59.8 2.0 copy_bitcast_fusion.1
  61.8 19.6 %all-to-all-done.2 = bf16[8,24,32,128]{3,2,1,0:T(8,128)(2,1)} async-done(((bf16[8,24,32,128]{3,2,1,0:T(8,128)(2,1)}), bf16[8,24,32,128]{3,2,1,0:T(8,128)(2,1)}, u32[]{:S(2)}, u32[]{:S(2)}) %all-to-all-start.2) | async-done | bytes 1572896 | tf_op jit(solution)/shard_map/all_to_all | solution.py:42
  81.4 8.1 %all-to-all-start = ((bf16[16,24,16,256]{3,2,1,0:T(8,128)(2,1)}), bf16[16,24,16,256]{3,2,1,0:T(8,128)(2,1)}, u32[]{:S(2)}, u32[]{:S(2)}) async-start(bf16[16,24,16,256]{3,2,1,0:T(8,128)(2,1)} %copy_bitcast_fusion.1), calls=%async_computation | async-start | bytes 6291456 | tf_op jit(solution)/shard_map/all_to_all | solution.py:212
  89.5 6.6 %copy.62 = bf16[24,128,8,32]{3,2,1,0:T(8,128)(2,1)} copy(bf16[24,128,8,32]{1,3,0,2:T(8,128)(2,1)} %bitcast.13) | data formatting | bytes 3145728 | tf_op jit(solution)/shard_map/transpose | solution.py:43
  96.1 8.4 %reshape_reshape.3 = bf16[12,2,16,8,256]{4,3,2,1,0:T(8,128)(2,1)} reshape(bf16[24,128,8,32]{3,2,1,0:T(8,128)(2,1)} %copy.62) | data formatting | bytes 3145728 | tf_op jit(solution)/shard_map/reshape;reshape | solution.py:210
  104.5 2.7 copy_bitcast_fusion.2
  107.2 29.3 %all-to-all-done.spec_in = bf16[16,24,16,256]{3,2,1,0:T(8,128)(2,1)} async-done(((bf16[16,24,16,256]{3,2,1,0:T(8,128)(2,1)}), bf16[16,24,16,256]{3,2,1,0:T(8,128)(2,1)}, u32[]{:S(2)}, u32[]{:S(2)}) %all-to-all-start) | async-done | bytes 3145760 | tf_op jit(solution)/shard_map/all_to_all | solution.py:212
  136.5 4.6 %all-to-all-start.3 = ((bf16[16,12,16,256]{3,2,1,0:T(8,128)(2,1)}), bf16[16,12,16,256]{3,2,1,0:T(8,128)(2,1)}, u32[]{:S(2)}, u32[]{:S(2)}) async-start(bf16[16,12,16,256]{3,2,1,0:T(8,128)(2,1)} %copy_bitcast_fusion.2), calls=%async_computation.3 | async-start | bytes 3145728 | tf_op jit(solution)/shard_map/all_to_all | solution.py:213
  141.1 3.0 %copy.61 = bf16[8,24,32,128]{3,2,0,1:T(8,128)(2,1)} copy(bf16[8,24,32,128]{3,2,1,0:T(8,128)(2,1)} %all-to-all-done.2) | data formatting | bytes 3145728 | tf_op jit(solution)/shard_map/all_to_all | solution.py:42
  144.2 2.6 copy.72
  146.7 16.7 %all-to-all-done.3.var_in = bf16[16,12,16,256]{3,2,1,0:T(8,128)(2,1)} async-done(((bf16[16,12,16,256]{3,2,1,0:T(8,128)(2,1)}), bf16[16,12,16,256]{3,2,1,0:T(8,128)(2,1)}, u32[]{:S(2)}, u32[]{:S(2)}) %all-to-all-start.3) | async-done | bytes 1572896 | tf_op jit(solution)/shard_map/all_to_all | solution.py:213
  163.4 66.7 %shard_map.95 = (f32[24,8,128]{2,1,0:T(8,128)}, f32[24,8,128]{2,1,0:T(8,128)}) custom-call(bf16[16,24,16,256]{3,2,1,0:T(8,128)(2,1)} %all-to-all-done.spec_in, bf16[16,12,16,256]{3,2,1,0:T(8,128)(2,1)} %all-to-all-done.3.var_in), custom_call_target="tpu_custom_call" | custom-call | tf_op jit(solution)/shard_map/pallas_call | solution.py:133
  231.8 11.9 %shard_map.96 = f32[16,72,128]{2,1,0:T(8,128)} custom-call(f32[72,128]{1,0:T(8,128)} %reshape.70.x_ref), custom_call_target="tpu_custom_call" | custom-call | tf_op jit(solution)/shard_map/pallas_call | solution.py:186
  243.7 4.1 %reshape.71 = f32[16,2,24,8,24]{4,3,2,1,0:T(8,128)} reshape(f32[16,72,128]{2,1,0:T(8,128)} %shard_map.96) | data formatting | bytes 1179648 | tf_op jit(solution)/shard_map/reshape | solution.py:219
  247.8 2.3 copy.90
  251.4 1.9 slice_bitcast_fusion
  253.3 1.8 copy.66
  255.1 2.6 copy.67
  257.7 2.6 copy.65
  260.3 2.3 maximum_maximum_fusion
  262.5 3.2 %copy.69 = f32[48,128,48]{2,0,1:T(8,128)} copy(f32[48,128,48]{1,2,0:T(8,128)} %maximum_maximum_fusion) | data formatting | bytes 2359296 | tf_op jit(solution)/shard_map/concatenate | solution.py:224
  265.7 5.3 %fusion.9 = f32[128,48,256]{2,1,0:T(8,128)S(1)} fusion(f32[48,128,48]{2,0,1:T(8,128)} %copy.69, bf16[48,128,256]{2,1,0:T(8,128)(2,1)S(1)} %bitcast.96), kind=kOutput, calls=%fused_computation.13 | convolution fusion | flops 452984832 | bytes 10616832 | tf_op jit(solution)/shard_map/jfa,aft->jft/dot_general | solution.py:226
  271.0 6.3 %copy.71 = f32[2,24,128,256]{3,2,1,0:T(8,128)} copy(f32[2,24,128,256]{3,1,0,2:T(8,128)S(1)} %bitcast.97) | data formatting | bytes 12582912
  (25 shorter events, 5.0 us)
Async XLA Ops:
  0.6 40.1 %copy-start = (bf16[1024,1024]{1,0:T(8,128)(2,1)S(1)}, bf16[1024,1024]{1,0:T(8,128)(2,1)}, u32[]{:S(2)}) copy-start(bf16[1024,1024]{1,0:T(8,128)(2,1)} %param.12) | copy-start | bytes 6291460
  13.0 27.8 %copy-start.4 = (f32[1024]{0:T(1024)S(1)}, f32[1024]{0:T(1024)}, u32[]{:S(2)}) copy-start(f32[1024]{0:T(1024)} %param.11) | copy-start | bytes 12292
  13.0 27.8 %copy-start.5 = (f32[1024]{0:T(1024)S(1)}, f32[1024]{0:T(1024)}, u32[]{:S(2)}) copy-start(f32[1024]{0:T(1024)} %param.9) | copy-start | bytes 12292
  39.0 1.1 copy-start.3
  40.7 7.3 %copy-start.6 = (f32[1024]{0:T(1024)S(1)}, f32[1024]{0:T(1024)}, u32[]{:S(2)}) copy-start(f32[1024]{0:T(1024)} %param.15) | copy-start | bytes 12292
  40.7 7.2 %copy-start.7 = (f32[1024]{0:T(1024)S(1)}, f32[1024]{0:T(1024)}, u32[]{:S(2)}) copy-start(f32[1024]{0:T(1024)} %param.13) | copy-start | bytes 12292
  53.9 5.9 %copy-start.2 = (bf16[2,24,128,256]{3,2,1,0:T(8,128)(2,1)S(1)}, bf16[2,24,128,256]{3,2,1,0:T(8,128)(2,1)}, u32[]{:S(2)}) copy-start(bf16[2,24,128,256]{3,2,1,0:T(8,128)(2,1)} %param.8) | copy-start | bytes 9437188
  55.4 26.0 %all-to-all-start.2 = ((bf16[8,24,32,128]{3,2,1,0:T(8,128)(2,1)}), bf16[8,24,32,128]{3,2,1,0:T(8,128)(2,1)}, u32[]{:S(2)}, u32[]{:S(2)}) async-start(bf16[8,24,32,128]{3,2,1,0:T(8,128)(2,1)} %bitcast.100), calls=%async_computation.2 | async-start | bytes 3145728 | tf_op jit(solution)/shard_map/all_to_all | solution.py:42
  81.4 55.1 %all-to-all-start = ((bf16[16,24,16,256]{3,2,1,0:T(8,128)(2,1)}), bf16[16,24,16,256]{3,2,1,0:T(8,128)(2,1)}, u32[]{:S(2)}, u32[]{:S(2)}) async-start(bf16[16,24,16,256]{3,2,1,0:T(8,128)(2,1)} %copy_bitcast_fusion.1), calls=%async_computation | async-start | bytes 6291456 | tf_op jit(solution)/shard_map/all_to_all | solution.py:212
  136.5 26.9 %all-to-all-start.3 = ((bf16[16,12,16,256]{3,2,1,0:T(8,128)(2,1)}), bf16[16,12,16,256]{3,2,1,0:T(8,128)(2,1)}, u32[]{:S(2)}, u32[]{:S(2)}) async-start(bf16[16,12,16,256]{3,2,1,0:T(8,128)(2,1)} %copy_bitcast_fusion.2), calls=%async_computation.3 | async-start | bytes 3145728 | tf_op jit(solution)/shard_map/all_to_all | solution.py:213
  271.0 6.4 %copy-start.1 = (bf16[1024,1024]{1,0:T(8,128)(2,1)S(1)}, bf16[1024,1024]{1,0:T(8,128)(2,1)}, u32[]{:S(2)}) copy-start(bf16[1024,1024]{1,0:T(8,128)(2,1)} %param.12) | copy-start | bytes 6291460

commit v15 on v12

--- a/solution.py
+++ b/solution.py
@@ -222,11 +222,12 @@
     top = jnp.concatenate([mix_real, -mix_imag], axis=2)
     bottom = jnp.concatenate([mix_imag, mix_real], axis=2)
     mix = jnp.concatenate([top, bottom], axis=0)
-    stacked = spectra.reshape(2 * count, spectra.shape[2], spectra.shape[3]).astype(jnp.float32)
+    stacked = spectra.reshape(2 * count, spectra.shape[2], spectra.shape[3])
+    mix_high = mix.astype(jnp.bfloat16)
+    mix_low = (mix - mix_high.astype(jnp.float32)).astype(jnp.bfloat16)
     demixed = jnp.einsum(
-        "jfa,aft->jft", mix, stacked, precision=lax.Precision.HIGH,
-        preferred_element_type=jnp.float32,
-    )
+        "jfa,aft->jft", mix_high, stacked, preferred_element_type=jnp.float32
+    ) + jnp.einsum("jfa,aft->jft", mix_low, stacked, preferred_element_type=jnp.float32)
     return (demixed.reshape(spectra.shape), variances)
 
 

time: 274 us -> 277 us (1.011)
  matrix products: 18.4 us -> 21.2 us
    dot_general x1 -> x2, matrix products: 5.26 us -> 8.01 us  [the longest x1 5.49 us: on_device(): jnp.einsum('jfa,aft->jft', mix_low, stacked, preferred_element_type=jnp.f...]
    unnamed x20 -> x22, local copies, waits for them, and re-layouts: 15 us -> 15 us
where the time goes in v15:
time: 277 us; the launch traced here: 275 us
  Pallas kernels  73.4 us (26%)
  waiting for transfers between devices  65.6 us (24%)
  local copies, waits for them, and re-layouts  63.7 us (23%)
  blocking collectives  26 us (9%)
  matrix products  21.2 us (8%)
  starting transfers between devices  17.1 us (6%)
  other arithmetic  7.23 us (3%)
    pallas_call x1, Pallas kernels, sweep(): pl.pallas_call(functools.partial(sweep_kernel, frames), out_shape=(jax.Sh...  61.5 us
    all_to_all x1, waiting for transfers between devices, on_device(): lax.all_to_all(spec_send, 'frame', split_axis=0, concat_axis=0, tiled=True)  29.3 us
    all_to_all x1, blocking collectives, source_model(): lax.all_to_all(send, 'freq', split_axis=0, concat_axis=0, tiled=True)  26 us
    all_to_all x1, waiting for transfers between devices, source_model(): lax.all_to_all(send, 'freq', split_axis=0, concat_axis=0, tiled=True)  19.6 us
    all_to_all x1, waiting for transfers between devices, on_device(): lax.all_to_all(var_send, 'frame', split_axis=0, concat_axis=0, tiled=True)  16.7 us
    unnamed x22, local copies, waits for them, and re-layouts  15 us
    pallas_call x1, Pallas kernels, frame_gather(): pl.pallas_call(gather_kernel, out_shape=jax.ShapeDtypeStruct((n,) + x.sha...  11.9 us
    another operation x1, local copies, waits for them, and re-layouts, on_device(): variances.reshape(count // 2, 2, peers, bins, span).transpose(2, 0, 1, 3, 4)  8.41 us
  transfers between devices with their start and end apart: 3, of which 3 were waited for; matrix products, arithmetic and copies ran while one was open for 9% of the time, Pallas kernels for 0%

profile of v15, /device:TPU:0, one launch (start us, length us, event | category | flops | bytes accessed | tf_op | source)
XLA Modules:
  0.0 275.0 jit_solution(13919841205761228171)
XLA Ops:
  0.6 4.0 %fusion.44 = (bf16[1,24,128,256]{3,2,1,0:T(8,128)(2,1)}, bf16[1,24,128,256]{3,2,1,0:T(8,128)(2,1)}) fusion(bf16[2,24,128,256]{3,2,1,0:T(8,128)(2,1)} %param.8), kind=kLoop, calls=%fused_computation.51 | loop fusion | bytes 6291456 | tf_op jit(solution)/shard_map/slice | solution.py:16
  4.7 2.6 copy.81
  7.3 2.6 copy.82
  9.9 2.8 %log_convert_fusion = bf16[1,24,128,256]{2,3,1,0:T(8,128)(2,1)S(1)} fusion(bf16[1,24,128,256]{2,3,1,0:T(8,128)(2,1)} %copy.82, bf16[1,24,128,256]{2,3,1,0:T(8,128)(2,1)} %copy.81), kind=kLoop, calls=%fused_computation.15 | loop fusion | flops 5505024 | bytes 4718592 | tf_op jit(solution)/shard_map/convert_element_type | solution.py:18
  13.0 26.0 %all_to_all.20 = bf16[8,24,32,128]{3,2,1,0:T(8,128)(2,1)S(1)} all-to-all(bf16[8,24,32,128]{3,2,1,0:T(8,128)(2,1)S(1)} %copy.63), channel_id=1, replica_groups=mesh['freq'=8,'frame'=16] {'freq'}, dimensions={0} | all-to-all | bytes 3145728 | tf_op jit(solution)/shard_map/all_to_all | solution.py:25
  40.8 7.2 %fusion.18 = f32[24,32,1024]{2,1,0:T(8,128)} fusion(bf16[1024,1024]{1,0:T(8,128)(2,1)S(1)} %copy-done, f32[1024]{0:T(1024)S(1)} %copy-done.5, bf16[1024,1024]{1,0:T(8,128)(2,1)} %param.10, f32[1024]{0:T(1024)S(1)} %copy-done.6, f32[24,32]{1,0:T(8,128)S(1)} %add_rsqrt_fusion, f32[24,32]{1,0:T(8,128)S(1)} %broadcast_multiply_fusion, ...), kind=kOutput, calls=%fused_computation.26 | convolution fusion | flops 3229876224 | bytes 8927232 | tf_op jit(solution)/shard_map/nth,hg->ntg/dot_general | solution.py:35
  48.0 5.9 %fusion.28 = bf16[24,4,8,8,128]{4,3,2,1,0:T(8,128)(2,1)S(1)} fusion(f32[1024]{0:T(1024)S(1)} %copy-done.7, bf16[1024,1024]{1,0:T(8,128)(2,1)} %param.14, f32[24,32,1024]{2,1,0:T(8,128)} %fusion.18, f32[1024]{0:T(1024)S(1)} %copy-done.8), kind=kOutput, calls=%fused_computation.39 | convolution fusion | flops 1622409216 | bytes 6823936 | tf_op jit(solution)/shard_map/nth,hf->ntf/dot_general | solution.py:38
  55.4 4.4 %all-to-all-start.2 = ((bf16[8,24,32,128]{3,2,1,0:T(8,128)(2,1)}), bf16[8,24,32,128]{3,2,1,0:T(8,128)(2,1)}, u32[]{:S(2)}, u32[]{:S(2)}) async-start(bf16[8,24,32,128]{3,2,1,0:T(8,128)(2,1)} %bitcast.100), calls=%async_computation.2 | async-start | bytes 3145728 | tf_op jit(solution)/shard_map/all_to_all | solution.py:42
  59.8 2.0 copy_bitcast_fusion.1
  61.8 19.6 %all-to-all-done.2 = bf16[8,24,32,128]{3,2,1,0:T(8,128)(2,1)} async-done(((bf16[8,24,32,128]{3,2,1,0:T(8,128)(2,1)}), bf16[8,24,32,128]{3,2,1,0:T(8,128)(2,1)}, u32[]{:S(2)}, u32[]{:S(2)}) %all-to-all-start.2) | async-done | bytes 1572896 | tf_op jit(solution)/shard_map/all_to_all | solution.py:42
  81.4 8.1 %all-to-all-start = ((bf16[16,24,16,256]{3,2,1,0:T(8,128)(2,1)}), bf16[16,24,16,256]{3,2,1,0:T(8,128)(2,1)}, u32[]{:S(2)}, u32[]{:S(2)}) async-start(bf16[16,24,16,256]{3,2,1,0:T(8,128)(2,1)} %copy_bitcast_fusion.1), calls=%async_computation | async-start | bytes 6291456 | tf_op jit(solution)/shard_map/all_to_all | solution.py:212
  89.5 6.6 %copy.67 = bf16[24,128,8,32]{3,2,1,0:T(8,128)(2,1)} copy(bf16[24,128,8,32]{1,3,0,2:T(8,128)(2,1)} %bitcast.13) | data formatting | bytes 3145728 | tf_op jit(solution)/shard_map/transpose | solution.py:43
  96.1 8.4 %reshape_reshape.3 = bf16[12,2,16,8,256]{4,3,2,1,0:T(8,128)(2,1)} reshape(bf16[24,128,8,32]{3,2,1,0:T(8,128)(2,1)} %copy.67) | data formatting | bytes 3145728 | tf_op jit(solution)/shard_map/reshape;reshape | solution.py:210
  104.5 2.7 copy_bitcast_fusion.2
  107.2 29.3 %all-to-all-done.spec_in = bf16[16,24,16,256]{3,2,1,0:T(8,128)(2,1)} async-done(((bf16[16,24,16,256]{3,2,1,0:T(8,128)(2,1)}), bf16[16,24,16,256]{3,2,1,0:T(8,128)(2,1)}, u32[]{:S(2)}, u32[]{:S(2)}) %all-to-all-start) | async-done | bytes 3145760 | tf_op jit(solution)/shard_map/all_to_all | solution.py:212
  136.5 4.6 %all-to-all-start.3 = ((bf16[16,12,16,256]{3,2,1,0:T(8,128)(2,1)}), bf16[16,12,16,256]{3,2,1,0:T(8,128)(2,1)}, u32[]{:S(2)}, u32[]{:S(2)}) async-start(bf16[16,12,16,256]{3,2,1,0:T(8,128)(2,1)} %copy_bitcast_fusion.2), calls=%async_computation.3 | async-start | bytes 3145728 | tf_op jit(solution)/shard_map/all_to_all | solution.py:213
  141.1 3.0 %copy.66 = bf16[8,24,32,128]{3,2,0,1:T(8,128)(2,1)} copy(bf16[8,24,32,128]{3,2,1,0:T(8,128)(2,1)} %all-to-all-done.2) | data formatting | bytes 3145728 | tf_op jit(solution)/shard_map/all_to_all | solution.py:42
  144.2 2.6 copy.79
  146.7 16.7 %all-to-all-done.3.var_in = bf16[16,12,16,256]{3,2,1,0:T(8,128)(2,1)} async-done(((bf16[16,12,16,256]{3,2,1,0:T(8,128)(2,1)}), bf16[16,12,16,256]{3,2,1,0:T(8,128)(2,1)}, u32[]{:S(2)}, u32[]{:S(2)}) %all-to-all-start.3) | async-done | bytes 1572896 | tf_op jit(solution)/shard_map/all_to_all | solution.py:213
  163.4 61.5 %shard_map.95 = (f32[24,8,128]{2,1,0:T(8,128)}, f32[24,8,128]{2,1,0:T(8,128)}) custom-call(bf16[16,24,16,256]{3,2,1,0:T(8,128)(2,1)} %all-to-all-done.spec_in, bf16[16,12,16,256]{3,2,1,0:T(8,128)(2,1)} %all-to-all-done.3.var_in), custom_call_target="tpu_custom_call" | custom-call | tf_op jit(solution)/shard_map/pallas_call | solution.py:133
  226.7 11.9 %shard_map.96 = f32[16,72,128]{2,1,0:T(8,128)} custom-call(f32[72,128]{1,0:T(8,128)} %reshape.70.x_ref), custom_call_target="tpu_custom_call" | custom-call | tf_op jit(solution)/shard_map/pallas_call | solution.py:186
  238.6 4.1 %reshape.71 = f32[16,2,24,8,24]{4,3,2,1,0:T(8,128)} reshape(f32[16,72,128]{2,1,0:T(8,128)} %shard_map.96) | data formatting | bytes 1179648 | tf_op jit(solution)/shard_map/reshape | solution.py:219
  242.7 2.3 copy.101
  246.2 1.9 slice_bitcast_fusion
  248.1 1.8 copy.71
  249.9 2.6 copy.72
  252.5 2.6 copy.70
  255.1 2.3 maximum_maximum_fusion
  257.4 3.2 %copy.74 = f32[48,128,48]{2,0,1:T(8,128)} copy(f32[48,128,48]{1,2,0:T(8,128)} %maximum_maximum_fusion) | data formatting | bytes 2359296 | tf_op jit(solution)/shard_map/concatenate | solution.py:224
  260.6 5.5 %fusion.9 = f32[128,48,256]{2,1,0:T(8,128)S(1)} fusion(bf16[48,128,256]{2,1,0:T(8,128)(2,1)S(1)} %bitcast.95, f32[48,128,48]{2,0,1:T(8,128)} %copy.74), kind=kOutput, calls=%fused_computation.19 | convolution fusion | flops 152174592 | bytes 10616832 | tf_op jit(solution)/shard_map/jfa,aft->jft/dot_general | solution.py:230
  266.1 2.5 fusion.13
  268.6 6.3 %copy.78 = f32[2,24,128,256]{3,2,1,0:T(8,128)} copy(f32[2,24,128,256]{3,1,0,2:T(8,128)S(1)} %bitcast.97) | data formatting | bytes 12582912
  (28 shorter events, 6.5 us)
Async XLA Ops:
  0.6 40.1 %copy-start = (bf16[1024,1024]{1,0:T(8,128)(2,1)S(1)}, bf16[1024,1024]{1,0:T(8,128)(2,1)}, u32[]{:S(2)}) copy-start(bf16[1024,1024]{1,0:T(8,128)(2,1)} %param.12) | copy-start | bytes 6291460
  13.0 27.8 %copy-start.5 = (f32[1024]{0:T(1024)S(1)}, f32[1024]{0:T(1024)}, u32[]{:S(2)}) copy-start(f32[1024]{0:T(1024)} %param.11) | copy-start | bytes 12292
  13.0 27.8 %copy-start.6 = (f32[1024]{0:T(1024)S(1)}, f32[1024]{0:T(1024)}, u32[]{:S(2)}) copy-start(f32[1024]{0:T(1024)} %param.9) | copy-start | bytes 12292
  39.0 1.1 copy-start.4
  40.8 7.3 %copy-start.7 = (f32[1024]{0:T(1024)S(1)}, f32[1024]{0:T(1024)}, u32[]{:S(2)}) copy-start(f32[1024]{0:T(1024)} %param.15) | copy-start | bytes 12292
  40.8 7.2 %copy-start.8 = (f32[1024]{0:T(1024)S(1)}, f32[1024]{0:T(1024)}, u32[]{:S(2)}) copy-start(f32[1024]{0:T(1024)} %param.13) | copy-start | bytes 12292
  53.9 5.9 %copy-start.2 = (bf16[2,24,128,256]{3,2,1,0:T(8,128)(2,1)S(1)}, bf16[2,24,128,256]{3,2,1,0:T(8,128)(2,1)}, u32[]{:S(2)}) copy-start(bf16[2,24,128,256]{3,2,1,0:T(8,128)(2,1)} %param.8) | copy-start | bytes 9437188
  55.4 26.0 %all-to-all-start.2 = ((bf16[8,24,32,128]{3,2,1,0:T(8,128)(2,1)}), bf16[8,24,32,128]{3,2,1,0:T(8,128)(2,1)}, u32[]{:S(2)}, u32[]{:S(2)}) async-start(bf16[8,24,32,128]{3,2,1,0:T(8,128)(2,1)} %bitcast.100), calls=%async_computation.2 | async-start | bytes 3145728 | tf_op jit(solution)/shard_map/all_to_all | solution.py:42
  81.4 55.1 %all-to-all-start = ((bf16[16,24,16,256]{3,2,1,0:T(8,128)(2,1)}), bf16[16,24,16,256]{3,2,1,0:T(8,128)(2,1)}, u32[]{:S(2)}, u32[]{:S(2)}) async-start(bf16[16,24,16,256]{3,2,1,0:T(8,128)(2,1)} %copy_bitcast_fusion.1), calls=%async_computation | async-start | bytes 6291456 | tf_op jit(solution)/shard_map/all_to_all | solution.py:212
  136.5 26.9 %all-to-all-start.3 = ((bf16[16,12,16,256]{3,2,1,0:T(8,128)(2,1)}), bf16[16,12,16,256]{3,2,1,0:T(8,128)(2,1)}, u32[]{:S(2)}, u32[]{:S(2)}) async-start(bf16[16,12,16,256]{3,2,1,0:T(8,128)(2,1)} %copy_bitcast_fusion.2), calls=%async_computation.3 | async-start | bytes 3145728 | tf_op jit(solution)/shard_map/all_to_all | solution.py:213
  260.6 5.5 %copy-start.3 = (f32[48,128,48]{2,0,1:T(8,128)S(1)}, f32[48,128,48]{2,0,1:T(8,128)}, u32[]{:S(2)}) copy-start(f32[48,128,48]{2,0,1:T(8,128)} %copy.74) | copy-start | bytes 3538948
  268.6 6.4 %copy-start.1 = (bf16[1024,1024]{1,0:T(8,128)(2,1)S(1)}, bf16[1024,1024]{1,0:T(8,128)(2,1)}, u32[]{:S(2)}) copy-start(bf16[1024,1024]{1,0:T(8,128)(2,1)} %param.12) | copy-start | bytes 6291460

commit v16 on v12

--- a/solution.py
+++ b/solution.py
@@ -219,15 +219,17 @@
     mix = mix.reshape(peers, 2, count, bins, count).transpose(1, 2, 0, 3, 4)
     mix = mix.reshape(2, count, peers * bins, count)
     mix_real, mix_imag = mix[0], mix[1]
-    top = jnp.concatenate([mix_real, -mix_imag], axis=2)
-    bottom = jnp.concatenate([mix_imag, mix_real], axis=2)
-    mix = jnp.concatenate([top, bottom], axis=0)
-    stacked = spectra.reshape(2 * count, spectra.shape[2], spectra.shape[3]).astype(jnp.float32)
-    demixed = jnp.einsum(
-        "jfa,aft->jft", mix, stacked, precision=lax.Precision.HIGH,
-        preferred_element_type=jnp.float32,
-    )
-    return (demixed.reshape(spectra.shape), variances)
+    real_part = spectra[0].astype(jnp.float32)
+    imag_part = spectra[1].astype(jnp.float32)
+
+    def apply(m, y):
+        return jnp.einsum(
+            "jfa,aft->jft", m, y, precision=lax.Precision.HIGH, preferred_element_type=jnp.float32
+        )
+
+    demixed_real = apply(mix_real, real_part) - apply(mix_imag, imag_part)
+    demixed_imag = apply(mix_real, imag_part) + apply(mix_imag, real_part)
+    return (jnp.stack([demixed_real, demixed_imag]), variances)
 
 
 def solution(mesh):

time: 274 us -> 260 us (0.949)
  local copies, waits for them, and re-layouts: 63.6 us -> 49.1 us
  matrix products: 18.4 us -> 21.3 us
    squeeze x3 -> x0, local copies, waits for them, and re-layouts: 7.05 us -> none  [on_device(): mix_real, mix_imag = (mix[0], mix[1])]
    transpose x1 -> x2, local copies, waits for them, and re-layouts: 0.28 us -> 4.53 us  [source_model(): logpower.transpose(0, 2, 1).reshape(count, shards, rows, freq)]
    unnamed x20 -> x24, local copies, waits for them, and re-layouts: 15 us -> 10.8 us
    transpose x0 -> x1, other arithmetic: none -> 3.27 us  [source_model(): logpower.transpose(0, 2, 1).reshape(count, shards, rows, freq)]
    concatenate x1 -> x0, local copies, waits for them, and re-layouts: 3.2 us -> none  [on_device(): mix = jnp.concatenate([top, bottom], axis=0)]
    dot_general x1 -> x4, matrix products: 5.26 us -> 8.18 us  [apply(): jnp.einsum('jfa,aft->jft', m, y, precision=lax.Precision.HIGH, preferred_...]
    convert_element_type x1 -> x0, other arithmetic: 2.8 us -> none  [source_model(): jnp.log(real_part * real_part + imag_part * imag_part + power_floor)]
    reshape x2 -> x1, local copies, waits for them, and re-layouts: 6.36 us -> 4.08 us  [on_device(): mix = mix.reshape(peers, 2, count, bins, count).transpose(1, 2, 0, 3, 4)]
where the time goes in v16:
time: 260 us; the launch traced here: 258 us
  Pallas kernels  73.4 us (28%)
  waiting for transfers between devices  66.9 us (26%)
  local copies, waits for them, and re-layouts  49.1 us (19%)
  blocking collectives  26 us (10%)
  matrix products  21.3 us (8%)
  starting transfers between devices  16.1 us (6%)
  other arithmetic  4.57 us (2%)
    pallas_call x1, Pallas kernels, sweep(): pl.pallas_call(functools.partial(sweep_kernel, frames), out_shape=(jax.Sh...  61.5 us
    all_to_all x1, waiting for transfers between devices, on_device(): lax.all_to_all(spec_send, 'frame', split_axis=0, concat_axis=0, tiled=True)  31 us
    all_to_all x1, blocking collectives, source_model(): lax.all_to_all(send, 'freq', split_axis=0, concat_axis=0, tiled=True)  26 us
    all_to_all x1, waiting for transfers between devices, on_device(): lax.all_to_all(var_send, 'frame', split_axis=0, concat_axis=0, tiled=True)  18.3 us
    all_to_all x1, waiting for transfers between devices, source_model(): lax.all_to_all(send, 'freq', split_axis=0, concat_axis=0, tiled=True)  17.6 us
    pallas_call x1, Pallas kernels, frame_gather(): pl.pallas_call(gather_kernel, out_shape=jax.ShapeDtypeStruct((n,) + x.sha...  11.9 us
    unnamed x24, local copies, waits for them, and re-layouts  10.8 us
    another operation x1, local copies, waits for them, and re-layouts, on_device(): variances.reshape(count // 2, 2, peers, bins, span).transpose(2, 0, 1, 3, 4)  8.41 us
  transfers between devices with their start and end apart: 3, of which 3 were waited for; matrix products, arithmetic and copies ran while one was open for 9% of the time, Pallas kernels for 0%

profile of v16, /device:TPU:0, one launch (start us, length us, event | category | flops | bytes accessed | tf_op | source)
XLA Modules:
  0.0 258.3 jit_solution(7672646310908977491)
XLA Ops:
  0.6 2.4 fusion.38
  3.0 1.2 copy-done.2
  4.7 3.3 %fusion.15 = bf16[24,256,128]{1,0,2:T(8,128)(2,1)} fusion(bf16[1,24,128,256]{3,2,1,0:T(8,128)(2,1)S(1)} %get-tuple-element.17, bf16[1,24,128,256]{3,2,1,0:T(8,128)(2,1)S(1)} %get-tuple-element.16), kind=kLoop, calls=%fused_computation.26 | loop fusion | flops 5505024 | bytes 4718592 | tf_op jit(solution)/shard_map/transpose | solution.py:24
  8.0 2.8 %copy.44 = bf16[24,256,128]{2,1,0:T(8,128)(2,1)} copy(bf16[24,256,128]{1,0,2:T(8,128)(2,1)} %fusion.15) | data formatting | bytes 3145728 | tf_op jit(solution)/shard_map/transpose | solution.py:24
  10.8 1.7 copy.45
  12.5 26.0 %all_to_all.20 = bf16[8,24,32,128]{3,2,1,0:T(8,128)(2,1)S(1)} all-to-all(bf16[8,24,32,128]{3,2,1,0:T(8,128)(2,1)S(1)} %copy.45), channel_id=1, replica_groups=mesh['freq'=8,'frame'=16] {'freq'}, dimensions={0} | all-to-all | bytes 3145728 | tf_op jit(solution)/shard_map/all_to_all | solution.py:25
  40.3 7.2 %fusion.11 = f32[24,32,1024]{2,1,0:T(8,128)} fusion(bf16[1024,1024]{1,0:T(8,128)(2,1)S(1)} %copy-done, f32[1024]{0:T(1024)S(1)} %copy-done.7, bf16[1024,1024]{1,0:T(8,128)(2,1)} %param.10, f32[1024]{0:T(1024)S(1)} %copy-done.8, f32[24,32]{1,0:T(8,128)S(1)} %add_rsqrt_fusion, f32[24,32]{1,0:T(8,128)S(1)} %broadcast_multiply_fusion, ...), kind=kOutput, calls=%fused_computation.22 | convolution fusion | flops 3229876224 | bytes 8927232 | tf_op jit(solution)/shard_map/nth,hg->ntg/dot_general | solution.py:35
  47.5 5.9 %fusion.22 = bf16[24,4,8,8,128]{4,3,2,1,0:T(8,128)(2,1)S(1)} fusion(f32[1024]{0:T(1024)S(1)} %copy-done.9, bf16[1024,1024]{1,0:T(8,128)(2,1)} %param.14, f32[24,32,1024]{2,1,0:T(8,128)} %fusion.11, f32[1024]{0:T(1024)S(1)} %copy-done.10), kind=kOutput, calls=%fused_computation.36 | convolution fusion | flops 1622409216 | bytes 6823936 | tf_op jit(solution)/shard_map/nth,hf->ntf/dot_general | solution.py:38
  53.5 1.4 copy.79
  54.9 3.6 %all-to-all-start.2 = ((bf16[8,24,32,128]{3,2,1,0:T(8,128)(2,1)}), bf16[8,24,32,128]{3,2,1,0:T(8,128)(2,1)S(1)}, u32[]{:S(2)}, u32[]{:S(2)}) async-start(bf16[8,24,32,128]{3,2,1,0:T(8,128)(2,1)} %bitcast.113), calls=%async_computation.2 | async-start | bytes 3145728 | tf_op jit(solution)/shard_map/all_to_all | solution.py:42
  58.5 3.9 %copy_bitcast_fusion = bf16[16,24,16,256]{3,2,1,0:T(8,128)(2,1)} fusion(bf16[2,24,128,256]{3,2,1,0:T(8,128)(2,1)} %param.8), kind=kLoop, calls=%fused_computation.14 | loop fusion | bytes 6291456 | tf_op jit(solution)/shard_map/reshape | solution.py:209
  62.4 17.6 %all-to-all-done.2 = bf16[8,24,32,128]{3,2,1,0:T(8,128)(2,1)S(1)} async-done(((bf16[8,24,32,128]{3,2,1,0:T(8,128)(2,1)}), bf16[8,24,32,128]{3,2,1,0:T(8,128)(2,1)S(1)}, u32[]{:S(2)}, u32[]{:S(2)}) %all-to-all-start.2) | async-done | bytes 1572896 | tf_op jit(solution)/shard_map/all_to_all | solution.py:42
  80.0 8.1 %all-to-all-start = ((bf16[16,24,16,256]{3,2,1,0:T(8,128)(2,1)}), bf16[16,24,16,256]{3,2,1,0:T(8,128)(2,1)}, u32[]{:S(2)}, u32[]{:S(2)}) async-start(bf16[16,24,16,256]{3,2,1,0:T(8,128)(2,1)} %copy_bitcast_fusion), calls=%async_computation | async-start | bytes 6291456 | tf_op jit(solution)/shard_map/all_to_all | solution.py:212
  88.1 4.9 %copy.49 = bf16[24,128,8,32]{3,2,1,0:T(8,128)(2,1)} copy(bf16[24,128,8,32]{1,3,0,2:T(8,128)(2,1)S(1)} %bitcast.111) | data formatting | bytes 3145728 | tf_op jit(solution)/shard_map/transpose | solution.py:43
  93.0 8.4 %reshape_reshape.3 = bf16[12,2,16,8,256]{4,3,2,1,0:T(8,128)(2,1)} reshape(bf16[24,128,8,32]{3,2,1,0:T(8,128)(2,1)} %copy.49) | data formatting | bytes 3145728 | tf_op jit(solution)/shard_map/reshape;reshape | solution.py:210
  101.4 2.7 %copy_bitcast_fusion.3 = bf16[16,12,16,256]{3,2,1,0:T(8,128)(2,1)} fusion(bf16[12,2,16,8,256]{4,3,2,1,0:T(8,128)(2,1)} %reshape_reshape.3), kind=kLoop, calls=%fused_computation.30 | loop fusion | bytes 3145728 | tf_op jit(solution)/shard_map/reshape | solution.py:211
  104.1 31.0 %all-to-all-done.spec_in = bf16[16,24,16,256]{3,2,1,0:T(8,128)(2,1)} async-done(((bf16[16,24,16,256]{3,2,1,0:T(8,128)(2,1)}), bf16[16,24,16,256]{3,2,1,0:T(8,128)(2,1)}, u32[]{:S(2)}, u32[]{:S(2)}) %all-to-all-start) | async-done | bytes 3145760 | tf_op jit(solution)/shard_map/all_to_all | solution.py:212
  135.1 4.4 %all-to-all-start.3 = ((bf16[16,12,16,256]{3,2,1,0:T(8,128)(2,1)}), bf16[16,12,16,256]{3,2,1,0:T(8,128)(2,1)}, u32[]{:S(2)}, u32[]{:S(2)}) async-start(bf16[16,12,16,256]{3,2,1,0:T(8,128)(2,1)} %copy_bitcast_fusion.3), calls=%async_computation.3 | async-start | bytes 3145728 | tf_op jit(solution)/shard_map/all_to_all | solution.py:213
  139.5 1.6 copy.48
  141.2 2.6 copy.54
  143.8 18.3 %all-to-all-done.3.var_in = bf16[16,12,16,256]{3,2,1,0:T(8,128)(2,1)} async-done(((bf16[16,12,16,256]{3,2,1,0:T(8,128)(2,1)}), bf16[16,12,16,256]{3,2,1,0:T(8,128)(2,1)}, u32[]{:S(2)}, u32[]{:S(2)}) %all-to-all-start.3) | async-done | bytes 1572896 | tf_op jit(solution)/shard_map/all_to_all | solution.py:213
  162.0 61.5 %shard_map.95 = (f32[24,8,128]{2,1,0:T(8,128)}, f32[24,8,128]{2,1,0:T(8,128)}) custom-call(bf16[16,24,16,256]{3,2,1,0:T(8,128)(2,1)} %all-to-all-done.spec_in, bf16[16,12,16,256]{3,2,1,0:T(8,128)(2,1)} %all-to-all-done.3.var_in), custom_call_target="tpu_custom_call" | custom-call | tf_op jit(solution)/shard_map/pallas_call | solution.py:133
  223.5 1.0 slice_bitcast_fusion
  225.3 11.9 %shard_map.96 = f32[16,72,128]{2,1,0:T(8,128)} custom-call(f32[72,128]{1,0:T(8,128)} %reshape.57.x_ref), custom_call_target="tpu_custom_call" | custom-call | tf_op jit(solution)/shard_map/pallas_call | solution.py:186
  237.2 4.1 %reshape.58 = f32[16,2,24,8,24]{4,3,2,1,0:T(8,128)} reshape(f32[16,72,128]{2,1,0:T(8,128)} %shard_map.96) | data formatting | bytes 1179648 | tf_op jit(solution)/shard_map/reshape | solution.py:219
  241.3 2.1 fusion.37
  243.7 1.1 copy-done.3
  244.8 1.9 fusion.31
  246.7 2.0 fusion.32
  249.0 2.1 subtract_bitcast_fusion
  251.1 2.1 add_bitcast_fusion
  253.7 4.6 %copy.53 = f32[2,24,128,256]{3,2,1,0:T(8,128)} copy(f32[2,24,128,256]{3,1,2,0:T(8,128)S(1)} %pad_maximum_fusion) | data formatting | bytes 12582912
  (29 shorter events, 3.9 us)
Async XLA Ops:
  0.6 39.6 %copy-start = (bf16[1024,1024]{1,0:T(8,128)(2,1)S(1)}, bf16[1024,1024]{1,0:T(8,128)(2,1)}, u32[]{:S(2)}) copy-start(bf16[1024,1024]{1,0:T(8,128)(2,1)} %param.12) | copy-start | bytes 6291460
  3.0 1.2 copy-start.2
  3.0 1.6 copy-start.4
  12.5 27.8 %copy-start.7 = (f32[1024]{0:T(1024)S(1)}, f32[1024]{0:T(1024)}, u32[]{:S(2)}) copy-start(f32[1024]{0:T(1024)} %param.11) | copy-start | bytes 12292
  12.5 27.8 %copy-start.8 = (f32[1024]{0:T(1024)S(1)}, f32[1024]{0:T(1024)}, u32[]{:S(2)}) copy-start(f32[1024]{0:T(1024)} %param.9) | copy-start | bytes 12292
  38.5 1.1 copy-start.6
  40.3 7.3 %copy-start.9 = (f32[1024]{0:T(1024)S(1)}, f32[1024]{0:T(1024)}, u32[]{:S(2)}) copy-start(f32[1024]{0:T(1024)} %param.15) | copy-start | bytes 12292
  40.3 7.2 %copy-start.10 = (f32[1024]{0:T(1024)S(1)}, f32[1024]{0:T(1024)}, u32[]{:S(2)}) copy-start(f32[1024]{0:T(1024)} %param.13) | copy-start | bytes 12292
  54.9 25.1 %all-to-all-start.2 = ((bf16[8,24,32,128]{3,2,1,0:T(8,128)(2,1)}), bf16[8,24,32,128]{3,2,1,0:T(8,128)(2,1)S(1)}, u32[]{:S(2)}, u32[]{:S(2)}) async-start(bf16[8,24,32,128]{3,2,1,0:T(8,128)(2,1)} %bitcast.113), calls=%async_computation.2 | async-start | bytes 3145728 | tf_op jit(solution)/shard_map/all_to_all | solution.py:42
  80.0 55.1 %all-to-all-start = ((bf16[16,24,16,256]{3,2,1,0:T(8,128)(2,1)}), bf16[16,24,16,256]{3,2,1,0:T(8,128)(2,1)}, u32[]{:S(2)}, u32[]{:S(2)}) async-start(bf16[16,24,16,256]{3,2,1,0:T(8,128)(2,1)} %copy_bitcast_fusion), calls=%async_computation | async-start | bytes 6291456 | tf_op jit(solution)/shard_map/all_to_all | solution.py:212
  135.1 26.9 %all-to-all-start.3 = ((bf16[16,12,16,256]{3,2,1,0:T(8,128)(2,1)}), bf16[16,12,16,256]{3,2,1,0:T(8,128)(2,1)}, u32[]{:S(2)}, u32[]{:S(2)}) async-start(bf16[16,12,16,256]{3,2,1,0:T(8,128)(2,1)} %copy_bitcast_fusion.3), calls=%async_computation.3 | async-start | bytes 3145728 | tf_op jit(solution)/shard_map/all_to_all | solution.py:213
  243.4 1.4 copy-start.3
  244.8 2.0 copy-start.5
  253.7 4.6 %copy-start.1 = (bf16[1024,1024]{1,0:T(8,128)(2,1)S(1)}, bf16[1024,1024]{1,0:T(8,128)(2,1)}, u32[]{:S(2)}) copy-start(bf16[1024,1024]{1,0:T(8,128)(2,1)} %param.12) | copy-start | bytes 6291460

commit v17 on v16

--- a/solution.py
+++ b/solution.py
@@ -216,16 +216,18 @@
     peers = lax.axis_size("frame")
     bins = mix.shape[2]
     mix = frame_gather(mix.reshape(-1, 128), peers)
-    mix = mix.reshape(peers, 2, count, bins, count).transpose(1, 2, 0, 3, 4)
-    mix = mix.reshape(2, count, peers * bins, count)
-    mix_real, mix_imag = mix[0], mix[1]
-    real_part = spectra[0].astype(jnp.float32)
-    imag_part = spectra[1].astype(jnp.float32)
+    mix = mix.reshape(peers, 2, count, bins, count)
+    mix_real, mix_imag = mix[:, 0], mix[:, 1]
+    view = (count, peers, bins, spectra.shape[3])
+    real_part = spectra[0].astype(jnp.float32).reshape(view)
+    imag_part = spectra[1].astype(jnp.float32).reshape(view)
 
     def apply(m, y):
-        return jnp.einsum(
-            "jfa,aft->jft", m, y, precision=lax.Precision.HIGH, preferred_element_type=jnp.float32
+        out = jnp.einsum(
+            "sjba,asbt->jsbt", m, y, precision=lax.Precision.HIGH,
+            preferred_element_type=jnp.float32,
         )
+        return out.reshape(count, peers * bins, view[3])
 
     demixed_real = apply(mix_real, real_part) - apply(mix_imag, imag_part)
     demixed_imag = apply(mix_real, imag_part) + apply(mix_imag, real_part)

time: 260 us -> 257 us (0.988)
    slice x3, local copies, waits for them, and re-layouts: 2.65 us -> 9.87 us  [the longest x2 7.61 us: on_device(): real_part = spectra[0].astype(jnp.float32).reshape(view)]
    transpose x2 -> x1, local copies, waits for them, and re-layouts: 4.53 us -> 0.28 us  [source_model(): logpower.transpose(0, 2, 1).reshape(count, shards, rows, freq)]
    all_to_all x1, waiting for transfers between devices: 18.3 us -> 14.6 us  [on_device(): lax.all_to_all(var_send, 'frame', split_axis=0, concat_axis=0, tiled=True)]
    transpose x1 -> x0, other arithmetic: 3.27 us -> none  [source_model(): logpower.transpose(0, 2, 1).reshape(count, shards, rows, freq)]
    another operation x1, other arithmetic: 0.41 us -> 3.43 us  [on_device(): return (jnp.stack([demixed_real, demixed_imag]), variances)]
    unnamed x24 -> x27, local copies, waits for them, and re-layouts: 10.8 us -> 7.86 us
    convert_element_type x0 -> x1, other arithmetic: none -> 2.8 us  [source_model(): jnp.log(real_part * real_part + imag_part * imag_part + power_floor)]
  transfers between devices with their start and end apart: 3 -> 3, of which waited for: 3 -> 3; matrix products, arithmetic and copies ran while one was open for 9% -> 10% of each run, Pallas kernels for 0% -> 0%
where the time goes in v17:
time: 257 us; the launch traced here: 255 us
  Pallas kernels  73.4 us (29%)
  waiting for transfers between devices  65.5 us (25%)
  local copies, waits for them, and re-layouts  47.4 us (18%)
  blocking collectives  26 us (10%)
  matrix products  18.8 us (7%)
  starting transfers between devices  16.3 us (6%)
  other arithmetic  7.12 us (3%)
    pallas_call x1, Pallas kernels, sweep(): pl.pallas_call(functools.partial(sweep_kernel, frames), out_shape=(jax.Sh...  61.5 us
    all_to_all x1, waiting for transfers between devices, on_device(): lax.all_to_all(spec_send, 'frame', split_axis=0, concat_axis=0, tiled=True)  33.3 us
    all_to_all x1, blocking collectives, source_model(): lax.all_to_all(send, 'freq', split_axis=0, concat_axis=0, tiled=True)  26 us
    all_to_all x1, waiting for transfers between devices, source_model(): lax.all_to_all(send, 'freq', split_axis=0, concat_axis=0, tiled=True)  17.6 us
    all_to_all x1, waiting for transfers between devices, on_device(): lax.all_to_all(var_send, 'frame', split_axis=0, concat_axis=0, tiled=True)  14.6 us
    pallas_call x1, Pallas kernels, frame_gather(): pl.pallas_call(gather_kernel, out_shape=jax.ShapeDtypeStruct((n,) + x.sha...  11.9 us
    all_to_all x1, starting transfers between devices, on_device(): lax.all_to_all(spec_send, 'frame', split_axis=0, concat_axis=0, tiled=True)  8.09 us
    unnamed x27, local copies, waits for them, and re-layouts  7.86 us
  transfers between devices with their start and end apart: 3, of which 3 were waited for; matrix products, arithmetic and copies ran while one was open for 10% of the time, Pallas kernels for 0%

profile of v17, /device:TPU:0, one launch (start us, length us, event | category | flops | bytes accessed | tf_op | source)
XLA Modules:
  0.0 255.4 jit_solution(11067496563900903928)
XLA Ops:
  0.6 4.0 %fusion.37 = (bf16[1,24,128,256]{3,2,1,0:T(8,128)(2,1)}, bf16[1,24,128,256]{3,2,1,0:T(8,128)(2,1)}) fusion(bf16[2,24,128,256]{3,2,1,0:T(8,128)(2,1)} %param.8), kind=kLoop, calls=%fused_computation.46 | loop fusion | bytes 6291456 | tf_op jit(solution)/shard_map/slice | solution.py:222
  4.7 2.6 %copy.63 = bf16[1,24,128,256]{2,3,1,0:T(8,128)(2,1)} copy(bf16[1,24,128,256]{3,2,1,0:T(8,128)(2,1)} %get-tuple-element.14) | data formatting | bytes 3145728
  7.3 2.6 %copy.64 = bf16[1,24,128,256]{2,3,1,0:T(8,128)(2,1)} copy(bf16[1,24,128,256]{3,2,1,0:T(8,128)(2,1)} %get-tuple-element.15) | data formatting | bytes 3145728
  9.9 2.8 %log_convert_fusion = bf16[1,24,128,256]{2,3,1,0:T(8,128)(2,1)S(1)} fusion(bf16[1,24,128,256]{2,3,1,0:T(8,128)(2,1)} %copy.64, bf16[1,24,128,256]{2,3,1,0:T(8,128)(2,1)} %copy.63), kind=kLoop, calls=%fused_computation.15 | loop fusion | flops 5505024 | bytes 4718592 | tf_op jit(solution)/shard_map/convert_element_type | solution.py:18
  13.0 26.0 %all_to_all.20 = bf16[8,24,32,128]{3,2,1,0:T(8,128)(2,1)S(1)} all-to-all(bf16[8,24,32,128]{3,2,1,0:T(8,128)(2,1)S(1)} %copy.49), channel_id=1, replica_groups=mesh['freq'=8,'frame'=16] {'freq'}, dimensions={0} | all-to-all | bytes 3145728 | tf_op jit(solution)/shard_map/all_to_all | solution.py:25
  40.8 7.2 %fusion.11 = f32[24,32,1024]{2,1,0:T(8,128)} fusion(bf16[1024,1024]{1,0:T(8,128)(2,1)S(1)} %copy-done, f32[1024]{0:T(1024)S(1)} %copy-done.8, bf16[1024,1024]{1,0:T(8,128)(2,1)} %param.10, f32[1024]{0:T(1024)S(1)} %copy-done.9, f32[24,32]{1,0:T(8,128)S(1)} %add_rsqrt_fusion, f32[24,32]{1,0:T(8,128)S(1)} %broadcast_multiply_fusion, ...), kind=kOutput, calls=%fused_computation.20 | convolution fusion | flops 3229876224 | bytes 8927232 | tf_op jit(solution)/shard_map/nth,hg->ntg/dot_general | solution.py:35
  48.1 5.9 %fusion.21 = bf16[24,4,8,8,128]{4,3,2,1,0:T(8,128)(2,1)S(1)} fusion(f32[1024]{0:T(1024)S(1)} %copy-done.10, bf16[1024,1024]{1,0:T(8,128)(2,1)} %param.14, f32[24,32,1024]{2,1,0:T(8,128)} %fusion.11, f32[1024]{0:T(1024)S(1)} %copy-done.11), kind=kOutput, calls=%fused_computation.35 | convolution fusion | flops 1622409216 | bytes 6823936 | tf_op jit(solution)/shard_map/nth,hf->ntf/dot_general | solution.py:38
  54.0 1.4 copy.86
  55.4 3.6 %all-to-all-start.2 = ((bf16[8,24,32,128]{3,2,1,0:T(8,128)(2,1)}), bf16[8,24,32,128]{3,2,1,0:T(8,128)(2,1)S(1)}, u32[]{:S(2)}, u32[]{:S(2)}) async-start(bf16[8,24,32,128]{3,2,1,0:T(8,128)(2,1)} %bitcast.109), calls=%async_computation.2 | async-start | bytes 3145728 | tf_op jit(solution)/shard_map/all_to_all | solution.py:42
  59.0 3.9 %copy_bitcast_fusion = bf16[16,24,16,256]{3,2,1,0:T(8,128)(2,1)} fusion(bf16[2,24,128,256]{3,2,1,0:T(8,128)(2,1)} %param.8), kind=kLoop, calls=%fused_computation.14 | loop fusion | bytes 6291456 | tf_op jit(solution)/shard_map/reshape | solution.py:209
  62.9 17.6 %all-to-all-done.2 = bf16[8,24,32,128]{3,2,1,0:T(8,128)(2,1)S(1)} async-done(((bf16[8,24,32,128]{3,2,1,0:T(8,128)(2,1)}), bf16[8,24,32,128]{3,2,1,0:T(8,128)(2,1)S(1)}, u32[]{:S(2)}, u32[]{:S(2)}) %all-to-all-start.2) | async-done | bytes 1572896 | tf_op jit(solution)/shard_map/all_to_all | solution.py:42
  80.5 8.1 %all-to-all-start = ((bf16[16,24,16,256]{3,2,1,0:T(8,128)(2,1)}), bf16[16,24,16,256]{3,2,1,0:T(8,128)(2,1)}, u32[]{:S(2)}, u32[]{:S(2)}) async-start(bf16[16,24,16,256]{3,2,1,0:T(8,128)(2,1)} %copy_bitcast_fusion), calls=%async_computation | async-start | bytes 6291456 | tf_op jit(solution)/shard_map/all_to_all | solution.py:212
  88.6 4.9 %copy.53 = bf16[24,128,8,32]{3,2,1,0:T(8,128)(2,1)} copy(bf16[24,128,8,32]{1,3,0,2:T(8,128)(2,1)S(1)} %bitcast.106) | data formatting | bytes 3145728 | tf_op jit(solution)/shard_map/transpose | solution.py:43
  93.6 7.5 %reshape_reshape.3 = bf16[12,2,16,8,256]{4,3,2,1,0:T(8,128)(2,1)S(1)} reshape(bf16[24,128,8,32]{3,2,1,0:T(8,128)(2,1)} %copy.53) | data formatting | bytes 3145728 | tf_op jit(solution)/shard_map/reshape;reshape | solution.py:210
  101.1 1.3 copy_bitcast_fusion.3
  102.4 33.3 %all-to-all-done.spec_in = bf16[16,24,16,256]{3,2,1,0:T(8,128)(2,1)} async-done(((bf16[16,24,16,256]{3,2,1,0:T(8,128)(2,1)}), bf16[16,24,16,256]{3,2,1,0:T(8,128)(2,1)}, u32[]{:S(2)}, u32[]{:S(2)}) %all-to-all-start) | async-done | bytes 3145760 | tf_op jit(solution)/shard_map/all_to_all | solution.py:212
  135.7 4.6 %all-to-all-start.3 = ((bf16[16,12,16,256]{3,2,1,0:T(8,128)(2,1)}), bf16[16,12,16,256]{3,2,1,0:T(8,128)(2,1)}, u32[]{:S(2)}, u32[]{:S(2)}) async-start(bf16[16,12,16,256]{3,2,1,0:T(8,128)(2,1)} %copy_bitcast_fusion.3), calls=%async_computation.3 | async-start | bytes 3145728 | tf_op jit(solution)/shard_map/all_to_all | solution.py:213
  140.3 3.6 %copy.56 = bf16[1,24,128,256]{3,1,2,0:T(8,128)(2,1)} copy(bf16[1,24,128,256]{3,2,1,0:T(8,128)(2,1)} %get-tuple-element.14) | data formatting | bytes 3145728 | tf_op jit(solution)/shard_map/slice | solution.py:222
  143.8 2.1 copy.58
  146.3 1.6 copy.61
  147.9 14.6 %all-to-all-done.3.var_in = bf16[16,12,16,256]{3,2,1,0:T(8,128)(2,1)} async-done(((bf16[16,12,16,256]{3,2,1,0:T(8,128)(2,1)}), bf16[16,12,16,256]{3,2,1,0:T(8,128)(2,1)}, u32[]{:S(2)}, u32[]{:S(2)}) %all-to-all-start.3) | async-done | bytes 1572896 | tf_op jit(solution)/shard_map/all_to_all | solution.py:213
  162.5 61.5 %shard_map.95 = (f32[24,8,128]{2,1,0:T(8,128)}, f32[24,8,128]{2,1,0:T(8,128)}) custom-call(bf16[16,24,16,256]{3,2,1,0:T(8,128)(2,1)} %all-to-all-done.spec_in, bf16[16,12,16,256]{3,2,1,0:T(8,128)(2,1)} %all-to-all-done.3.var_in), custom_call_target="tpu_custom_call" | custom-call | tf_op jit(solution)/shard_map/pallas_call | solution.py:133
  225.8 11.9 %shard_map.96 = f32[16,72,128]{2,1,0:T(8,128)} custom-call(f32[72,128]{1,0:T(8,128)} %reshape.107.x_ref), custom_call_target="tpu_custom_call" | custom-call | tf_op jit(solution)/shard_map/pallas_call | solution.py:186
  237.7 4.1 %reshape.108 = f32[16,2,24,8,24]{4,3,2,1,0:T(8,128)} reshape(f32[16,72,128]{2,1,0:T(8,128)} %shard_map.96) | data formatting | bytes 1179648 | tf_op jit(solution)/shard_map/reshape | solution.py:219
  241.8 2.3 fusion.36
  244.1 1.3 fusion.23
  245.6 1.3 fusion.22
  246.9 1.5 convolution_subtract_fusion
  248.4 1.0 copy.59
  249.5 1.5 convolution_add_fusion
  250.9 1.0 copy.60
  251.9 3.4 %pad_maximum_fusion = f32[2,24,128,256]{3,2,1,0:T(8,128)} fusion(f32[1,24,128,256]{3,2,1,0:T(8,128)S(1)} %copy.60, f32[1,24,128,256]{3,2,1,0:T(8,128)S(1)} %copy.59), kind=kLoop, calls=%fused_computation.1 | loop fusion | flops 1572864 | bytes 12582912 | tf_op jit(solution)/shard_map/stack | solution.py:234
  (33 shorter events, 4.4 us)
Async XLA Ops:
  0.6 40.1 %copy-start = (bf16[1024,1024]{1,0:T(8,128)(2,1)S(1)}, bf16[1024,1024]{1,0:T(8,128)(2,1)}, u32[]{:S(2)}) copy-start(bf16[1024,1024]{1,0:T(8,128)(2,1)} %param.12) | copy-start | bytes 6291460
  13.0 27.8 %copy-start.8 = (f32[1024]{0:T(1024)S(1)}, f32[1024]{0:T(1024)}, u32[]{:S(2)}) copy-start(f32[1024]{0:T(1024)} %param.11) | copy-start | bytes 12292
  13.0 27.8 %copy-start.9 = (f32[1024]{0:T(1024)S(1)}, f32[1024]{0:T(1024)}, u32[]{:S(2)}) copy-start(f32[1024]{0:T(1024)} %param.9) | copy-start | bytes 12292
  39.0 1.2 copy-start.5
  40.8 7.3 %copy-start.10 = (f32[1024]{0:T(1024)S(1)}, f32[1024]{0:T(1024)}, u32[]{:S(2)}) copy-start(f32[1024]{0:T(1024)} %param.15) | copy-start | bytes 12292
  40.8 7.2 %copy-start.11 = (f32[1024]{0:T(1024)S(1)}, f32[1024]{0:T(1024)}, u32[]{:S(2)}) copy-start(f32[1024]{0:T(1024)} %param.13) | copy-start | bytes 12292
  55.4 25.1 %all-to-all-start.2 = ((bf16[8,24,32,128]{3,2,1,0:T(8,128)(2,1)}), bf16[8,24,32,128]{3,2,1,0:T(8,128)(2,1)S(1)}, u32[]{:S(2)}, u32[]{:S(2)}) async-start(bf16[8,24,32,128]{3,2,1,0:T(8,128)(2,1)} %bitcast.109), calls=%async_computation.2 | async-start | bytes 3145728 | tf_op jit(solution)/shard_map/all_to_all | solution.py:42
  80.5 8.1 %copy-start.6 = (bf16[8,24,32,128]{3,2,1,0:T(8,128)(2,1)}, bf16[8,24,32,128]{3,2,1,0:T(8,128)(2,1)S(1)}, u32[]{:S(2)}) copy-start(bf16[8,24,32,128]{3,2,1,0:T(8,128)(2,1)S(1)} %all-to-all-done.2) | copy-start | bytes 4718596
  80.5 55.1 %all-to-all-start = ((bf16[16,24,16,256]{3,2,1,0:T(8,128)(2,1)}), bf16[16,24,16,256]{3,2,1,0:T(8,128)(2,1)}, u32[]{:S(2)}, u32[]{:S(2)}) async-start(bf16[16,24,16,256]{3,2,1,0:T(8,128)(2,1)} %copy_bitcast_fusion), calls=%async_computation | async-start | bytes 6291456 | tf_op jit(solution)/shard_map/all_to_all | solution.py:212
  102.4 41.5 %copy-start.2 = (bf16[1,24,128,256]{3,2,1,0:T(8,128)(2,1)S(1)}, bf16[1,24,128,256]{3,2,1,0:T(8,128)(2,1)}, u32[]{:S(2)}) copy-start(bf16[1,24,128,256]{3,2,1,0:T(8,128)(2,1)} %get-tuple-element.15) | copy-start | bytes 4718596
  135.7 26.9 %all-to-all-start.3 = ((bf16[16,12,16,256]{3,2,1,0:T(8,128)(2,1)}), bf16[16,12,16,256]{3,2,1,0:T(8,128)(2,1)}, u32[]{:S(2)}, u32[]{:S(2)}) async-start(bf16[16,12,16,256]{3,2,1,0:T(8,128)(2,1)} %copy_bitcast_fusion.3), calls=%async_computation.3 | async-start | bytes 3145728 | tf_op jit(solution)/shard_map/all_to_all | solution.py:213
  140.3 5.7 %copy-start.7 = (bf16[8,24,32,128]{3,2,1,0:T(8,128)(2,1)S(1)}, bf16[8,24,32,128]{3,2,1,0:T(8,128)(2,1)}, u32[]{:S(2)}) copy-start(bf16[8,24,32,128]{3,2,1,0:T(8,128)(2,1)} %copy-done.6) | copy-start | bytes 4718596
  241.8 2.4 copy-start.3
  244.1 1.4 copy-start.4
  251.9 3.4 %copy-start.1 = (bf16[1024,1024]{1,0:T(8,128)(2,1)S(1)}, bf16[1024,1024]{1,0:T(8,128)(2,1)}, u32[]{:S(2)}) copy-start(bf16[1024,1024]{1,0:T(8,128)(2,1)} %param.12) | copy-start | bytes 6291460
